TPU v7x, 256 devices: a whole 4x4x8 slice. The times are simulated.
256 devices in a mesh: pool: 32 (over z_hi, x, y), serve: 8 (over z_lo, core).
Axes of the slice: x: 4, y: 4, z: 8 (z_hi: 2, z_lo: 4; z = z_hi * 4 + z_lo), core: 2. Of those that a mesh axis runs over, the one named last changes fastest.
Arguments:
- queries: bfloat16 [8, 256, 73728], P('serve', None, 'pool'), may hold values from -16 to 16
- new_latent: bfloat16 [8, 147456], P('serve', 'pool'), may hold values from -8 to 8
- pool: bfloat16 [8, 384, 36864], P('serve', 'pool'), may hold values from -6 to 6
- page_owner: int32 [8, 32], P('serve'), may hold values from 0 to 31, as said below
- page_slot: int32 [8, 32], P('serve'), may hold values from 0 to 10
- new_owner: int32 [8, 4], P('serve'), may hold values from 0 to 31, as said below
- new_slot: int32 [8, 4], P('serve'), may hold values from 0 to 11
- prefix_len: int32 [8], P('serve'), may hold values from 512 to 2048, as said below
- w_uv: bfloat16 [128, 512, 128], P('pool', 'serve'), may hold values from -1 to 1
Outputs:
- attn_out: bfloat16 [8, 256, 16384], P('serve', None, 'pool')
- new_pool: bfloat16 [8, 384, 36864], P('serve', 'pool')
Inputs may be any that keep to these rules, and one draw needn't show every extreme that they name: Within a request the pairs (page_owner, page_slot) differ from one another and from the pairs (new_owner, new_slot); at most 3 entries of a request's table name the same owner, and in every request some owner is named exactly 3 times. `new_owner`: the 4 new pages of a request go to different owners. `prefix_len`: some request has exactly 2048 prefix tokens.
All inputs are finite; a program needn't handle non-finite values.
Results may differ from a plain program's by a relative error of at most 0.0075.
Values may be sent and summed in bfloat16 or wider, within the bound.
No kernel may reach another device: no remote copies, remote signals or barrier semaphores. Data moves between devices by JAX's collectives and lax.ppermute only.
A program may use at most 128 MiB of HBM per device.

v0:
```python
import jax
import jax.numpy as jnp
from jax import lax
from jax.sharding import Mesh
from jax.sharding import PartitionSpec as P

VLAT = 512
VHEAD = 128
PAGE = 64
SUF = 256
HOT = 3
LAT = 576
PPAGES = 32
NEWP = 4
SLOTS = 12
POOL = ("pool_0", "pool_1", "pool_2")


softmax_scale = 192.0 ** (-0.5)
masked_score = -1e30


def laid_out(pieces, dim):
    lengths = list(pieces.shape[1:])
    lengths[dim] *= pieces.shape[0]
    return jnp.moveaxis(pieces, 0, dim).reshape(lengths)


def copy_for_each(x, axis):
    copies = jnp.broadcast_to(x, (lax.axis_size(axis), *x.shape))
    return lax.all_to_all(copies, axis, split_axis=0, concat_axis=0, tiled=True)


def collect(x, axis, dim):
    return laid_out(copy_for_each(x, axis), dim)


def all_blocks(x, axes, order):
    pieces = x[None]
    for k in order:
        pieces = lax.all_gather(pieces, axes[k], axis=0, tiled=True)
    carried = [lax.axis_size(axes[k]) for k in reversed(order)]
    pieces = pieces.reshape(*carried, *x.shape)
    turned = sorted(range(len(order)), key=lambda place: order[len(order) - 1 - place])
    return pieces.transpose(*turned, *range(len(order), pieces.ndim)).reshape(-1, *x.shape)


def gathered_by_axis(x, axes, order, dim):
    return laid_out(all_blocks(x, axes, order), dim)


def absorb(running, query_rows, key_rows, allowed):
    top_old, sum_old, mixture_old = running
    scores = (
        jnp.einsum("qhd,kd->hqk", query_rows, key_rows, preferred_element_type=jnp.float32)
        * softmax_scale
    )
    scores = jnp.where(allowed, scores, masked_score)
    top_score = jnp.maximum(top_old, jnp.max(scores, axis=-1))
    rescale = jnp.exp(top_old - top_score)
    weights = jnp.exp(scores - top_score[..., None])
    weight_sum = sum_old * rescale + jnp.sum(weights, axis=-1)
    mixture = mixture_old * rescale[..., None] + jnp.einsum(
        "hqk,kv->hqv",
        weights.astype(jnp.bfloat16),
        key_rows[:, :VLAT],
        preferred_element_type=jnp.float32,
    )
    return (top_score, weight_sum, mixture)


def local(queries, new_latent, pool, page_owner, page_slot, new_owner, new_slot, prefix_len, w_uv):
    holder = lax.axis_index(POOL)
    head_count = queries.shape[2] // LAT
    query_rows = queries.reshape(SUF, head_count, LAT)
    suffix_all = collect(new_latent, POOL, 1)
    suffix = suffix_all.reshape(SUF, LAT)
    position = jnp.arange(SUF, dtype=jnp.int32)
    causal = position[None, :] <= position[:, None]
    start_state = (
        jnp.full((head_count, SUF), masked_score, jnp.float32),
        jnp.zeros((head_count, SUF), jnp.float32),
        jnp.zeros((head_count, SUF, VLAT), jnp.float32),
    )
    running = absorb(start_state, query_rows, suffix, causal[None])
    owners = page_owner[0]
    slot_ids = page_slot[0]
    length = prefix_len[0]
    page_index = jnp.arange(PPAGES, dtype=jnp.int32)
    tokens = jnp.clip(length - PAGE * page_index, 0, PAGE)
    local_pages = pool[0]
    block_pages = max(1, 512 // PAGE)
    earlier = (page_index[None, :] < page_index[:, None]) & (owners[None, :] == owners[:, None])
    rank_among = jnp.sum(earlier.astype(jnp.int32), axis=1)
    gathered_row = owners * HOT + rank_among
    my_ranks = jnp.arange(HOT, dtype=jnp.int32)
    my_rows = (owners[None, :] == holder) & (rank_among[None, :] == my_ranks[:, None])
    slot_rows = jnp.sum(jnp.where(my_rows, slot_ids[None, :], 0), axis=1)
    outgoing = local_pages[slot_rows]
    gathered = gathered_by_axis(outgoing, POOL, (0, 1, 2), 0)
    prefix_pages = gathered[gathered_row]
    for opening in range(0, PPAGES, block_pages):
        closing = min(PPAGES, opening + block_pages)
        key_rows = prefix_pages[opening:closing].reshape(-1, LAT)
        inside = (
            lax.broadcasted_iota(jnp.int32, (closing - opening, PAGE), 1)
            < tokens[opening:closing, None]
        ).reshape(-1)
        running = absorb(running, query_rows, key_rows, inside[None, None, :])
    latent_out = (running[2] / running[1][..., None]).astype(jnp.bfloat16)
    projected = jnp.einsum(
        "hqv,hve->qhe", latent_out, collect(w_uv, "serve", 1), preferred_element_type=jnp.float32
    )
    attended = projected.astype(jnp.bfloat16).reshape(1, SUF, head_count * VHEAD)
    fresh_pages = suffix_all.reshape(NEWP, PAGE * LAT)
    placing = (jnp.arange(SLOTS, dtype=jnp.int32)[:, None] == new_slot[0][None, :]) & (
        new_owner[0][None, :] == holder
    )
    written = jnp.dot(
        placing.astype(jnp.bfloat16), fresh_pages, preferred_element_type=jnp.float32
    ).astype(jnp.bfloat16)
    updated = jnp.where(jnp.any(placing, axis=1)[:, None], written, local_pages)
    return (attended, updated[None])


def solution(mesh):
    split = Mesh(
        mesh.devices.reshape(2, 4, 4, mesh.shape["serve"]), ("pool_0", "pool_1", "pool_2", "serve")
    )
    placed = (
        P("serve", None, POOL),
        P("serve", POOL),
        P("serve", POOL, None),
        P("serve", None),
        P("serve", None),
        P("serve", None),
        P("serve", None),
        P("serve"),
        P(POOL, "serve", None),
    )
    return jax.shard_map(
        local,
        mesh=split,
        in_specs=placed,
        out_specs=(P("serve", None, POOL), P("serve", POOL, None)),
        check_vma=False,
    )
```

profile of v0, /device:TPU:64, one launch (start us, length us, event | category | flops | bytes accessed | tf_op | source)
XLA Modules:
  0.0 233.3 jit_solution(17039694362229609466)
XLA Ops:
  9.6 2.4 %gather_fusion = bf16[3,36864]{1,0:T(4,128)(2,1)S(1)} fusion(bf16[12,36864]{1,0:T(8,128)(2,1)} %bitcast.132, s32[1024]{0:T(1024)S(1)} %pad_clamp_fusion.1), kind=kCustom, calls=%fused_computation | custom fusion | bytes 442380 | tf_op jit(solution)/shard_map/gather | solution.py:99
  12.0 19.9 %all-gather.1 = bf16[2,3,36864]{2,1,0:T(4,128)(2,1)} all-gather(bf16[1,3,36864]{2,1,0:T(4,128)(2,1)S(1)} %bitcast.138), channel_id=2, replica_groups=mesh['pool_0'=2,'pool_1'=4,'pool_2'=4,'serve'=8] {'pool_0'}, dimensions={0}, use_global_device_ids=true | all-gather | bytes 663552 | tf_op jit(solution)/shard_map/all_gather | solution.py:41
  32.0 37.2 %all-gather.5.cloned.1.call-done = bf16[8,3,36864]{2,1,0:T(4,128)(2,1)} async-done(((bf16[2,3,36864]{2,1,0:T(4,128)(2,1)}), bf16[8,3,36864]{2,1,0:T(4,128)(2,1)}) %all-gather.5.cloned.1.call-update) | async-done | bytes 1769488 | tf_op jit(solution)/shard_map/all_gather | solution.py:41
  69.3 4.3 %copy.47 = bf16[8,3,36864]{2,0,1:T(8,128)(2,1)} copy(bf16[8,3,36864]{2,1,0:T(4,128)(2,1)} %all-gather.5.cloned.1.call-done) | data formatting | bytes 3538944 | tf_op jit(solution)/shard_map/all_gather | solution.py:41
  74.5 2.4 %reduce.3 = bf16[32,4608]{1,0:T(8,128)(2,1)S(1)} reduce(bf16[32,1,4608]{2,1,0:T(2,128)(2,1)S(1)} %broadcast_in_dim.111, bf16[]{:T(256)} %broadcast.182), dimensions={1}, to_apply=%broadcast_in_dim.111.reduce_sub_computation | reduce | bytes 589826 | tf_op jit(solution)/shard_map/broadcast_in_dim | solution.py:30
  77.7 9.3 %all-to-all-start = ((bf16[32,2,2304]{2,1,0:T(2,128)(2,1)}), bf16[32,2,2304]{2,1,0:T(2,128)(2,1)S(1)}, u32[]{:S(2)}, u32[]{:S(2)}) async-start(bf16[32,2,2304]{2,1,0:T(2,128)(2,1)} %reshape.291), calls=%async_computation | async-start | bytes 589824 | tf_op jit(solution)/shard_map/all_to_all | solution.py:31
  89.8 13.6 %all-to-all-done = bf16[32,2,2304]{2,1,0:T(2,128)(2,1)S(1)} async-done(((bf16[32,2,2304]{2,1,0:T(2,128)(2,1)}), bf16[32,2,2304]{2,1,0:T(2,128)(2,1)S(1)}, u32[]{:S(2)}, u32[]{:S(2)}) %all-to-all-start) | async-done | bytes 294944 | tf_op jit(solution)/shard_map/all_to_all | solution.py:31
  104.4 4.4 %all-to-all-start.1 = ((bf16[8,4,64,128]{3,2,1,0:T(8,128)(2,1)}), bf16[8,4,64,128]{3,2,1,0:T(8,128)(2,1)}, u32[]{:S(2)}, u32[]{:S(2)}) async-start(bf16[8,4,64,128]{3,2,1,0:T(8,128)(2,1)} %broadcast_in_dim.123), calls=%async_computation.1 | async-start | bytes 1048576 | tf_op jit(solution)/shard_map/all_to_all | solution.py:31
  113.1 1.9 fusion.90
  115.0 5.8 %all-to-all-done.1 = bf16[8,4,64,128]{3,2,1,0:T(8,128)(2,1)} async-done(((bf16[8,4,64,128]{3,2,1,0:T(8,128)(2,1)}), bf16[8,4,64,128]{3,2,1,0:T(8,128)(2,1)}, u32[]{:S(2)}, u32[]{:S(2)}) %all-to-all-start.1) | async-done | bytes 524320 | tf_op jit(solution)/shard_map/all_to_all | solution.py:31
  120.8 1.9 copy.57
  122.7 28.8 %all-gather.7.cloned.1.call-done = bf16[32,3,36864]{2,0,1:T(8,128)(2,1)} async-done(((bf16[8,3,36864]{2,0,1:T(8,128)(2,1)}), bf16[32,3,36864]{2,0,1:T(8,128)(2,1)}) %all-gather.7.cloned.1.call-update) | async-done | bytes 7077904 | tf_op jit(solution)/shard_map/all_gather | solution.py:41
  151.5 11.4 %reshape.251 = bf16[4,4,2,3,36864]{4,2,1,0,3:T(2,128)(2,1)} reshape(bf16[32,3,36864]{2,0,1:T(8,128)(2,1)} %all-gather.7.cloned.1.call-done) | data formatting | bytes 14155776 | tf_op jit(solution)/shard_map/reshape | solution.py:43
  162.9 10.8 %copy.77 = bf16[4,4,2,3,36864]{4,3,0,1,2:T(4,128)(2,1)} copy(bf16[4,4,2,3,36864]{4,2,1,0,3:T(2,128)(2,1)} %reshape.251) | data formatting | bytes 14155776 | tf_op jit(solution)/shard_map/reshape | solution.py:43
  173.7 9.8 %reshape_reshape.3 = bf16[96,36864]{1,0:T(8,128)(2,1)} reshape(bf16[2,4,4,3,36864]{4,3,2,1,0:T(4,128)(2,1)} %bitcast.131) | data formatting | bytes 14155776 | tf_op jit(solution)/shard_map/reshape;reshape | solution.py:26
  183.5 8.0 %gather_fusion.1 = bf16[32,36864]{1,0:T(8,128)(2,1)S(1)} fusion(bf16[96,36864]{1,0:T(8,128)(2,1)} %reshape_reshape.3, s32[1024]{0:T(1024)S(1)} %pad_clamp_fusion), kind=kCustom, calls=%fused_computation.1 | custom fusion | bytes 4718720 | tf_op jit(solution)/shard_map/gather | solution.py:101
  192.9 2.8 %reshape.254 = bf16[512,576]{1,0:T(8,128)(2,1)} reshape(bf16[8,36864]{1,0:T(8,128)(2,1)} %get-tuple-element.20) | data formatting | bytes 1179648 | tf_op jit(solution)/shard_map/reshape | solution.py:104
  195.7 2.8 %reshape.253 = bf16[512,576]{1,0:T(8,128)(2,1)} reshape(bf16[8,36864]{1,0:T(8,128)(2,1)} %get-tuple-element.21) | data formatting | bytes 1179648 | tf_op jit(solution)/shard_map/reshape | solution.py:104
  201.9 2.2 bitcast_reduce_fusion.1
  208.2 2.3 fusion.24
  211.2 2.4 %fusion.22 = f32[4,256,512]{2,1,0:T(8,128)} fusion(f32[512,256,4]{1,0,2:T(8,128)S(1)} %get-tuple-element.34, f32[4,256]{1,0:T(4,128)S(1)} %get-tuple-element.17, pred[512]{0:T(512)(128)(4,1)S(1)} %lt.104, bf16[512,576]{1,0:T(8,128)(2,1)S(1)} %copy-done.11), kind=kOutput, calls=%fused_computation.37 | convolution fusion | flops 538968064 | bytes 4723200 | tf_op jit(solution)/shard_map/hqk,kv->hqv/dot_general | solution.py:63
  214.7 2.3 fusion.20
  217.2 1.8 fusion.62
  220.2 5.4 %fusion.17 = bf16[4,256,128]{1,2,0:T(8,128)(2,1)S(1)} fusion(bf16[4,512,128]{2,1,0:T(8,128)(2,1)S(1)} %bitcast.139, f32[4,256,512]{2,1,0:T(8,128)} %fusion.20, f32[4,256,512]{2,1,0:T(8,128)} %fusion.22, f32[4,256,512]{2,1,0:T(8,128)} %fusion.24, f32[4,256,512]{2,1,0:T(8,128)} %fusion.62, f32[512,256,4]{1,0,2:T(8,128)S(1)} %get-tuple-element.30, ...), kind=kOutput, calls=%fused_computation.35 | convolution fusion | flops 679084032 | bytes 11825664 | tf_op jit(solution)/shard_map/hqv,hve->qhe/dot_general | solution.py:111
  (88 shorter events, 24.5 us)
Async XLA Ops:
  7.2 62.1 %all-gather.5.cloned.1.call-start = ((), (), s32[]{:S(2)}) async-start(), calls=%async_computation.2 | async-start | bytes 2949120 | tf_op jit(solution)/shard_map/all_gather | solution.py:41
  32.0 41.6 %copy-start.15 = (bf16[1,4608]{1,0:T(2,128)(2,1)S(1)}, bf16[1,4608]{1,0:T(2,128)(2,1)}, u32[]{:S(2)}) copy-start(bf16[1,4608]{1,0:T(2,128)(2,1)} %param.10) | copy-start | bytes 27652
  32.0 119.5 %all-gather.7.cloned.1.call-start = ((), (), s32[]{:S(2)}) async-start(), calls=%async_computation.3 | async-start | bytes 8847360 | tf_op jit(solution)/shard_map/all_gather | solution.py:41
  73.5 14.5 %copy-start.3 = (bf16[1,256,2304]{2,1,0:T(8,128)(2,1)S(1)}, bf16[1,256,2304]{2,1,0:T(8,128)(2,1)}, u32[]{:S(2)}) copy-start(bf16[1,256,2304]{2,1,0:T(8,128)(2,1)} %param.9) | copy-start | bytes 3538948
  74.5 15.3 %copy-start.18 = (s32[1,32]{1,0:T(1,128)S(1)}, s32[1,32]{1,0:T(1,128)}, u32[]{:S(2)}) copy-start(s32[1,32]{1,0:T(1,128)} %param.12) | copy-start | bytes 388
  74.5 29.0 %copy-start.14 = (bf16[4,64,128]{2,1,0:T(8,128)(2,1)S(1)}, bf16[4,64,128]{2,1,0:T(8,128)(2,1)}, u32[]{:S(2)}) copy-start(bf16[4,64,128]{2,1,0:T(8,128)(2,1)} %param.17) | copy-start | bytes 196612
  77.7 25.8 %all-to-all-start = ((bf16[32,2,2304]{2,1,0:T(2,128)(2,1)}), bf16[32,2,2304]{2,1,0:T(2,128)(2,1)S(1)}, u32[]{:S(2)}, u32[]{:S(2)}) async-start(bf16[32,2,2304]{2,1,0:T(2,128)(2,1)} %reshape.291), calls=%async_computation | async-start | bytes 589824 | tf_op jit(solution)/shard_map/all_to_all | solution.py:31
  86.9 21.8 %copy-start.19 = (s32[1,4]{1,0:T(1,128)S(1)}, s32[1,4]{1,0:T(1,128)}, u32[]{:S(2)}) copy-start(s32[1,4]{1,0:T(1,128)} %param.14) | copy-start | bytes 52
  87.0 21.8 %copy-start.17 = (s32[1,4]{1,0:T(1,128)S(1)}, s32[1,4]{1,0:T(1,128)}, u32[]{:S(2)}) copy-start(s32[1,4]{1,0:T(1,128)} %param.15) | copy-start | bytes 52
  89.6 129.4 %copy-start.16 = (pred[512]{0:T(512)(128)(4,1)}, pred[512]{0:T(512)(128)(4,1)S(1)}, u32[]{:S(2)}) copy-start(pred[512]{0:T(512)(128)(4,1)S(1)} %lt.110) | copy-start | bytes 1540
  104.4 7.1 %copy-start = (bf16[1,12,36864]{2,1,0:T(8,128)(2,1)S(1)}, bf16[1,12,36864]{2,1,0:T(8,128)(2,1)}, u32[]{:S(2)}) copy-start(bf16[1,12,36864]{2,1,0:T(8,128)(2,1)} %param.11) | copy-start | bytes 2654212
  104.4 16.4 %all-to-all-start.1 = ((bf16[8,4,64,128]{3,2,1,0:T(8,128)(2,1)}), bf16[8,4,64,128]{3,2,1,0:T(8,128)(2,1)}, u32[]{:S(2)}, u32[]{:S(2)}) async-start(bf16[8,4,64,128]{3,2,1,0:T(8,128)(2,1)} %broadcast_in_dim.123), calls=%async_computation.1 | async-start | bytes 1048576 | tf_op jit(solution)/shard_map/all_to_all | solution.py:31
  111.2 3.8 %copy-start.6 = (bf16[256,576]{1,0:T(8,128)(2,1)}, bf16[256,576]{1,0:T(8,128)(2,1)S(1)}, u32[]{:S(2)}) copy-start(bf16[256,576]{1,0:T(8,128)(2,1)S(1)} %reshape_reshape_transpose.6) | copy-start | bytes 884740
  192.9 5.6 %copy-start.2 = (bf16[8,36864]{1,0:T(8,128)(2,1)S(1)}, bf16[8,36864]{1,0:T(8,128)(2,1)}, u32[]{:S(2)}) copy-start(bf16[8,36864]{1,0:T(8,128)(2,1)} %get-tuple-element.22) | copy-start | bytes 1769476
  192.9 7.3 %copy-start.1 = (bf16[8,36864]{1,0:T(8,128)(2,1)S(1)}, bf16[8,36864]{1,0:T(8,128)(2,1)}, u32[]{:S(2)}) copy-start(bf16[8,36864]{1,0:T(8,128)(2,1)} %get-tuple-element.19) | copy-start | bytes 1769476
  195.7 6.2 %copy-start.4 = (bf16[1,256,2304]{1,2,0:T(8,128)(2,1)S(1)}, bf16[1,256,2304]{1,2,0:T(8,128)(2,1)}, u32[]{:S(2)}) copy-start(bf16[1,256,2304]{1,2,0:T(8,128)(2,1)} %copy.44) | copy-start | bytes 3538948
  201.9 2.2 copy-start.11
  204.1 1.3 copy-start.5
  204.1 1.4 copy-start.8
  205.5 1.1 copy-start.12
  213.6 1.1 copy-start.10
  214.7 2.5 %copy-start.7 = (bf16[256,576]{1,0:T(8,128)(2,1)S(1)}, bf16[256,576]{1,0:T(8,128)(2,1)}, u32[]{:S(2)}) copy-start(bf16[256,576]{1,0:T(8,128)(2,1)} %copy-done.6) | copy-start | bytes 884740
  219.0 1.1 copy-start.9
  219.0 1.2 copy-start.13
Sparse Core Ops, SparseCore 0:
  32.1 37.1 all-gather.4
  73.7 77.7 all-gather.6
where the time goes:
time: 236 us; the launch traced here: 233 us
  waiting for transfers between devices  85.5 us (36%)
  local copies, waits for them, and re-layouts  66.1 us (28%)
  matrix products  23 us (10%)
  blocking collectives  19.9 us (8%)
  between operations  15 us (6%)
  starting transfers between devices  13.8 us (6%)
  other arithmetic  9.97 us (4%)
    all_gather x2, waiting for transfers between devices, all_blocks(): pieces = lax.all_gather(pieces, axes[k], axis=0, tiled=True)  66.1 us
    reshape x2, local copies, waits for them, and re-layouts, all_blocks(): pieces = pieces.reshape(*carried, *x.shape)  22.2 us
    all_gather x1, blocking collectives, all_blocks(): pieces = lax.all_gather(pieces, axes[k], axis=0, tiled=True)  19.9 us
    all_to_all x2, waiting for transfers between devices, copy_for_each(): return lax.all_to_all(copies, axis, split_axis=0, concat_axis=0, tiled=True)  19.4 us
    all_to_all x2, starting transfers between devices, copy_for_each(): return lax.all_to_all(copies, axis, split_axis=0, concat_axis=0, tiled=True)  13.7 us
    another operation x1, local copies, waits for them, and re-layouts, laid_out(): return jnp.moveaxis(pieces, 0, dim).reshape(lengths)  9.77 us
    reshape x4, local copies, waits for them, and re-layouts, local(): key_rows = prefix_pages[opening:closing].reshape(-1, LAT)  8.95 us
    dot_general x4, matrix products, absorb(): jnp.einsum('hqk,kv->hqv', weights.astype(jnp.bfloat16), key_rows[:, :VLAT...  8.79 us
  transfers between devices with their start and end apart: 4, of which 4 were waited for; matrix products, arithmetic and copies ran while one was open for 6% of the time, Pallas kernels for 0%

commit v1 on v0

v1 whole, which is shorter than its diff:
```python
import jax
import jax.numpy as jnp
from jax import lax
from jax.experimental import pallas as pl
from jax.experimental.pallas import tpu as pltpu
from jax.sharding import Mesh
from jax.sharding import PartitionSpec as P

VLAT = 512
VHEAD = 128
PAGE = 64
SUF = 256
HOT = 3
LAT = 576
PPAGES = 32
NEWP = 4
SLOTS = 12
PAIR = 2 * LAT
CHUNKS = PAGE * LAT // PAIR
POOL = ("pool_0", "pool_1", "pool_2")
PLANE = ("pool_1", "pool_2")
SIDE = 4
HOPS = (0, 1, 3, 2)
HEAD_ROWS = 40
TAIL_ROWS = 32
KEYS = 16 * (HEAD_ROWS + TAIL_ROWS)

softmax_scale = 192.0 ** (-0.5)
exponent_scale = softmax_scale * 1.4426950408889634
masked_score = -1e30
MIB = 1 << 20


def select_kernel(owner, slot, place, pool_ref, out_ref):
    me = place[0]
    count = jnp.int32(0)
    chosen = [jnp.int32(0)] * HOT
    for j in range(PPAGES):
        hit = owner[j] == me
        chosen = [jnp.where(hit & (count == k), slot[j], chosen[k]) for k in range(HOT)]
        count = count + hit.astype(jnp.int32)
    row = lax.broadcasted_iota(jnp.int32, (8, SLOTS), 0) % 4
    col = lax.broadcasted_iota(jnp.int32, (8, SLOTS), 1)
    want = jnp.where(row == 0, chosen[0], jnp.where(row == 1, chosen[1], chosen[2]))
    pick = ((col == want) & (row < HOT)).astype(jnp.float32).astype(jnp.bfloat16)
    picked = jnp.dot(pick, pool_ref[...], preferred_element_type=jnp.float32)
    upper = lax.broadcasted_iota(jnp.int32, (8, PAIR), 0) < 4
    for d in range(4):
        first = picked[:, 2 * d * PAIR : (2 * d + 1) * PAIR]
        second = picked[:, (2 * d + 1) * PAIR : (2 * d + 2) * PAIR]
        out_ref[d] = jnp.where(upper, first, second).astype(jnp.bfloat16)


def selected_pieces(owner, slot, place, pool):
    return pl.pallas_call(
        select_kernel,
        out_shape=jax.ShapeDtypeStruct((16, 8, PAIR), jnp.bfloat16),
        grid_spec=pltpu.PrefetchScalarGridSpec(
            num_scalar_prefetch=3,
            grid=(4,),
            in_specs=[pl.BlockSpec((SLOTS, 8 * PAIR), lambda i, *_: (0, i))],
            out_specs=pl.BlockSpec((4, 8, PAIR), lambda i, *_: (i, 0, 0)),
        ),
        compiler_params=pltpu.CompilerParams(vmem_limit_bytes=32 * MIB),
        name="select_pages",
    )(owner, slot, place, pool)


def merge_kernel(owner, place, received_ref, suffix_ref, out_ref, count):
    depth = place[0] // 16
    for j in range(PPAGES):
        count[j] = 0
    row = lax.broadcasted_iota(jnp.int32, (PPAGES, 128), 0)
    col = lax.broadcasted_iota(jnp.int32, (PPAGES, 128), 1)
    source = jnp.full((PPAGES, 128), -1, jnp.int32)
    for j in range(PPAGES):
        holder = owner[j]
        rank = count[holder]
        count[holder] = rank + 1
        at = jnp.where(holder // 16 == depth, (holder % 16) * 8 + rank, -8)
        source = jnp.where(row == j, at, source)
    suffix = suffix_ref[...].astype(jnp.float32)
    place_row = lax.broadcasted_iota(jnp.int32, (8, PAIR), 0)
    own = jnp.zeros((8, PAIR), jnp.float32)
    for t in range(4):
        own = jnp.where(place_row == depth * 4 + t, suffix[:, t * PAIR : (t + 1) * PAIR], own)
    received = received_ref[...]
    halves = []
    for p in range(2):
        pick = (col == source + 4 * p).astype(jnp.float32).astype(jnp.bfloat16)
        halves.append(jnp.dot(pick, received, preferred_element_type=jnp.float32))
    rows = jnp.concatenate([halves[0], own, halves[1]], axis=0)
    turned = pltpu.roll(rows[:, VLAT:], LAT, 1)
    out_ref[:, :VLAT] = rows[:, :VLAT].astype(jnp.bfloat16)
    out_ref[:, VLAT : VLAT + 128] = turned[:, VLAT:].astype(jnp.bfloat16)
    out_ref[:, VLAT + 128 :] = turned[:, :VLAT].astype(jnp.bfloat16)


def merged_rows(owner, place, received, suffix):
    rows = HEAD_ROWS + TAIL_ROWS
    return pl.pallas_call(
        merge_kernel,
        out_shape=jax.ShapeDtypeStruct((rows, PAIR), jnp.bfloat16),
        grid_spec=pltpu.PrefetchScalarGridSpec(
            num_scalar_prefetch=2,
            grid=(1,),
            in_specs=[
                pl.BlockSpec((128, PAIR), lambda i, *_: (0, 0)),
                pl.BlockSpec((1, 4 * PAIR), lambda i, *_: (0, 0)),
            ],
            out_specs=pl.BlockSpec((rows, PAIR), lambda i, *_: (0, 0)),
            scratch_shapes=[pltpu.SMEM((PPAGES,), jnp.int32)],
        ),
        compiler_params=pltpu.CompilerParams(vmem_limit_bytes=32 * MIB),
        name="merge_pages",
    )(owner, place, received, suffix)


def shifted(x, axis, hop):
    return lax.ppermute(x, axis, [(i, (i + hop) % SIDE) for i in range(SIDE)])


def gray(s):
    return s ^ (s >> 1)


def limits(parity, x, y, length):
    lane = lax.broadcasted_iota(jnp.int32, (1, KEYS), 1)
    block, part, page = (lane >> 7) & 3, (lane >> 5) & 3, lane & 31
    head = lane < 512
    far = (x - gray(jnp.where(head, part, block))) & 3
    near = (y - gray(jnp.where(head, block, part))) & 3
    token = page * PAGE + (far * 4 + near) * 4 + jnp.where(head, 0, 2) + parity
    seen = jnp.where(token < length, 0, 1 << 20)
    suffix = lane - 1024
    block, part = (suffix >> 5) & 3, (suffix >> 3) & 3
    far, near = (x - gray(part)) & 3, (y - gray(block)) & 3
    holder = ((suffix >> 2) & 1) * 16 + far * 4 + near
    fresh = holder * 8 + (suffix & 3) * 2 + parity
    return jnp.where(lane < 1024, seen, fresh)


def attend_kernel(place, length, q_ref, *refs):
    heads, tails = refs[:4], refs[4:8]
    w_ref, out_ref, keys, even_q, odd_q, limit = refs[8:]

    @pl.when(pl.program_id(0) == 0)
    def _():
        for b in range(4):
            for s in range(4):
                k = 4 * b + s
                keys[k * 32 : (k + 1) * 32] = heads[b][s * HEAD_ROWS : s * HEAD_ROWS + 32]
                keys[1024 + k * 8 : 1024 + (k + 1) * 8] = heads[b][
                    s * HEAD_ROWS + 32 : (s + 1) * HEAD_ROWS
                ]
            keys[512 + b * 128 : 512 + (b + 1) * 128] = tails[b][...]
        lane = lax.broadcasted_iota(jnp.int32, (SUF, 128), 1)
        for h in range(4):
            if h % 2 == 0:
                whole = q_ref[:, h * LAT : h * LAT + LAT + 64].astype(jnp.float32)
            else:
                whole = q_ref[:, h * LAT - 64 : h * LAT + LAT].astype(jnp.float32)
                whole = pltpu.roll(whole, LAT, 1)
            latent = whole[:, :VLAT].astype(jnp.bfloat16)
            tail = whole[:, VLAT:]
            even_q[h, :, :VLAT] = latent
            odd_q[h, :, 128:] = latent
            odd_q[h, :, :128] = jnp.where(lane < 64, tail, 0.0).astype(jnp.bfloat16)
            even_q[h, :, VLAT:] = jnp.where(lane < 64, 0.0, pltpu.roll(tail, 64, 1)).astype(jnp.bfloat16)
        x, y = (place[0] // 4) % 4, place[0] % 4
        for parity in range(2):
            limit[parity : parity + 1] = limits(parity, x, y, length[0])

    h = pl.program_id(0)
    token = lax.broadcasted_iota(jnp.int32, (SUF, 1), 0)
    contract = (((1,), (1,)), ((), ()))
    scores = []
    for parity, queries, cut in ((0, even_q, 0), (1, odd_q, VLAT)):
        s = lax.dot_general(
            queries[h], keys[:, cut : cut + VLAT + 128], contract, preferred_element_type=jnp.float32
        )
        scores.append(jnp.where(limit[parity : parity + 1] <= token, s, masked_score))
    top = jnp.maximum(
        jnp.max(scores[0], axis=1, keepdims=True), jnp.max(scores[1], axis=1, keepdims=True)
    )
    total = jnp.zeros((SUF, 1), jnp.float32)
    mixture = jnp.zeros((SUF, VLAT), jnp.float32)
    for parity, cut in ((0, 0), (1, VLAT + 128)):
        weights = jnp.exp2((scores[parity] - top) * exponent_scale)
        total = total + jnp.sum(weights, axis=1, keepdims=True)
        mixture = mixture + jnp.dot(
            weights.astype(jnp.bfloat16),
            keys[:, cut : cut + VLAT],
            preferred_element_type=jnp.float32,
        )
    mixture = (mixture / total).astype(jnp.bfloat16)
    w = w_ref[...].reshape(VLAT, VHEAD).astype(jnp.bfloat16)
    out_ref[...] = jnp.dot(mixture, w, preferred_element_type=jnp.float32).astype(jnp.bfloat16)


def attended_rows(place, length, queries, heads, tails, w):
    whole = lambda rows: pl.BlockSpec((rows, PAIR), lambda h, *_: (0, 0))
    return pl.pallas_call(
        attend_kernel,
        out_shape=jax.ShapeDtypeStruct((SUF, 4 * VHEAD), jnp.bfloat16),
        grid_spec=pltpu.PrefetchScalarGridSpec(
            num_scalar_prefetch=2,
            grid=(4,),
            in_specs=[
                pl.BlockSpec((SUF, 4 * LAT), lambda h, *_: (0, 0)),
                *[whole(4 * HEAD_ROWS)] * 4,
                *[whole(4 * TAIL_ROWS)] * 4,
                pl.BlockSpec((8, 1, VLAT // 8, VHEAD), lambda h, *_: (0, h, 0, 0)),
            ],
            out_specs=pl.BlockSpec((SUF, VHEAD), lambda h, *_: (0, h)),
            scratch_shapes=[
                pltpu.VMEM((KEYS, PAIR), jnp.bfloat16),
                pltpu.VMEM((4, SUF, VLAT + 128), jnp.bfloat16),
                pltpu.VMEM((4, SUF, VLAT + 128), jnp.bfloat16),
                pltpu.VMEM((2, KEYS), jnp.int32),
            ],
        ),
        compiler_params=pltpu.CompilerParams(vmem_limit_bytes=48 * MIB),
        name="attend",
    )(place, length, queries, *heads, *tails, w)


def update_kernel(place, new_owner, new_slot, pool_ref, *refs):
    heads, out_ref, fresh = refs[:4], refs[4], refs[5]
    me = place[0]
    page, target = jnp.int32(0), jnp.int32(-1)
    for m in range(NEWP):
        hit = new_owner[m] == me
        page = jnp.where(hit, m, page)
        target = jnp.where(hit, new_slot[m], target)
    for b in range(4):
        for s in range(4):
            k = 4 * b + s
            fresh[k * 8 : (k + 1) * 8] = heads[b][s * HEAD_ROWS + 32 : (s + 1) * HEAD_ROWS]
    x, y = (me // 4) % 4, me % 4
    row = lax.broadcasted_iota(jnp.int32, (CHUNKS, 128), 0)
    col = lax.broadcasted_iota(jnp.int32, (CHUNKS, 128), 1)
    holder = page * 8 + (row >> 2)
    part, block = gray((x - (holder >> 2)) & 3), gray((y - holder) & 3)
    source = block * 32 + part * 8 + (holder >> 4) * 4 + (row & 3)
    pick = (col == source).astype(jnp.float32).astype(jnp.bfloat16)
    rows = jnp.dot(pick, fresh[...], preferred_element_type=jnp.float32)
    turned = pltpu.roll(rows[:, VLAT:], LAT, 1)
    rows = jnp.concatenate([rows[:, :VLAT], turned], axis=1)
    mine = lax.broadcasted_iota(jnp.int32, (SLOTS, PAIR), 0) == target
    for c in range(CHUNKS):
        old = pool_ref[:, c * PAIR : (c + 1) * PAIR].astype(jnp.float32)
        out_ref[:, c * PAIR : (c + 1) * PAIR] = jnp.where(mine, rows[c : c + 1], old).astype(jnp.bfloat16)


def updated_pool(place, new_owner, new_slot, pool, heads):
    return pl.pallas_call(
        update_kernel,
        out_shape=jax.ShapeDtypeStruct(pool.shape, pool.dtype),
        grid_spec=pltpu.PrefetchScalarGridSpec(
            num_scalar_prefetch=3,
            grid=(1,),
            in_specs=[
                pl.BlockSpec(pool.shape, lambda i, *_: (0, 0)),
                *[pl.BlockSpec((4 * HEAD_ROWS, PAIR), lambda i, *_: (0, 0))] * 4,
            ],
            out_specs=pl.BlockSpec(pool.shape, lambda i, *_: (0, 0)),
            scratch_shapes=[pltpu.VMEM((128, PAIR), jnp.bfloat16)],
        ),
        compiler_params=pltpu.CompilerParams(vmem_limit_bytes=32 * MIB),
        name="update_pool",
    )(place, new_owner, new_slot, pool, *heads)


def local(queries, new_latent, pool, page_owner, page_slot, new_owner, new_slot, prefix_len, w_uv):
    place = lax.axis_index(POOL).astype(jnp.int32)[None]
    w = lax.all_gather(w_uv.astype(jnp.float32), "serve", axis=0)
    pieces = selected_pieces(page_owner[0], page_slot[0], place, pool[0])
    received = lax.all_to_all(pieces, PLANE, 0, 0, tiled=True).reshape(128, PAIR)
    mine = merged_rows(page_owner[0], place, received, new_latent)
    both = mine + lax.ppermute(mine, "pool_0", [(0, 1), (1, 0)])
    head, tail = both[:HEAD_ROWS], both[HEAD_ROWS:]
    head_row = jnp.concatenate([head] + [shifted(head, "pool_1", k) for k in HOPS[1:]])
    tail_row = jnp.concatenate([tail] + [shifted(tail, "pool_2", k) for k in HOPS[1:]])
    heads = [head_row] + [shifted(head_row, "pool_2", k) for k in HOPS[1:]]
    tails = [tail_row] + [shifted(tail_row, "pool_1", k) for k in HOPS[1:]]
    attended = attended_rows(place, prefix_len, queries[0], heads, tails, w)
    updated = updated_pool(place, new_owner[0], new_slot[0], pool[0], heads)
    return (attended[None], updated[None])


def solution(mesh):
    split = Mesh(
        mesh.devices.reshape(2, 4, 4, mesh.shape["serve"]), ("pool_0", "pool_1", "pool_2", "serve")
    )
    placed = (
        P("serve", None, POOL),
        P("serve", POOL),
        P("serve", POOL, None),
        P("serve", None),
        P("serve", None),
        P("serve", None),
        P("serve", None),
        P("serve"),
        P(POOL, "serve", None),
    )
    return jax.shard_map(
        local,
        mesh=split,
        in_specs=placed,
        out_specs=(P("serve", None, POOL), P("serve", POOL, None)),
        check_vma=False,
    )
```

time: 236 us -> 106 us (0.45)
  local copies, waits for them, and re-layouts: 66.1 us -> 5.53 us
  waiting for transfers between devices: 85.5 us -> 26.2 us
  matrix products: 23 us -> 0 us
  Pallas kernels: 0 us -> 17.4 us
  starting transfers between devices: 13.8 us -> 23.7 us
  other arithmetic: 9.97 us -> 1.6 us
  blocking collectives: 19.9 us -> 15.7 us
    all_gather x2 -> x1, waiting for transfers between devices: 66.1 us -> 0.01 us  [local(): w = lax.all_gather(w_uv.astype(jnp.float32), 'serve', axis=0)]
    reshape x6 -> x0, local copies, waits for them, and re-layouts: 31.2 us -> none  [the longest x2 22.2 us: all_blocks(): pieces = pieces.reshape(*carried, *x.shape)]
    ppermute x0 -> x13, waiting for transfers between devices: none -> 26.2 us  [the longest x12 16.6 us: shifted(): return lax.ppermute(x, axis, [(i, (i + hop) % SIDE) for i in range(SIDE)])]
    ppermute x0 -> x13, starting transfers between devices: none -> 23.6 us  [the longest x12 18.1 us: shifted(): return lax.ppermute(x, axis, [(i, (i + hop) % SIDE) for i in range(SIDE)])]
    dot_general x11 -> x0, matrix products: 23 us -> none  [the longest x4 8.79 us: absorb(): jnp.einsum('hqk,kv->hqv', weights.astype(jnp.bfloat16), key_rows[:, :VLAT...]
    all_gather x1 -> x0, blocking collectives: 19.9 us -> none  [all_blocks(): pieces = lax.all_gather(pieces, axes[k], axis=0, tiled=True)]
    all_to_all x2 -> x0, waiting for transfers between devices: 19.4 us -> none  [copy_for_each(): return lax.all_to_all(copies, axis, split_axis=0, concat_axis=0, tiled=True)]
    pallas_call x0 -> x4, Pallas kernels: none -> 17.4 us  [the longest x1 12.3 us: attended_rows(): pl.pallas_call(attend_kernel, out_shape=jax.ShapeDtypeStruct((SUF, 4 * VH...]
  transfers between devices with their start and end apart: 4 -> 14, of which waited for: 4 -> 9; matrix products, arithmetic and copies ran while one was open for 6% -> 0% of each run, Pallas kernels for 0% -> 5%
where the time goes in v1:
time: 106 us; the launch traced here: 105 us
  waiting for transfers between devices  26.2 us (25%)
  starting transfers between devices  23.7 us (22%)
  Pallas kernels  17.4 us (16%)
  blocking collectives  15.7 us (15%)
  between operations  14.8 us (14%)
  local copies, waits for them, and re-layouts  5.53 us (5%)
  other arithmetic  1.6 us (2%)
    ppermute x12, starting transfers between devices, shifted(): return lax.ppermute(x, axis, [(i, (i + hop) % SIDE) for i in range(SIDE)])  18.1 us
    ppermute x12, waiting for transfers between devices, shifted(): return lax.ppermute(x, axis, [(i, (i + hop) % SIDE) for i in range(SIDE)])  16.6 us
    all_to_all x1, blocking collectives, local(): lax.all_to_all(pieces, PLANE, 0, 0, tiled=True).reshape(128, PAIR)  15.7 us
    pallas_call x1, Pallas kernels, attended_rows(): pl.pallas_call(attend_kernel, out_shape=jax.ShapeDtypeStruct((SUF, 4 * VH...  12.3 us
    ppermute x1, waiting for transfers between devices, local(): both = mine + lax.ppermute(mine, 'pool_0', [(0, 1), (1, 0)])  9.66 us
    unnamed x22, local copies, waits for them, and re-layouts  5.52 us
    ppermute x1, starting transfers between devices, local(): both = mine + lax.ppermute(mine, 'pool_0', [(0, 1), (1, 0)])  5.48 us
  transfers between devices with their start and end apart: 14, of which 9 were waited for; matrix products, arithmetic and copies ran while one was open for 0% of the time, Pallas kernels for 5%

profile of v1, /device:TPU:64, one launch (start us, length us, event | category | flops | bytes accessed | tf_op | source)
XLA Modules:
  0.0 104.9 jit_solution(10614377008572582198)
XLA Ops:
  7.2 1.5 %all_gather.12 = f32[4,64,128]{2,1,0:T(8,128)} convert(bf16[4,64,128]{2,1,0:T(8,128)(2,1)} %param.17) | non-fusion elementwise | flops 32768 | bytes 196608 | tf_op jit(solution)/shard_map/all_gather | solution.py:277
  8.8 1.3 %copy-done = bf16[1,12,36864]{2,1,0:T(8,128)(2,1)S(1)} copy-done((bf16[1,12,36864]{2,1,0:T(8,128)(2,1)S(1)}, bf16[1,12,36864]{2,1,0:T(8,128)(2,1)}, u32[]{:S(2)}) %copy-start) | copy-done | bytes 884760
  11.3 2.0 %select_pages.1 = bf16[16,8,1152]{2,1,0:T(8,128)(2,1)S(1)} custom-call(s32[32]{0:T(128)S(1)} %bitcast.16, s32[32]{0:T(128)S(1)} %bitcast.18, s32[1]{0:T(128)} %bitcast.place, bf16[12,36864]{1,0:T(8,128)(2,1)S(1)} %bitcast.11), custom_call_target="tpu_custom_call" | custom-call | tf_op jit(solution)/shard_map/select_pages/pallas_call | solution.py:55
  13.4 15.7 %all_to_all.5 = bf16[16,8,1152]{2,1,0:T(8,128)(2,1)S(1)} all-to-all(bf16[16,8,1152]{2,1,0:T(8,128)(2,1)S(1)} %select_pages.1), channel_id=1, replica_groups=mesh['pool_0'=2,'pool_1'=4,'pool_2'=4,'serve'=8] {'pool_1','pool_2'}, dimensions={0} | all-to-all | bytes 589824 | tf_op jit(solution)/shard_map/all_to_all | solution.py:279
  29.0 1.0 %merge_pages.1 = bf16[72,1152]{1,0:T(8,128)(2,1)S(1)} custom-call(s32[32]{0:T(128)S(1)} %bitcast.17, s32[1]{0:T(128)} %bitcast.place, bf16[128,1152]{1,0:T(8,128)(2,1)S(1)} %bitcast.13, bf16[1,4608]{1,0:T(2,128)(2,1)S(1)} %copy-done.6), custom_call_target="tpu_custom_call" | custom-call | tf_op jit(solution)/shard_map/merge_pages/pallas_call | solution.py:101
  30.1 5.5 %collective-permute-start = (bf16[72,1152]{1,0:T(8,128)(2,1)S(1)}, bf16[72,1152]{1,0:T(8,128)(2,1)S(1)}, u32[]{:S(2)}, u32[]{:S(2)}) collective-permute-start(bf16[72,1152]{1,0:T(8,128)(2,1)S(1)} %merge_pages.1), channel_id=1, source_target_pairs={{0,128},{128,0},{1,129},{129,1},{2,130},{130,2},{3,131},{131,3},{4... | collective-permute-start | bytes 497672 | tf_op jit(solution)/shard_map/ppermute | solution.py:281
  35.6 9.7 %collective-permute-done = bf16[72,1152]{1,0:T(8,128)(2,1)S(1)} collective-permute-done((bf16[72,1152]{1,0:T(8,128)(2,1)S(1)}, bf16[72,1152]{1,0:T(8,128)(2,1)S(1)}, u32[]{:S(2)}, u32[]{:S(2)}) %collective-permute-start) | collective-permute-done | bytes 165920 | tf_op jit(solution)/shard_map/ppermute | solution.py:281
  45.3 2.5 %collective-permute-start.3 = (bf16[40,1152]{1,0:T(8,128)(2,1)S(1)}, bf16[40,1152]{1,0:T(8,128)(2,1)S(1)}, u32[]{:S(2)}, u32[]{:S(2)}) collective-permute-start(bf16[40,1152]{1,0:T(8,128)(2,1)S(1)} %slice.8), channel_id=1, source_target_pairs={{0,64},{32,96},{64,0},{96,32},{1,65},{33,97},{65,1},{97,33},{2,66}... | collective-permute-start | bytes 276488 | tf_op jit(solution)/shard_map/ppermute | solution.py:120
  47.8 1.4 %collective-permute-start.2 = (bf16[40,1152]{1,0:T(8,128)(2,1)S(1)}, bf16[40,1152]{1,0:T(8,128)(2,1)S(1)}, u32[]{:S(2)}, u32[]{:S(2)}) collective-permute-start(bf16[40,1152]{1,0:T(8,128)(2,1)S(1)} %slice.8), channel_id=1, source_target_pairs={{0,96},{32,0},{64,32},{96,64},{1,97},{33,1},{65,33},{97,65},{2,98}... | collective-permute-start | bytes 276488 | tf_op jit(solution)/shard_map/ppermute | solution.py:120
  49.8 2.4 %collective-permute-done.3 = bf16[40,1152]{1,0:T(8,128)(2,1)S(1)} collective-permute-done((bf16[40,1152]{1,0:T(8,128)(2,1)S(1)}, bf16[40,1152]{1,0:T(8,128)(2,1)S(1)}, u32[]{:S(2)}, u32[]{:S(2)}) %collective-permute-start.3) | collective-permute-done | bytes 92192 | tf_op jit(solution)/shard_map/ppermute | solution.py:120
  52.4 2.6 %collective-permute-done.1 = bf16[40,1152]{1,0:T(8,128)(2,1)S(1)} collective-permute-done((bf16[40,1152]{1,0:T(8,128)(2,1)S(1)}, bf16[40,1152]{1,0:T(8,128)(2,1)S(1)}, u32[]{:S(2)}, u32[]{:S(2)}) %collective-permute-start.1) | collective-permute-done | bytes 92192 | tf_op jit(solution)/shard_map/ppermute | solution.py:120
  55.0 2.2 %collective-permute-start.6 = (bf16[160,1152]{1,0:T(8,128)(2,1)S(1)}, bf16[160,1152]{1,0:T(8,128)(2,1)S(1)}, u32[]{:S(2)}, u32[]{:S(2)}) collective-permute-start(bf16[160,1152]{1,0:T(8,128)(2,1)S(1)} %pad_maximum_fusion.refs_0_), channel_id=1, source_target_pairs={{0,16},{8,24},{16,0},{24,8},{1,17},{9,25},{17,1},{25,9},{2,18},{10... | collective-permute-start | bytes 1105928 | tf_op jit(solution)/shard_map/ppermute | solution.py:120
  57.2 1.5 %collective-permute-start.9 = (bf16[32,1152]{1,0:T(8,128)(2,1)S(1)}, bf16[32,1152]{1,0:T(8,128)(2,1)S(1)}, u32[]{:S(2)}, u32[]{:S(2)}) collective-permute-start(bf16[32,1152]{1,0:T(8,128)(2,1)S(1)} %slice.9), channel_id=1, source_target_pairs={{0,16},{8,24},{16,0},{24,8},{1,17},{9,25},{17,1},{25,9},{2,18},{10... | collective-permute-start | bytes 221192 | tf_op jit(solution)/shard_map/ppermute | solution.py:120
  58.7 1.4 %collective-permute-start.8 = (bf16[32,1152]{1,0:T(8,128)(2,1)S(1)}, bf16[32,1152]{1,0:T(8,128)(2,1)S(1)}, u32[]{:S(2)}, u32[]{:S(2)}) collective-permute-start(bf16[32,1152]{1,0:T(8,128)(2,1)S(1)} %slice.9), channel_id=1, source_target_pairs={{0,24},{8,0},{16,8},{24,16},{1,25},{9,1},{17,9},{25,17},{2,26},{10... | collective-permute-start | bytes 221192 | tf_op jit(solution)/shard_map/ppermute | solution.py:120
  60.7 2.6 %collective-permute-start.5 = (bf16[160,1152]{1,0:T(8,128)(2,1)S(1)}, bf16[160,1152]{1,0:T(8,128)(2,1)S(1)}, u32[]{:S(2)}, u32[]{:S(2)}) collective-permute-start(bf16[160,1152]{1,0:T(8,128)(2,1)S(1)} %pad_maximum_fusion.refs_0_), channel_id=1, source_target_pairs={{0,24},{8,0},{16,8},{24,16},{1,25},{9,1},{17,9},{25,17},{2,26},{10... | collective-permute-start | bytes 1105928 | tf_op jit(solution)/shard_map/ppermute | solution.py:120
  63.3 4.1 %collective-permute-done.9 = bf16[32,1152]{1,0:T(8,128)(2,1)S(1)} collective-permute-done((bf16[32,1152]{1,0:T(8,128)(2,1)S(1)}, bf16[32,1152]{1,0:T(8,128)(2,1)S(1)}, u32[]{:S(2)}, u32[]{:S(2)}) %collective-permute-start.9) | collective-permute-done | bytes 73760 | tf_op jit(solution)/shard_map/ppermute | solution.py:120
  67.4 3.1 %collective-permute-start.4 = (bf16[160,1152]{1,0:T(8,128)(2,1)S(1)}, bf16[160,1152]{1,0:T(8,128)(2,1)S(1)}, u32[]{:S(2)}, u32[]{:S(2)}) collective-permute-start(bf16[160,1152]{1,0:T(8,128)(2,1)S(1)} %pad_maximum_fusion.refs_0_), channel_id=1, source_target_pairs={{0,8},{8,16},{16,24},{24,0},{1,9},{9,17},{17,25},{25,1},{2,10},{10... | collective-permute-start | bytes 1105928 | tf_op jit(solution)/shard_map/ppermute | solution.py:120
  70.8 1.8 %collective-permute-start.11 = (bf16[128,1152]{1,0:T(8,128)(2,1)S(1)}, bf16[128,1152]{1,0:T(8,128)(2,1)S(1)}, u32[]{:S(2)}, u32[]{:S(2)}) collective-permute-start(bf16[128,1152]{1,0:T(8,128)(2,1)S(1)} %pad_maximum_fusion.1.refs_4_), channel_id=1, source_target_pairs={{0,96},{32,0},{64,32},{96,64},{1,97},{33,1},{65,33},{97,65},{2,98}... | collective-permute-start | bytes 884744 | tf_op jit(solution)/shard_map/ppermute | solution.py:120
  73.5 1.5 %collective-permute-done.5.refs_2_ = bf16[160,1152]{1,0:T(8,128)(2,1)S(1)} collective-permute-done((bf16[160,1152]{1,0:T(8,128)(2,1)S(1)}, bf16[160,1152]{1,0:T(8,128)(2,1)S(1)}, u32[]{:S(2)}, u32[]{:S(2)}) %collective-permute-start.5) | collective-permute-done | bytes 368672 | tf_op jit(solution)/shard_map/ppermute | solution.py:120
  75.0 1.7 %collective-permute-done.4.refs_1_ = bf16[160,1152]{1,0:T(8,128)(2,1)S(1)} collective-permute-done((bf16[160,1152]{1,0:T(8,128)(2,1)S(1)}, bf16[160,1152]{1,0:T(8,128)(2,1)S(1)}, u32[]{:S(2)}, u32[]{:S(2)}) %collective-permute-start.4) | collective-permute-done | bytes 368672 | tf_op jit(solution)/shard_map/ppermute | solution.py:120
  76.7 2.0 %update_pool.1 = bf16[12,36864]{1,0:T(8,128)(2,1)} custom-call(s32[1]{0:T(128)} %bitcast.place, s32[4]{0:T(128)S(1)} %bitcast.19, s32[4]{0:T(128)S(1)} %bitcast.20, bf16[12,36864]{1,0:T(8,128)(2,1)S(1)} %bitcast.12, bf16[160,1152]{1,0:T(8,128)(2,1)S(1)} %pad_maximum_fusion.refs_0_, bf16[160,1152]{1,0:T(8,128)(2,1)S(1)} %collective-permute-done.4.refs_1_, ...), custom_call_target="tpu_custom_call" | custom-call | tf_op jit(solution)/shard_map/update_pool/pallas_call | solution.py:257
  78.9 3.8 %collective-permute-done.11.refs_6_ = bf16[128,1152]{1,0:T(8,128)(2,1)S(1)} collective-permute-done((bf16[128,1152]{1,0:T(8,128)(2,1)S(1)}, bf16[128,1152]{1,0:T(8,128)(2,1)S(1)}, u32[]{:S(2)}, u32[]{:S(2)}) %collective-permute-start.11) | collective-permute-done | bytes 294944 | tf_op jit(solution)/shard_map/ppermute | solution.py:120
  83.5 1.2 %copy-done.3 = f32[32,64,128]{2,1,0:T(8,128)S(1)} copy-done((f32[32,64,128]{2,1,0:T(8,128)S(1)}, f32[32,64,128]{2,1,0:T(8,128)}, u32[]{:S(2)}) %copy-start.3) | copy-done | bytes 1048600
  85.7 12.3 %attend.1 = bf16[256,512]{1,0:T(8,128)(2,1)} custom-call(s32[1]{0:T(128)} %bitcast.place, s32[1]{0:T(128)S(6)} %copy.11.length, bf16[256,2304]{1,0:T(8,128)(2,1)S(1)} %bitcast.14, bf16[160,1152]{1,0:T(8,128)(2,1)S(1)} %pad_maximum_fusion.refs_0_, bf16[160,1152]{1,0:T(8,128)(2,1)S(1)} %collective-permute-done.4.refs_1_, ...), custom_call_target="tpu_custom_call" | custom-call | tf_op jit(solution)/shard_map/attend/pallas_call | solution.py:203
  (38 shorter events, 5.2 us)
Async XLA Ops:
  7.2 21.9 %copy-start.6 = (bf16[1,4608]{1,0:T(2,128)(2,1)S(1)}, bf16[1,4608]{1,0:T(2,128)(2,1)}, u32[]{:S(2)}) copy-start(bf16[1,4608]{1,0:T(2,128)(2,1)} %suffix_ref.1) | copy-start | bytes 27652
  7.2 76.3 %all-gather.3.cloned.1.call-start = ((), (), s32[]{:S(2)}) async-start(), calls=%async_computation.1 | async-start | bytes 1179648 | tf_op jit(solution)/shard_map/all_gather | solution.py:277
  8.8 1.3 %copy-start = (bf16[1,12,36864]{2,1,0:T(8,128)(2,1)S(1)}, bf16[1,12,36864]{2,1,0:T(8,128)(2,1)}, u32[]{:S(2)}) copy-start(bf16[1,12,36864]{2,1,0:T(8,128)(2,1)} %param.11) | copy-start | bytes 2654212
  10.0 0.7 copy-start.7
  30.1 46.6 %copy-start.1 = (bf16[1,12,36864]{2,1,0:T(8,128)(2,1)S(1)}, bf16[1,12,36864]{2,1,0:T(8,128)(2,1)}, u32[]{:S(2)}) copy-start(bf16[1,12,36864]{2,1,0:T(8,128)(2,1)} %param.11) | copy-start | bytes 2654212
  30.1 46.6 %copy-start.9 = (s32[1,4]{1,0:T(1,128)S(1)}, s32[1,4]{1,0:T(1,128)}, u32[]{:S(2)}) copy-start(s32[1,4]{1,0:T(1,128)} %param.14) | copy-start | bytes 52
  30.1 46.6 %copy-start.10 = (s32[1,4]{1,0:T(1,128)S(1)}, s32[1,4]{1,0:T(1,128)}, u32[]{:S(2)}) copy-start(s32[1,4]{1,0:T(1,128)} %param.15) | copy-start | bytes 52
  30.1 15.1 %collective-permute-start = (bf16[72,1152]{1,0:T(8,128)(2,1)S(1)}, bf16[72,1152]{1,0:T(8,128)(2,1)S(1)}, u32[]{:S(2)}, u32[]{:S(2)}) collective-permute-start(bf16[72,1152]{1,0:T(8,128)(2,1)S(1)} %merge_pages.1), channel_id=1, source_target_pairs={{0,128},{128,0},{1,129},{129,1},{2,130},{130,2},{3,131},{131,3},{4... | collective-permute-start | bytes 497672 | tf_op jit(solution)/shard_map/ppermute | solution.py:281
  45.3 6.9 %collective-permute-start.3 = (bf16[40,1152]{1,0:T(8,128)(2,1)S(1)}, bf16[40,1152]{1,0:T(8,128)(2,1)S(1)}, u32[]{:S(2)}, u32[]{:S(2)}) collective-permute-start(bf16[40,1152]{1,0:T(8,128)(2,1)S(1)} %slice.8), channel_id=1, source_target_pairs={{0,64},{32,96},{64,0},{96,32},{1,65},{33,97},{65,1},{97,33},{2,66}... | collective-permute-start | bytes 276488 | tf_op jit(solution)/shard_map/ppermute | solution.py:120
  47.8 4.6 %collective-permute-start.2 = (bf16[40,1152]{1,0:T(8,128)(2,1)S(1)}, bf16[40,1152]{1,0:T(8,128)(2,1)S(1)}, u32[]{:S(2)}, u32[]{:S(2)}) collective-permute-start(bf16[40,1152]{1,0:T(8,128)(2,1)S(1)} %slice.8), channel_id=1, source_target_pairs={{0,96},{32,0},{64,32},{96,64},{1,97},{33,1},{65,33},{97,65},{2,98}... | collective-permute-start | bytes 276488 | tf_op jit(solution)/shard_map/ppermute | solution.py:120
  49.2 5.8 %collective-permute-start.1 = (bf16[40,1152]{1,0:T(8,128)(2,1)S(1)}, bf16[40,1152]{1,0:T(8,128)(2,1)S(1)}, u32[]{:S(2)}, u32[]{:S(2)}) collective-permute-start(bf16[40,1152]{1,0:T(8,128)(2,1)S(1)} %slice.8), channel_id=1, source_target_pairs={{0,32},{32,64},{64,96},{96,0},{1,33},{33,65},{65,97},{97,1},{2,34}... | collective-permute-start | bytes 276488 | tf_op jit(solution)/shard_map/ppermute | solution.py:120
  55.0 17.6 %collective-permute-start.6 = (bf16[160,1152]{1,0:T(8,128)(2,1)S(1)}, bf16[160,1152]{1,0:T(8,128)(2,1)S(1)}, u32[]{:S(2)}, u32[]{:S(2)}) collective-permute-start(bf16[160,1152]{1,0:T(8,128)(2,1)S(1)} %pad_maximum_fusion.refs_0_), channel_id=1, source_target_pairs={{0,16},{8,24},{16,0},{24,8},{1,17},{9,25},{17,1},{25,9},{2,18},{10... | collective-permute-start | bytes 1105928 | tf_op jit(solution)/shard_map/ppermute | solution.py:120
  57.2 10.2 %collective-permute-start.9 = (bf16[32,1152]{1,0:T(8,128)(2,1)S(1)}, bf16[32,1152]{1,0:T(8,128)(2,1)S(1)}, u32[]{:S(2)}, u32[]{:S(2)}) collective-permute-start(bf16[32,1152]{1,0:T(8,128)(2,1)S(1)} %slice.9), channel_id=1, source_target_pairs={{0,16},{8,24},{16,0},{24,8},{1,17},{9,25},{17,1},{25,9},{2,18},{10... | collective-permute-start | bytes 221192 | tf_op jit(solution)/shard_map/ppermute | solution.py:120
  58.7 11.8 %collective-permute-start.8 = (bf16[32,1152]{1,0:T(8,128)(2,1)S(1)}, bf16[32,1152]{1,0:T(8,128)(2,1)S(1)}, u32[]{:S(2)}, u32[]{:S(2)}) collective-permute-start(bf16[32,1152]{1,0:T(8,128)(2,1)S(1)} %slice.9), channel_id=1, source_target_pairs={{0,24},{8,0},{16,8},{24,16},{1,25},{9,1},{17,9},{25,17},{2,26},{10... | collective-permute-start | bytes 221192 | tf_op jit(solution)/shard_map/ppermute | solution.py:120
  60.1 10.4 %collective-permute-start.7 = (bf16[32,1152]{1,0:T(8,128)(2,1)S(1)}, bf16[32,1152]{1,0:T(8,128)(2,1)S(1)}, u32[]{:S(2)}, u32[]{:S(2)}) collective-permute-start(bf16[32,1152]{1,0:T(8,128)(2,1)S(1)} %slice.9), channel_id=1, source_target_pairs={{0,8},{8,16},{16,24},{24,0},{1,9},{9,17},{17,25},{25,1},{2,10},{10... | collective-permute-start | bytes 221192 | tf_op jit(solution)/shard_map/ppermute | solution.py:120
  60.7 14.3 %collective-permute-start.5 = (bf16[160,1152]{1,0:T(8,128)(2,1)S(1)}, bf16[160,1152]{1,0:T(8,128)(2,1)S(1)}, u32[]{:S(2)}, u32[]{:S(2)}) collective-permute-start(bf16[160,1152]{1,0:T(8,128)(2,1)S(1)} %pad_maximum_fusion.refs_0_), channel_id=1, source_target_pairs={{0,24},{8,0},{16,8},{24,16},{1,25},{9,1},{17,9},{25,17},{2,26},{10... | collective-permute-start | bytes 1105928 | tf_op jit(solution)/shard_map/ppermute | solution.py:120
  67.4 9.3 %collective-permute-start.4 = (bf16[160,1152]{1,0:T(8,128)(2,1)S(1)}, bf16[160,1152]{1,0:T(8,128)(2,1)S(1)}, u32[]{:S(2)}, u32[]{:S(2)}) collective-permute-start(bf16[160,1152]{1,0:T(8,128)(2,1)S(1)} %pad_maximum_fusion.refs_0_), channel_id=1, source_target_pairs={{0,8},{8,16},{16,24},{24,0},{1,9},{9,17},{17,25},{25,1},{2,10},{10... | collective-permute-start | bytes 1105928 | tf_op jit(solution)/shard_map/ppermute | solution.py:120
  70.5 8.4 %collective-permute-start.12 = (bf16[128,1152]{1,0:T(8,128)(2,1)S(1)}, bf16[128,1152]{1,0:T(8,128)(2,1)S(1)}, u32[]{:S(2)}, u32[]{:S(2)}) collective-permute-start(bf16[128,1152]{1,0:T(8,128)(2,1)S(1)} %pad_maximum_fusion.1.refs_4_), channel_id=1, source_target_pairs={{0,64},{32,96},{64,0},{96,32},{1,65},{33,97},{65,1},{97,33},{2,66}... | collective-permute-start | bytes 884744 | tf_op jit(solution)/shard_map/ppermute | solution.py:120
  70.8 12.0 %collective-permute-start.11 = (bf16[128,1152]{1,0:T(8,128)(2,1)S(1)}, bf16[128,1152]{1,0:T(8,128)(2,1)S(1)}, u32[]{:S(2)}, u32[]{:S(2)}) collective-permute-start(bf16[128,1152]{1,0:T(8,128)(2,1)S(1)} %pad_maximum_fusion.1.refs_4_), channel_id=1, source_target_pairs={{0,96},{32,0},{64,32},{96,64},{1,97},{33,1},{65,33},{97,65},{2,98}... | collective-permute-start | bytes 884744 | tf_op jit(solution)/shard_map/ppermute | solution.py:120
  72.6 10.2 %collective-permute-start.10 = (bf16[128,1152]{1,0:T(8,128)(2,1)S(1)}, bf16[128,1152]{1,0:T(8,128)(2,1)S(1)}, u32[]{:S(2)}, u32[]{:S(2)}) collective-permute-start(bf16[128,1152]{1,0:T(8,128)(2,1)S(1)} %pad_maximum_fusion.1.refs_4_), channel_id=1, source_target_pairs={{0,32},{32,64},{64,96},{96,0},{1,33},{33,65},{65,97},{97,1},{2,34}... | collective-permute-start | bytes 884744 | tf_op jit(solution)/shard_map/ppermute | solution.py:120
  76.7 6.8 %copy-start.2 = (bf16[1,256,2304]{2,1,0:T(8,128)(2,1)S(1)}, bf16[1,256,2304]{2,1,0:T(8,128)(2,1)}, u32[]{:S(2)}) copy-start(bf16[1,256,2304]{2,1,0:T(8,128)(2,1)} %param.9) | copy-start | bytes 3538948
  82.8 0.7 copy-start.4
  83.5 1.2 %copy-start.3 = (f32[32,64,128]{2,1,0:T(8,128)S(1)}, f32[32,64,128]{2,1,0:T(8,128)}, u32[]{:S(2)}) copy-start(f32[32,64,128]{2,1,0:T(8,128)} %all-gather.3.cloned.1.call-done) | copy-start | bytes 3145732
  84.7 1.0 copy-start.5
  (1 other events, 0.7 us)
Sparse Core Ops, SparseCore 0:
  10.4 36.7 all-gather.2

commit v2 on v1

v2 whole, which is shorter than its diff:
```python
import jax
import jax.numpy as jnp
from jax import lax
from jax.experimental import pallas as pl
from jax.experimental.pallas import tpu as pltpu
from jax.sharding import Mesh
from jax.sharding import PartitionSpec as P

VLAT = 512
VHEAD = 128
PAGE = 64
SUF = 256
HOT = 3
LAT = 576
PPAGES = 32
NEWP = 4
SLOTS = 12
PAIR = 2 * LAT
CHUNKS = PAGE * LAT // PAIR
POOL = ("pool_0", "pool_1", "pool_2")
PLANE = ("pool_1", "pool_2")
SERVE = ("serve_0", "serve_1")
SIDE = 4
HOPS = (0, 1, 3, 2)
HEAD_ROWS = 40
TAIL_ROWS = 32
KEYS = 16 * (HEAD_ROWS + TAIL_ROWS)

softmax_scale = 192.0 ** (-0.5)
exponent_scale = softmax_scale * 1.4426950408889634
masked_score = -1e30
MIB = 1 << 20


def select_kernel(owner, slot, place, pool_hbm, out_ref, rows, arrived):
    copies = []
    for i in range(4):
        columns = slice(i * 8 * PAIR, (i + 1) * 8 * PAIR)
        copies.append(
            pltpu.make_async_copy(pool_hbm.at[:, columns], rows.at[:, columns], arrived.at[i])
        )
        copies[i].start()
    me = place[0]
    count = jnp.int32(0)
    chosen = [jnp.int32(0)] * HOT
    for j in range(PPAGES):
        hit = owner[0, j] == me
        chosen = [jnp.where(hit & (count == k), slot[0, j], chosen[k]) for k in range(HOT)]
        count = count + hit.astype(jnp.int32)
    row = lax.broadcasted_iota(jnp.int32, (8, SLOTS), 0) % 4
    col = lax.broadcasted_iota(jnp.int32, (8, SLOTS), 1)
    want = jnp.where(row == 0, chosen[0], jnp.where(row == 1, chosen[1], chosen[2]))
    pick = ((col == want) & (row < HOT)).astype(jnp.float32).astype(jnp.bfloat16)
    upper = lax.broadcasted_iota(jnp.int32, (8, PAIR), 0) < 4
    for d in range(16):
        if d % 4 == 0:
            copies[d // 4].wait()
        both = rows[:, 2 * d * PAIR : (2 * d + 2) * PAIR]
        picked = jnp.dot(pick, both, preferred_element_type=jnp.float32)
        out_ref[d] = jnp.where(upper, picked[:, :PAIR], picked[:, PAIR:]).astype(jnp.bfloat16)


def selected_pieces(owner, slot, place, pool):
    return pl.pallas_call(
        select_kernel,
        out_shape=jax.ShapeDtypeStruct((16, 8, PAIR), jnp.bfloat16),
        grid_spec=pltpu.PrefetchScalarGridSpec(
            num_scalar_prefetch=3,
            grid=(1,),
            in_specs=[pl.BlockSpec(memory_space=pltpu.HBM)],
            out_specs=pl.BlockSpec((16, 8, PAIR), lambda i, *_: (0, 0, 0)),
            scratch_shapes=[
                pltpu.VMEM((SLOTS, PAGE * LAT), jnp.bfloat16),
                pltpu.SemaphoreType.DMA((4,)),
            ],
        ),
        compiler_params=pltpu.CompilerParams(vmem_limit_bytes=32 * MIB),
        name="select_pages",
    )(owner, slot, place, pool)


def merge_kernel(owner, place, received_ref, suffix_ref, out_ref, count):
    depth = place[0] // 16
    for j in range(PPAGES):
        count[j] = 0
    row = lax.broadcasted_iota(jnp.int32, (PPAGES, 128), 0)
    col = lax.broadcasted_iota(jnp.int32, (PPAGES, 128), 1)
    source = jnp.full((PPAGES, 128), -1, jnp.int32)
    for j in range(PPAGES):
        holder = owner[0, j]
        rank = count[holder]
        count[holder] = rank + 1
        at = jnp.where(holder // 16 == depth, (holder % 16) * 8 + rank, -8)
        source = jnp.where(row == j, at, source)
    suffix = suffix_ref[...].astype(jnp.float32)
    place_row = lax.broadcasted_iota(jnp.int32, (8, PAIR), 0)
    own = jnp.zeros((8, PAIR), jnp.float32)
    for t in range(4):
        own = jnp.where(place_row == depth * 4 + t, suffix[:, t * PAIR : (t + 1) * PAIR], own)
    received = received_ref[...]
    halves = []
    for p in range(2):
        pick = (col == source + 4 * p).astype(jnp.float32).astype(jnp.bfloat16)
        halves.append(jnp.dot(pick, received, preferred_element_type=jnp.float32))
    rows = jnp.concatenate([halves[0], own, halves[1]], axis=0)
    turned = pltpu.roll(rows[:, VLAT:], LAT, 1)
    out_ref[:, :VLAT] = rows[:, :VLAT].astype(jnp.bfloat16)
    out_ref[:, VLAT : VLAT + 128] = turned[:, VLAT:].astype(jnp.bfloat16)
    out_ref[:, VLAT + 128 :] = turned[:, :VLAT].astype(jnp.bfloat16)


def merged_rows(owner, place, received, suffix):
    rows = HEAD_ROWS + TAIL_ROWS
    return pl.pallas_call(
        merge_kernel,
        out_shape=jax.ShapeDtypeStruct((rows, PAIR), jnp.bfloat16),
        grid_spec=pltpu.PrefetchScalarGridSpec(
            num_scalar_prefetch=2,
            grid=(1,),
            in_specs=[
                pl.BlockSpec((128, PAIR), lambda i, *_: (0, 0)),
                pl.BlockSpec((1, 4 * PAIR), lambda i, *_: (0, 0)),
            ],
            out_specs=pl.BlockSpec((rows, PAIR), lambda i, *_: (0, 0)),
            scratch_shapes=[pltpu.SMEM((PPAGES,), jnp.int32)],
        ),
        compiler_params=pltpu.CompilerParams(vmem_limit_bytes=32 * MIB),
        name="merge_pages",
    )(owner, place, received, suffix)


def shifted(x, axis, hop):
    return lax.ppermute(x, axis, [(i, (i + hop) % SIDE) for i in range(SIDE)])


def gray(s):
    return s ^ (s >> 1)


def spread_kernel(q_ref, even_ref, odd_ref):
    lane = lax.broadcasted_iota(jnp.int32, (SUF, 128), 1)
    for h in range(4):
        if h % 2 == 0:
            whole = q_ref[:, h * LAT : h * LAT + LAT + 64].astype(jnp.float32)
        else:
            whole = q_ref[:, h * LAT - 64 : h * LAT + LAT].astype(jnp.float32)
            whole = pltpu.roll(whole, LAT, 1)
        latent = whole[:, :VLAT].astype(jnp.bfloat16)
        rest = whole[:, VLAT:]
        even_ref[h, :, :VLAT] = latent
        odd_ref[h, :, 128:] = latent
        odd_ref[h, :, :128] = jnp.where(lane < 64, rest, 0.0).astype(jnp.bfloat16)
        even_ref[h, :, VLAT:] = jnp.where(lane < 64, 0.0, pltpu.roll(rest, 64, 1)).astype(jnp.bfloat16)


def spread_queries(queries):
    shape = (4, SUF, VLAT + 128)
    return pl.pallas_call(
        spread_kernel,
        out_shape=[jax.ShapeDtypeStruct(shape, jnp.bfloat16)] * 2,
        grid=(1,),
        in_specs=[pl.BlockSpec((SUF, 4 * LAT), lambda i: (0, 0))],
        out_specs=[pl.BlockSpec(shape, lambda i: (0, 0, 0))] * 2,
        compiler_params=pltpu.CompilerParams(vmem_limit_bytes=32 * MIB),
        cost_estimate=pl.CostEstimate(flops=0, transcendentals=0, bytes_accessed=4 * MIB),
        name="spread_queries",
    )(queries)


def prefix_bias(blocks, parity, x, y, length):
    lane = lax.broadcasted_iota(jnp.int32, (1, 256 * len(blocks)), 1)
    part, page = (lane >> 5) & 3, lane & 31
    index = (lane >> 7) & (len(blocks) - 1)
    hop = jnp.full(lane.shape, HOPS[blocks[0]], jnp.int32)
    for n in range(1, len(blocks)):
        hop = jnp.where(index == n, HOPS[blocks[n]], hop)
    head = lane < 128 * len(blocks)
    turn = gray(part)
    far = (x - jnp.where(head, turn, hop)) & 3
    near = (y - jnp.where(head, hop, turn)) & 3
    token = page * PAGE + (far * 4 + near) * 4 + jnp.where(head, 0, 2) + parity
    return jnp.where(token < length, 0.0, masked_score)


def suffix_order(parity, x, y):
    lane = lax.broadcasted_iota(jnp.int32, (1, 128), 1)
    block, part = lane >> 5, (lane >> 3) & 3
    far, near = (x - gray(part)) & 3, (y - gray(block)) & 3
    holder = ((lane >> 2) & 1) * 16 + far * 4 + near
    return holder * 8 + (lane & 3) * 2 + parity


def attend_kernel(blocks, first, last, place, length, even_q, odd_q, *refs):
    n = len(blocks)
    refs = list(refs)
    heads, tails = [refs.pop(0) for _ in range(n)], [refs.pop(0) for _ in range(n)]
    others = [refs.pop(0) for _ in range(4 - n)] if last else []
    weights_in = [refs.pop(0) for _ in range(2)] if last else []
    before = [] if first else [refs.pop(0) for _ in range(2)]
    after = [refs.pop(0) for _ in range(1 if last else 2)]
    keys = refs[0]
    pages = 256 * n

    for b in range(n):
        for t in range(4):
            row = b * 128 + t * 32
            keys[row : row + 32] = heads[b][t * HEAD_ROWS : t * HEAD_ROWS + 32]
        keys[(n + b) * 128 : (n + b + 1) * 128] = tails[b][...]
    x, y = (place[0] // 4) % 4, place[0] % 4
    bias = [prefix_bias(blocks, parity, x, y, length[0]) for parity in range(2)]
    if last:
        w = refs[1]
        for b, head in enumerate([*others, *heads]):
            for t in range(4):
                row = pages + b * 32 + t * 8
                keys[row : row + 8] = head[t * HEAD_ROWS + 32 : (t + 1) * HEAD_ROWS]
        token = lax.broadcasted_iota(jnp.int32, (SUF, 128), 0)
        hidden = [suffix_order(parity, x, y) > token for parity in range(2)]
        for k in range(4):
            for other in range(2):
                part = ((place[1] // 2 - HOPS[k]) & 3) * 2 + ((place[1] & 1) ^ other)
                rows = pl.ds(pl.multiple_of(part * (VLAT // 8), VLAT // 8), VLAT // 8)
                w[:, rows, :] = weights_in[other][k]

    def scored(h):
        pieces = []
        for parity, queries, cut in ((0, even_q, 0), (1, odd_q, VLAT)):
            s = lax.dot_general(
                queries[h],
                keys[:, cut : cut + VLAT + 128],
                (((1,), (1,)), ((), ())),
                preferred_element_type=jnp.float32,
            )
            if last:
                fresh = jnp.where(hidden[parity], masked_score, s[:, pages:])
                s = jnp.concatenate([s[:, :pages] + bias[parity], fresh], axis=1)
            else:
                s = s + bias[parity]
            pieces.append(s)
        return pieces

    def mixed(h, pieces):
        top = jnp.max(jnp.maximum(pieces[0], pieces[1]), axis=1, keepdims=True)
        if not first:
            top_old, total_old = before[1][h, :, :1], before[1][h, :, 1:2]
            top = jnp.maximum(top, top_old)
        weights = [jnp.exp2((piece - top) * exponent_scale) for piece in pieces]
        total = jnp.sum(weights[0] + weights[1], axis=1, keepdims=True)
        parts = [
            jnp.dot(
                weights[parity].astype(jnp.bfloat16),
                keys[:, cut : cut + VLAT],
                preferred_element_type=jnp.float32,
            )
            for parity, cut in ((0, 0), (1, VLAT + 128))
        ]
        mixture = parts[0] + parts[1]
        if not first:
            rescale = jnp.exp2((top_old - top) * exponent_scale)
            total = total + total_old * rescale
            mixture = mixture + before[0][h] * rescale
        if last:
            mixture = (mixture / total).astype(jnp.bfloat16)
            out = jnp.dot(mixture, w[h], preferred_element_type=jnp.float32)
            after[0][:, h * VHEAD : (h + 1) * VHEAD] = out.astype(jnp.bfloat16)
        else:
            after[0][h] = mixture
            lane = lax.broadcasted_iota(jnp.int32, (SUF, 128), 1)
            after[1][h] = jnp.where(lane == 0, top, total)

    pieces = scored(0)
    for h in range(4):
        following = scored(h + 1) if h < 3 else None
        mixed(h, pieces)
        pieces = following


def attended(blocks, place, length, spread, heads, tails, state, w):
    n, first, last = len(blocks), not state, bool(w)
    whole = lambda *shape: pl.BlockSpec(shape, lambda h, *_: (0,) * len(shape))
    state_specs = [whole(4, SUF, VLAT), whole(4, SUF, 128)]
    own_heads, own_tails = [heads[b] for b in blocks], [tails[b] for b in blocks]
    others = [heads[b] for b in range(4) if b not in blocks] if last else []
    rows = 256 * n + (128 if last else 0)
    scratch = [pltpu.VMEM((rows, PAIR), jnp.bfloat16)]
    if last:
        out_shape = jax.ShapeDtypeStruct((SUF, 4 * VHEAD), jnp.bfloat16)
        out_specs = whole(SUF, 4 * VHEAD)
        scratch.append(pltpu.VMEM((4, VLAT, VHEAD), jnp.bfloat16))
    else:
        out_shape = [
            jax.ShapeDtypeStruct((4, SUF, VLAT), jnp.float32),
            jax.ShapeDtypeStruct((4, SUF, 128), jnp.float32),
        ]
        out_specs = state_specs

    def kernel(*refs):
        attend_kernel(blocks, first, last, *refs)

    return pl.pallas_call(
        kernel,
        out_shape=out_shape,
        grid_spec=pltpu.PrefetchScalarGridSpec(
            num_scalar_prefetch=2,
            grid=(1,),
            in_specs=[
                *[whole(4, SUF, VLAT + 128)] * 2,
                *[whole(4 * HEAD_ROWS, PAIR)] * n,
                *[whole(4 * TAIL_ROWS, PAIR)] * n,
                *[whole(4 * HEAD_ROWS, PAIR)] * len(others),
                *([whole(4, 4, VLAT // 8, VHEAD)] * 2 if last else []),
                *([] if first else state_specs),
            ],
            out_specs=out_specs,
            scratch_shapes=scratch,
        ),
        compiler_params=pltpu.CompilerParams(vmem_limit_bytes=40 * MIB),
        cost_estimate=pl.CostEstimate(
            flops=8 * SUF * rows * (2 * VLAT + 128) * 2,
            transcendentals=8 * SUF * rows,
            bytes_accessed=16 * MIB,
        ),
        name="attend_" + "".join(str(b) for b in blocks),
    )(place, length, *spread, *own_heads, *own_tails, *others, *w, *state)


def update_kernel(place, new_owner, new_slot, pool_ref, *refs):
    heads, out_ref, fresh = refs[:4], refs[4], refs[5]
    me = place[0]
    page, target = jnp.int32(0), jnp.int32(-1)
    for m in range(NEWP):
        hit = new_owner[0, m] == me
        page = jnp.where(hit, m, page)
        target = jnp.where(hit, new_slot[0, m], target)
    for b in range(4):
        for s in range(4):
            k = 4 * b + s
            fresh[k * 8 : (k + 1) * 8] = heads[b][s * HEAD_ROWS + 32 : (s + 1) * HEAD_ROWS]
    x, y = (me // 4) % 4, me % 4
    row = lax.broadcasted_iota(jnp.int32, (CHUNKS, 128), 0)
    col = lax.broadcasted_iota(jnp.int32, (CHUNKS, 128), 1)
    holder = page * 8 + (row >> 2)
    part, block = gray((x - (holder >> 2)) & 3), gray((y - holder) & 3)
    source = block * 32 + part * 8 + (holder >> 4) * 4 + (row & 3)
    pick = (col == source).astype(jnp.float32).astype(jnp.bfloat16)
    rows = jnp.dot(pick, fresh[...], preferred_element_type=jnp.float32)
    turned = pltpu.roll(rows[:, VLAT:], LAT, 1)
    rows = jnp.concatenate([rows[:, :VLAT], turned], axis=1)
    mine = lax.broadcasted_iota(jnp.int32, (SLOTS, PAIR), 0) == target
    for c in range(CHUNKS):
        old = pool_ref[:, c * PAIR : (c + 1) * PAIR].astype(jnp.float32)
        out_ref[:, c * PAIR : (c + 1) * PAIR] = jnp.where(mine, rows[c : c + 1], old).astype(jnp.bfloat16)


def updated_pool(place, new_owner, new_slot, pool, heads):
    return pl.pallas_call(
        update_kernel,
        out_shape=jax.ShapeDtypeStruct(pool.shape, pool.dtype),
        grid_spec=pltpu.PrefetchScalarGridSpec(
            num_scalar_prefetch=3,
            grid=(1,),
            in_specs=[
                pl.BlockSpec(pool.shape, lambda i, *_: (0, 0)),
                *[pl.BlockSpec((4 * HEAD_ROWS, PAIR), lambda i, *_: (0, 0))] * 4,
            ],
            out_specs=pl.BlockSpec(pool.shape, lambda i, *_: (0, 0)),
            scratch_shapes=[pltpu.VMEM((128, PAIR), jnp.bfloat16)],
        ),
        compiler_params=pltpu.CompilerParams(vmem_limit_bytes=32 * MIB),
        cost_estimate=pl.CostEstimate(flops=0, transcendentals=0, bytes_accessed=6 * MIB),
        name="update_pool",
    )(place, new_owner, new_slot, pool, *heads)


def local(queries, new_latent, pool, page_owner, page_slot, new_owner, new_slot, prefix_len, w_uv):
    place = jnp.stack([lax.axis_index(POOL), lax.axis_index(SERVE)]).astype(jnp.int32)
    w_row = jnp.stack([w_uv] + [shifted(w_uv, "serve_0", k) for k in HOPS[1:]])
    pieces = selected_pieces(page_owner, page_slot, place, pool[0])
    received = lax.all_to_all(pieces, PLANE, 0, 0, tiled=True).reshape(128, PAIR)
    mine = merged_rows(page_owner, place, received, new_latent)
    mine, queries, w_row = lax.optimization_barrier((mine, queries, w_row))
    w = [w_row, lax.ppermute(w_row, "serve_1", [(0, 1), (1, 0)])]
    spread = spread_queries(queries[0])
    both = mine + lax.ppermute(mine, "pool_0", [(0, 1), (1, 0)])
    head, tail = both[:HEAD_ROWS], both[HEAD_ROWS:]
    head_row = jnp.concatenate([head] + [shifted(head, "pool_1", k) for k in HOPS[1:]])
    tail_row = jnp.concatenate([tail] + [shifted(tail, "pool_2", k) for k in HOPS[1:]])
    head_row, tail_row, *w = lax.optimization_barrier((head_row, tail_row, *w))
    state = attended((0,), place, prefix_len, spread, [head_row], [tail_row], (), ())
    state, late = lax.optimization_barrier((state, tail_row))
    tail_far = shifted(late, "pool_1", HOPS[3])
    head_far = shifted(head_row, "pool_2", HOPS[3])
    tails = [tail_row] + [shifted(tail_row, "pool_1", k) for k in HOPS[1:3]] + [tail_far]
    heads = [head_row] + [shifted(head_row, "pool_2", k) for k in HOPS[1:3]] + [head_far]
    state = attended((1, 2), place, prefix_len, spread, heads, tails, state, ())
    out = attended((3,), place, prefix_len, spread, heads, tails, state, w)
    updated = updated_pool(place, new_owner, new_slot, pool[0], heads)
    return (out[None], updated[None])


def solution(mesh):
    shape = (2, SIDE, SIDE, SIDE, 2)
    split = Mesh(mesh.devices.reshape(shape), (*POOL, *SERVE))
    placed = (
        P(SERVE, None, POOL),
        P(SERVE, POOL),
        P(SERVE, POOL, None),
        P(SERVE, None),
        P(SERVE, None),
        P(SERVE, None),
        P(SERVE, None),
        P(SERVE),
        P(POOL, SERVE, None),
    )
    return jax.shard_map(
        local,
        mesh=split,
        in_specs=placed,
        out_specs=(P(SERVE, None, POOL), P(SERVE, POOL, None)),
        check_vma=False,
    )
```

time: 106 us -> 83 us (0.78)
  the two profiles are of different devices: /device:TPU:64 before, /device:TPU:1 now
where the time goes in v2:
time: 83 us; the launch traced here: 82.7 us
  starting transfers between devices  42.4 us (51%)
  waiting for transfers between devices  18.7 us (23%)
  Pallas kernels  17.3 us (21%)
  local copies, waits for them, and re-layouts  2.63 us (3%)
  between operations  1.49 us (2%)
    ppermute x15, starting transfers between devices, shifted(): return lax.ppermute(x, axis, [(i, (i + hop) % SIDE) for i in range(SIDE)])  22.9 us
    ppermute x15, waiting for transfers between devices, shifted(): return lax.ppermute(x, axis, [(i, (i + hop) % SIDE) for i in range(SIDE)])  15.9 us
    pallas_call x3, Pallas kernels, attended(): pl.pallas_call(kernel, out_shape=out_shape, grid_spec=pltpu.PrefetchScala...  11.4 us
    all_to_all x1, starting transfers between devices, local(): lax.all_to_all(pieces, PLANE, 0, 0, tiled=True).reshape(128, PAIR)  7.6 us
    ppermute x1, starting transfers between devices, local(): w = [w_row, lax.ppermute(w_row, 'serve_1', [(0, 1), (1, 0)])]  6.26 us
    ppermute x1, starting transfers between devices, local(): both = mine + lax.ppermute(mine, 'pool_0', [(0, 1), (1, 0)])  5.57 us
    ppermute x1, waiting for transfers between devices, local(): both = mine + lax.ppermute(mine, 'pool_0', [(0, 1), (1, 0)])  2.83 us
    unnamed x20, local copies, waits for them, and re-layouts  2.62 us
  transfers between devices with their start and end apart: 18, of which 8 were waited for; matrix products, arithmetic and copies ran while one was open for 0% of the time, Pallas kernels for 10%

profile of v2, /device:TPU:1, one launch (start us, length us, event | category | flops | bytes accessed | tf_op | source)
XLA Modules:
  0.0 82.7 jit_solution(11456887035786323256)
XLA Ops:
  0.7 1.3 %copy-done = bf16[1,12,36864]{2,1,0:T(8,128)(2,1)S(1)} copy-done((bf16[1,12,36864]{2,1,0:T(8,128)(2,1)S(1)}, bf16[1,12,36864]{2,1,0:T(8,128)(2,1)}, u32[]{:S(2)}) %copy-start) | copy-done | bytes 884760
  3.3 2.4 %select_pages.1 = bf16[16,8,1152]{2,1,0:T(8,128)(2,1)} custom-call(s32[1,32]{1,0:T(1,128)S(1)} %copy-done.4, s32[1,32]{1,0:T(1,128)S(1)} %copy-done.6, s32[2]{0:T(128)S(1)} %pad_add_fusion.place.refs_0_, bf16[12,36864]{1,0:T(8,128)(2,1)S(1)} %bitcast.11), custom_call_target="tpu_custom_call" | custom-call | tf_op jit(solution)/shard_map/select_pages/pallas_call | solution.py:64
  5.8 7.6 %all-to-all-start = ((bf16[16,8,1152]{2,1,0:T(8,128)(2,1)}), bf16[16,8,1152]{2,1,0:T(8,128)(2,1)S(1)}, u32[]{:S(2)}, u32[]{:S(2)}) async-start(bf16[16,8,1152]{2,1,0:T(8,128)(2,1)} %select_pages.1), calls=%async_computation | async-start | bytes 589824 | tf_op jit(solution)/shard_map/all_to_all | solution.py:379
  13.4 3.1 %collective-permute-start.2 = (bf16[4,64,128]{2,1,0:T(8,128)(2,1)S(1)}, bf16[4,64,128]{2,1,0:T(8,128)(2,1)S(1)}, u32[]{:S(2)}, u32[]{:S(2)}) collective-permute-start(bf16[4,64,128]{2,1,0:T(8,128)(2,1)S(1)} %copy-done.9), channel_id=1, source_target_pairs={{0,4},{2,6},{4,0},{6,2},{1,5},{3,7},{5,1},{7,3},{8,12},{10,14},{12... | collective-permute-start | bytes 196616 | tf_op jit(solution)/shard_map/ppermute | solution.py:133
  16.5 1.4 %collective-permute-start.1 = (bf16[4,64,128]{2,1,0:T(8,128)(2,1)S(1)}, bf16[4,64,128]{2,1,0:T(8,128)(2,1)S(1)}, u32[]{:S(2)}, u32[]{:S(2)}) collective-permute-start(bf16[4,64,128]{2,1,0:T(8,128)(2,1)S(1)} %copy-done.9), channel_id=1, source_target_pairs={{0,6},{2,0},{4,2},{6,4},{1,7},{3,1},{5,3},{7,5},{8,14},{10,8},{12,... | collective-permute-start | bytes 196616 | tf_op jit(solution)/shard_map/ppermute | solution.py:133
  18.1 2.3 %collective-permute-done.1 = bf16[4,64,128]{2,1,0:T(8,128)(2,1)S(1)} collective-permute-done((bf16[4,64,128]{2,1,0:T(8,128)(2,1)S(1)}, bf16[4,64,128]{2,1,0:T(8,128)(2,1)S(1)}, u32[]{:S(2)}, u32[]{:S(2)}) %collective-permute-start.1) | collective-permute-done | bytes 65568 | tf_op jit(solution)/shard_map/ppermute | solution.py:133
  20.4 2.5 %collective-permute-done = bf16[4,64,128]{2,1,0:T(8,128)(2,1)S(1)} collective-permute-done((bf16[4,64,128]{2,1,0:T(8,128)(2,1)S(1)}, bf16[4,64,128]{2,1,0:T(8,128)(2,1)S(1)}, u32[]{:S(2)}, u32[]{:S(2)}) %collective-permute-start) | collective-permute-done | bytes 65568 | tf_op jit(solution)/shard_map/ppermute | solution.py:133
  23.0 1.1 %merge_pages.1 = bf16[72,1152]{1,0:T(8,128)(2,1)S(1)} custom-call(s32[1,32]{1,0:T(1,128)S(1)} %copy-done.5, s32[2]{0:T(128)S(1)} %pad_add_fusion.place.refs_0_, bf16[128,1152]{1,0:T(8,128)(2,1)S(1)} %bitcast.14, bf16[1,4608]{1,0:T(2,128)(2,1)S(1)} %copy-done.3), custom_call_target="tpu_custom_call" | custom-call | tf_op jit(solution)/shard_map/merge_pages/pallas_call | solution.py:114
  24.1 5.6 %collective-permute-start.3 = (bf16[72,1152]{1,0:T(8,128)(2,1)S(1)}, bf16[72,1152]{1,0:T(8,128)(2,1)S(1)}, u32[]{:S(2)}, u32[]{:S(2)}) collective-permute-start(bf16[72,1152]{1,0:T(8,128)(2,1)S(1)} %merge_pages.1), channel_id=1, source_target_pairs={{0,128},{128,0},{1,129},{129,1},{2,130},{130,2},{3,131},{131,3},{4... | collective-permute-start | bytes 497672 | tf_op jit(solution)/shard_map/ppermute | solution.py:384
  29.6 2.8 %collective-permute-done.3 = bf16[72,1152]{1,0:T(8,128)(2,1)S(1)} collective-permute-done((bf16[72,1152]{1,0:T(8,128)(2,1)S(1)}, bf16[72,1152]{1,0:T(8,128)(2,1)S(1)}, u32[]{:S(2)}, u32[]{:S(2)}) %collective-permute-start.3) | collective-permute-done | bytes 165920 | tf_op jit(solution)/shard_map/ppermute | solution.py:384
  32.5 2.9 %collective-permute-start.9 = (bf16[32,1152]{1,0:T(8,128)(2,1)S(1)}, bf16[32,1152]{1,0:T(8,128)(2,1)S(1)}, u32[]{:S(2)}, u32[]{:S(2)}) collective-permute-start(bf16[32,1152]{1,0:T(8,128)(2,1)S(1)} %slice.9), channel_id=1, source_target_pairs={{0,16},{8,24},{16,0},{24,8},{1,17},{9,25},{17,1},{25,9},{2,18},{10... | collective-permute-start | bytes 221192 | tf_op jit(solution)/shard_map/ppermute | solution.py:133
  35.4 1.1 %collective-permute-start.8 = (bf16[32,1152]{1,0:T(8,128)(2,1)S(1)}, bf16[32,1152]{1,0:T(8,128)(2,1)S(1)}, u32[]{:S(2)}, u32[]{:S(2)}) collective-permute-start(bf16[32,1152]{1,0:T(8,128)(2,1)S(1)} %slice.9), channel_id=1, source_target_pairs={{0,24},{8,0},{16,8},{24,16},{1,25},{9,1},{17,9},{25,17},{2,26},{10... | collective-permute-start | bytes 221192 | tf_op jit(solution)/shard_map/ppermute | solution.py:133
  36.8 6.3 %collective-permute-start.10 = (bf16[4,4,64,128]{3,2,1,0:T(8,128)(2,1)S(1)}, bf16[4,4,64,128]{3,2,1,0:T(8,128)(2,1)S(1)}, u32[]{:S(2)}, u32[]{:S(2)}) collective-permute-start(bf16[4,4,64,128]{3,2,1,0:T(8,128)(2,1)S(1)} %pad_maximum_fusion.2.refs_9_), channel_id=1, source_target_pairs={{0,1},{1,0},{2,3},{3,2},{4,5},{5,4},{6,7},{7,6},{8,9},{9,8},{10,11... | collective-permute-start | bytes 786440 | tf_op jit(solution)/shard_map/ppermute | solution.py:382
  43.1 2.8 %collective-permute-start.6 = (bf16[40,1152]{1,0:T(8,128)(2,1)S(1)}, bf16[40,1152]{1,0:T(8,128)(2,1)S(1)}, u32[]{:S(2)}, u32[]{:S(2)}) collective-permute-start(bf16[40,1152]{1,0:T(8,128)(2,1)S(1)} %slice.8), channel_id=1, source_target_pairs={{0,64},{32,96},{64,0},{96,32},{1,65},{33,97},{65,1},{97,33},{2,66}... | collective-permute-start | bytes 276488 | tf_op jit(solution)/shard_map/ppermute | solution.py:133
  47.5 1.6 %collective-permute-done.6 = bf16[40,1152]{1,0:T(8,128)(2,1)S(1)} collective-permute-done((bf16[40,1152]{1,0:T(8,128)(2,1)S(1)}, bf16[40,1152]{1,0:T(8,128)(2,1)S(1)}, u32[]{:S(2)}, u32[]{:S(2)}) %collective-permute-start.6) | collective-permute-done | bytes 92192 | tf_op jit(solution)/shard_map/ppermute | solution.py:133
  49.0 2.0 %collective-permute-done.5 = bf16[40,1152]{1,0:T(8,128)(2,1)S(1)} collective-permute-done((bf16[40,1152]{1,0:T(8,128)(2,1)S(1)}, bf16[40,1152]{1,0:T(8,128)(2,1)S(1)}, u32[]{:S(2)}, u32[]{:S(2)}) %collective-permute-start.5) | collective-permute-done | bytes 92192 | tf_op jit(solution)/shard_map/ppermute | solution.py:133
  51.9 2.3 %collective-permute-start.13 = (bf16[160,1152]{1,0:T(8,128)(2,1)S(1)}, bf16[160,1152]{1,0:T(8,128)(2,1)S(1)}, u32[]{:S(2)}, u32[]{:S(2)}) collective-permute-start(bf16[160,1152]{1,0:T(8,128)(2,1)S(1)} %pad_maximum_fusion.refs_4_.refs_6_.refs_0_), channel_id=1, source_target_pairs={{0,8},{8,16},{16,24},{24,0},{1,9},{9,17},{17,25},{25,1},{2,10},{10... | collective-permute-start | bytes 1105928 | tf_op jit(solution)/shard_map/ppermute | solution.py:133
  55.5 1.8 %collective-permute-start.16 = (bf16[128,1152]{1,0:T(8,128)(2,1)S(1)}, bf16[128,1152]{1,0:T(8,128)(2,1)S(1)}, u32[]{:S(2)}, u32[]{:S(2)}) collective-permute-start(bf16[128,1152]{1,0:T(8,128)(2,1)S(1)} %pad_maximum_fusion.1.refs_5_), channel_id=1, source_target_pairs={{0,96},{32,0},{64,32},{96,64},{1,97},{33,1},{65,33},{97,65},{2,98}... | collective-permute-start | bytes 884744 | tf_op jit(solution)/shard_map/ppermute | solution.py:133
  58.4 2.2 %attend_0.1 = (f32[4,256,512]{2,1,0:T(8,128)S(1)}, f32[4,256,128]{2,1,0:T(8,128)S(1)}) custom-call(s32[2]{0:T(128)S(1)} %pad_add_fusion.place.refs_0_, s32[1]{0:T(128)S(6)} %copy.11.refs_1_, bf16[4,256,640]{2,1,0:T(8,128)(2,1)S(1)} %get-tuple-element.19.refs_2_, bf16[4,256,640]{2,1,0:T(8,128)(2,1)S(1)} %get-tuple-element.20.refs_3_, ...), custom_call_target="tpu_custom_call" | custom-call | flops 1207959552 | bytes 16777216 | tf_op jit(solution)/shard_map/attend_0/pallas_call | solution.py:300
  61.5 3.8 %collective-permute-start.12 = (bf16[128,1152]{1,0:T(8,128)(2,1)S(1)}, bf16[128,1152]{1,0:T(8,128)(2,1)S(1)}, u32[]{:S(2)}, u32[]{:S(2)}) collective-permute-start(bf16[128,1152]{1,0:T(8,128)(2,1)S(1)} %pad_maximum_fusion.1.refs_5_), channel_id=1, source_target_pairs={{0,64},{32,96},{64,0},{96,32},{1,65},{33,97},{65,1},{97,33},{2,66}... | collective-permute-start | bytes 884744 | tf_op jit(solution)/shard_map/ppermute | solution.py:133
  65.4 6.1 %collective-permute-done.13.refs_4_.refs_7_.refs_1_ = bf16[160,1152]{1,0:T(8,128)(2,1)S(1)} collective-permute-done((bf16[160,1152]{1,0:T(8,128)(2,1)S(1)}, bf16[160,1152]{1,0:T(8,128)(2,1)S(1)}, u32[]{:S(2)}, u32[]{:S(2)}) %collective-permute-start.13) | collective-permute-done | bytes 368672 | tf_op jit(solution)/shard_map/ppermute | solution.py:133
  71.5 2.0 %update_pool.1 = bf16[12,36864]{1,0:T(8,128)(2,1)} custom-call(s32[2]{0:T(128)S(1)} %pad_add_fusion.place.refs_0_, s32[1,4]{1,0:T(1,128)S(1)} %copy-done.7, s32[1,4]{1,0:T(1,128)S(1)} %copy-done.8, bf16[12,36864]{1,0:T(8,128)(2,1)S(1)} %bitcast.12, bf16[160,1152]{1,0:T(8,128)(2,1)S(1)} %pad_maximum_fusion.refs_4_.refs_6_.refs_0_, ...), custom_call_target="tpu_custom_call" | custom-call | bytes 6291456 | tf_op jit(solution)/shard_map/update_pool/pallas_call | solution.py:356
  73.5 3.8 %attend_12.1 = (f32[4,256,512]{2,1,0:T(8,128)S(1)}, f32[4,256,128]{2,1,0:T(8,128)S(1)}) custom-call(s32[2]{0:T(128)S(1)} %pad_add_fusion.place.refs_0_, s32[1]{0:T(128)S(6)} %copy.11.refs_1_, bf16[4,256,640]{2,1,0:T(8,128)(2,1)S(1)} %get-tuple-element.19.refs_2_, bf16[4,256,640]{2,1,0:T(8,128)(2,1)S(1)} %get-tuple-element.20.refs_3_, ...), custom_call_target="tpu_custom_call" | custom-call | flops 2415919104 | bytes 16777216 | tf_op jit(solution)/shard_map/attend_12/pallas_call | solution.py:300
  77.4 5.4 %attend_3.1 = bf16[256,512]{1,0:T(8,128)(2,1)} custom-call(s32[2]{0:T(128)S(1)} %pad_add_fusion.place.refs_0_, s32[1]{0:T(128)S(6)} %copy.11.refs_1_, bf16[4,256,640]{2,1,0:T(8,128)(2,1)S(1)} %get-tuple-element.19.refs_2_, bf16[4,256,640]{2,1,0:T(8,128)(2,1)S(1)} %get-tuple-element.20.refs_3_, bf16[160,1152]{1,0:T(8,128)(2,1)S(1)} %collective-permute-done.11.refs_4_.refs_3_, ...), custom_call_target="tpu_custom_call" | custom-call | flops 1811939328 | bytes 16777216 | tf_op jit(solution)/shard_map/attend_3/pallas_call | solution.py:300
  (46 shorter events, 7.1 us)
Async XLA Ops:
  0.6 22.3 %copy-start.3 = (bf16[1,4608]{1,0:T(2,128)(2,1)S(1)}, bf16[1,4608]{1,0:T(2,128)(2,1)}, u32[]{:S(2)}) copy-start(bf16[1,4608]{1,0:T(2,128)(2,1)} %suffix_ref.1) | copy-start | bytes 27652
  0.6 22.3 %copy-start.5 = (s32[1,32]{1,0:T(1,128)S(1)}, s32[1,32]{1,0:T(1,128)}, u32[]{:S(2)}) copy-start(s32[1,32]{1,0:T(1,128)} %owner.3) | copy-start | bytes 388
  5.8 17.2 %all-to-all-start = ((bf16[16,8,1152]{2,1,0:T(8,128)(2,1)}), bf16[16,8,1152]{2,1,0:T(8,128)(2,1)S(1)}, u32[]{:S(2)}, u32[]{:S(2)}) async-start(bf16[16,8,1152]{2,1,0:T(8,128)(2,1)} %select_pages.1), calls=%async_computation | async-start | bytes 589824 | tf_op jit(solution)/shard_map/all_to_all | solution.py:379
  13.4 4.7 %collective-permute-start.2 = (bf16[4,64,128]{2,1,0:T(8,128)(2,1)S(1)}, bf16[4,64,128]{2,1,0:T(8,128)(2,1)S(1)}, u32[]{:S(2)}, u32[]{:S(2)}) collective-permute-start(bf16[4,64,128]{2,1,0:T(8,128)(2,1)S(1)} %copy-done.9), channel_id=1, source_target_pairs={{0,4},{2,6},{4,0},{6,2},{1,5},{3,7},{5,1},{7,3},{8,12},{10,14},{12... | collective-permute-start | bytes 196616 | tf_op jit(solution)/shard_map/ppermute | solution.py:133
  16.5 4.0 %collective-permute-start.1 = (bf16[4,64,128]{2,1,0:T(8,128)(2,1)S(1)}, bf16[4,64,128]{2,1,0:T(8,128)(2,1)S(1)}, u32[]{:S(2)}, u32[]{:S(2)}) collective-permute-start(bf16[4,64,128]{2,1,0:T(8,128)(2,1)S(1)} %copy-done.9), channel_id=1, source_target_pairs={{0,6},{2,0},{4,2},{6,4},{1,7},{3,1},{5,3},{7,5},{8,14},{10,8},{12,... | collective-permute-start | bytes 196616 | tf_op jit(solution)/shard_map/ppermute | solution.py:133
  17.9 5.0 %collective-permute-start = (bf16[4,64,128]{2,1,0:T(8,128)(2,1)S(1)}, bf16[4,64,128]{2,1,0:T(8,128)(2,1)S(1)}, u32[]{:S(2)}, u32[]{:S(2)}) collective-permute-start(bf16[4,64,128]{2,1,0:T(8,128)(2,1)S(1)} %copy-done.9), channel_id=1, source_target_pairs={{0,2},{2,4},{4,6},{6,0},{1,3},{3,5},{5,7},{7,1},{8,10},{10,12},{12... | collective-permute-start | bytes 196616 | tf_op jit(solution)/shard_map/ppermute | solution.py:133
  23.0 34.9 %copy-start.2 = (bf16[1,256,2304]{2,1,0:T(8,128)(2,1)S(1)}, bf16[1,256,2304]{2,1,0:T(8,128)(2,1)}, u32[]{:S(2)}) copy-start(bf16[1,256,2304]{2,1,0:T(8,128)(2,1)} %param.9) | copy-start | bytes 3538948
  24.1 8.4 %collective-permute-start.3 = (bf16[72,1152]{1,0:T(8,128)(2,1)S(1)}, bf16[72,1152]{1,0:T(8,128)(2,1)S(1)}, u32[]{:S(2)}, u32[]{:S(2)}) collective-permute-start(bf16[72,1152]{1,0:T(8,128)(2,1)S(1)} %merge_pages.1), channel_id=1, source_target_pairs={{0,128},{128,0},{1,129},{129,1},{2,130},{130,2},{3,131},{131,3},{4... | collective-permute-start | bytes 497672 | tf_op jit(solution)/shard_map/ppermute | solution.py:384
  32.5 13.4 %collective-permute-start.9 = (bf16[32,1152]{1,0:T(8,128)(2,1)S(1)}, bf16[32,1152]{1,0:T(8,128)(2,1)S(1)}, u32[]{:S(2)}, u32[]{:S(2)}) collective-permute-start(bf16[32,1152]{1,0:T(8,128)(2,1)S(1)} %slice.9), channel_id=1, source_target_pairs={{0,16},{8,24},{16,0},{24,8},{1,17},{9,25},{17,1},{25,9},{2,18},{10... | collective-permute-start | bytes 221192 | tf_op jit(solution)/shard_map/ppermute | solution.py:133
  35.4 11.5 %collective-permute-start.8 = (bf16[32,1152]{1,0:T(8,128)(2,1)S(1)}, bf16[32,1152]{1,0:T(8,128)(2,1)S(1)}, u32[]{:S(2)}, u32[]{:S(2)}) collective-permute-start(bf16[32,1152]{1,0:T(8,128)(2,1)S(1)} %slice.9), channel_id=1, source_target_pairs={{0,24},{8,0},{16,8},{24,16},{1,25},{9,1},{17,9},{25,17},{2,26},{10... | collective-permute-start | bytes 221192 | tf_op jit(solution)/shard_map/ppermute | solution.py:133
  36.5 11.0 %collective-permute-start.7 = (bf16[32,1152]{1,0:T(8,128)(2,1)S(1)}, bf16[32,1152]{1,0:T(8,128)(2,1)S(1)}, u32[]{:S(2)}, u32[]{:S(2)}) collective-permute-start(bf16[32,1152]{1,0:T(8,128)(2,1)S(1)} %slice.9), channel_id=1, source_target_pairs={{0,8},{8,16},{16,24},{24,0},{1,9},{9,17},{17,25},{25,1},{2,10},{10... | collective-permute-start | bytes 221192 | tf_op jit(solution)/shard_map/ppermute | solution.py:133
  36.8 14.6 %collective-permute-start.10 = (bf16[4,4,64,128]{3,2,1,0:T(8,128)(2,1)S(1)}, bf16[4,4,64,128]{3,2,1,0:T(8,128)(2,1)S(1)}, u32[]{:S(2)}, u32[]{:S(2)}) collective-permute-start(bf16[4,4,64,128]{3,2,1,0:T(8,128)(2,1)S(1)} %pad_maximum_fusion.2.refs_9_), channel_id=1, source_target_pairs={{0,1},{1,0},{2,3},{3,2},{4,5},{5,4},{6,7},{7,6},{8,9},{9,8},{10,11... | collective-permute-start | bytes 786440 | tf_op jit(solution)/shard_map/ppermute | solution.py:382
  43.1 5.9 %collective-permute-start.6 = (bf16[40,1152]{1,0:T(8,128)(2,1)S(1)}, bf16[40,1152]{1,0:T(8,128)(2,1)S(1)}, u32[]{:S(2)}, u32[]{:S(2)}) collective-permute-start(bf16[40,1152]{1,0:T(8,128)(2,1)S(1)} %slice.8), channel_id=1, source_target_pairs={{0,64},{32,96},{64,0},{96,32},{1,65},{33,97},{65,1},{97,33},{2,66}... | collective-permute-start | bytes 276488 | tf_op jit(solution)/shard_map/ppermute | solution.py:133
  45.9 5.1 %collective-permute-start.5 = (bf16[40,1152]{1,0:T(8,128)(2,1)S(1)}, bf16[40,1152]{1,0:T(8,128)(2,1)S(1)}, u32[]{:S(2)}, u32[]{:S(2)}) collective-permute-start(bf16[40,1152]{1,0:T(8,128)(2,1)S(1)} %slice.8), channel_id=1, source_target_pairs={{0,96},{32,0},{64,32},{96,64},{1,97},{33,1},{65,33},{97,65},{2,98}... | collective-permute-start | bytes 276488 | tf_op jit(solution)/shard_map/ppermute | solution.py:133
  46.8 4.6 %collective-permute-start.4 = (bf16[40,1152]{1,0:T(8,128)(2,1)S(1)}, bf16[40,1152]{1,0:T(8,128)(2,1)S(1)}, u32[]{:S(2)}, u32[]{:S(2)}) collective-permute-start(bf16[40,1152]{1,0:T(8,128)(2,1)S(1)} %slice.8), channel_id=1, source_target_pairs={{0,32},{32,64},{64,96},{96,0},{1,33},{33,65},{65,97},{97,1},{2,34}... | collective-permute-start | bytes 276488 | tf_op jit(solution)/shard_map/ppermute | solution.py:133
  51.5 10.0 %collective-permute-start.11 = (bf16[160,1152]{1,0:T(8,128)(2,1)S(1)}, bf16[160,1152]{1,0:T(8,128)(2,1)S(1)}, u32[]{:S(2)}, u32[]{:S(2)}) collective-permute-start(bf16[160,1152]{1,0:T(8,128)(2,1)S(1)} %pad_maximum_fusion.refs_4_.refs_6_.refs_0_), channel_id=1, source_target_pairs={{0,16},{8,24},{16,0},{24,8},{1,17},{9,25},{17,1},{25,9},{2,18},{10... | collective-permute-start | bytes 1105928 | tf_op jit(solution)/shard_map/ppermute | solution.py:133
  51.9 19.6 %collective-permute-start.13 = (bf16[160,1152]{1,0:T(8,128)(2,1)S(1)}, bf16[160,1152]{1,0:T(8,128)(2,1)S(1)}, u32[]{:S(2)}, u32[]{:S(2)}) collective-permute-start(bf16[160,1152]{1,0:T(8,128)(2,1)S(1)} %pad_maximum_fusion.refs_4_.refs_6_.refs_0_), channel_id=1, source_target_pairs={{0,8},{8,16},{16,24},{24,0},{1,9},{9,17},{17,25},{25,1},{2,10},{10... | collective-permute-start | bytes 1105928 | tf_op jit(solution)/shard_map/ppermute | solution.py:133
  54.3 17.2 %collective-permute-start.14 = (bf16[160,1152]{1,0:T(8,128)(2,1)S(1)}, bf16[160,1152]{1,0:T(8,128)(2,1)S(1)}, u32[]{:S(2)}, u32[]{:S(2)}) collective-permute-start(bf16[160,1152]{1,0:T(8,128)(2,1)S(1)} %pad_maximum_fusion.refs_4_.refs_6_.refs_0_), channel_id=1, source_target_pairs={{0,24},{8,0},{16,8},{24,16},{1,25},{9,1},{17,9},{25,17},{2,26},{10... | collective-permute-start | bytes 1105928 | tf_op jit(solution)/shard_map/ppermute | solution.py:133
  54.6 18.9 %collective-permute-start.15 = (bf16[128,1152]{1,0:T(8,128)(2,1)S(1)}, bf16[128,1152]{1,0:T(8,128)(2,1)S(1)}, u32[]{:S(2)}, u32[]{:S(2)}) collective-permute-start(bf16[128,1152]{1,0:T(8,128)(2,1)S(1)} %pad_maximum_fusion.1.refs_5_), channel_id=1, source_target_pairs={{0,32},{32,64},{64,96},{96,0},{1,33},{33,65},{65,97},{97,1},{2,34}... | collective-permute-start | bytes 884744 | tf_op jit(solution)/shard_map/ppermute | solution.py:133
  55.5 18.0 %collective-permute-start.16 = (bf16[128,1152]{1,0:T(8,128)(2,1)S(1)}, bf16[128,1152]{1,0:T(8,128)(2,1)S(1)}, u32[]{:S(2)}, u32[]{:S(2)}) collective-permute-start(bf16[128,1152]{1,0:T(8,128)(2,1)S(1)} %pad_maximum_fusion.1.refs_5_), channel_id=1, source_target_pairs={{0,96},{32,0},{64,32},{96,64},{1,97},{33,1},{65,33},{97,65},{2,98}... | collective-permute-start | bytes 884744 | tf_op jit(solution)/shard_map/ppermute | solution.py:133
  58.4 13.1 %copy-start.1 = (bf16[1,12,36864]{2,1,0:T(8,128)(2,1)S(1)}, bf16[1,12,36864]{2,1,0:T(8,128)(2,1)}, u32[]{:S(2)}) copy-start(bf16[1,12,36864]{2,1,0:T(8,128)(2,1)} %param.11) | copy-start | bytes 2654212
  58.4 13.1 %copy-start.7 = (s32[1,4]{1,0:T(1,128)S(1)}, s32[1,4]{1,0:T(1,128)}, u32[]{:S(2)}) copy-start(s32[1,4]{1,0:T(1,128)} %new_owner.1) | copy-start | bytes 52
  58.4 13.1 %copy-start.8 = (s32[1,4]{1,0:T(1,128)S(1)}, s32[1,4]{1,0:T(1,128)}, u32[]{:S(2)}) copy-start(s32[1,4]{1,0:T(1,128)} %new_slot.1) | copy-start | bytes 52
  61.5 15.8 %collective-permute-start.12 = (bf16[128,1152]{1,0:T(8,128)(2,1)S(1)}, bf16[128,1152]{1,0:T(8,128)(2,1)S(1)}, u32[]{:S(2)}, u32[]{:S(2)}) collective-permute-start(bf16[128,1152]{1,0:T(8,128)(2,1)S(1)} %pad_maximum_fusion.1.refs_5_), channel_id=1, source_target_pairs={{0,64},{32,96},{64,0},{96,32},{1,65},{33,97},{65,1},{97,33},{2,66}... | collective-permute-start | bytes 884744 | tf_op jit(solution)/shard_map/ppermute | solution.py:133
  (4 other events, 12.6 us)

commit v3 on v2

--- a/solution.py
+++ b/solution.py
@@ -182,85 +182,132 @@
     return jnp.where(token < length, 0.0, masked_score)
 
 
-def suffix_order(parity, x, y):
-    lane = lax.broadcasted_iota(jnp.int32, (1, 128), 1)
-    block, part = lane >> 5, (lane >> 3) & 3
+def suffix_order(x, y):
+    lane = lax.broadcasted_iota(jnp.int32, (1, SUF), 1)
+    block, part = (lane >> 5) & 3, (lane >> 3) & 3
     far, near = (x - gray(part)) & 3, (y - gray(block)) & 3
     holder = ((lane >> 2) & 1) * 16 + far * 4 + near
-    return holder * 8 + (lane & 3) * 2 + parity
-
-
-def attend_kernel(blocks, first, last, place, length, even_q, odd_q, *refs):
+    return holder * 8 + (lane & 3) * 2 + (lane >> 7)
+
+
+def new_page(place, new_owner, new_slot):
+    page, target = jnp.int32(0), jnp.int32(-1)
+    for m in range(NEWP):
+        hit = new_owner[0, m] == place[0]
+        page = jnp.where(hit, m, page)
+        target = jnp.where(hit, new_slot[0, m], target)
+    return page, target
+
+
+def write_page(place, page, target, fresh, slots):
+    x, y = (place[0] // 4) % 4, place[0] % 4
+    row = lax.broadcasted_iota(jnp.int32, (CHUNKS, 128), 0)
+    col = lax.broadcasted_iota(jnp.int32, (CHUNKS, 128), 1)
+    holder = page * 8 + (row >> 2)
+    part, block = gray((x - (holder >> 2)) & 3), gray((y - holder) & 3)
+    source = block * 32 + part * 8 + (holder >> 4) * 4 + (row & 3)
+    pick = (col == source).astype(jnp.float32).astype(jnp.bfloat16)
+    rows = jnp.dot(pick, fresh, preferred_element_type=jnp.float32)
+    rows = jnp.concatenate([rows[:, :VLAT], pltpu.roll(rows[:, VLAT:], LAT, 1)], axis=1)
+    for low, high in ((0, 8), (8, SLOTS)):
+
+        @pl.when((target >= low) & (target < high))
+        def _():
+            mine = lax.broadcasted_iota(jnp.int32, (high - low, PAIR), 0) + low == target
+            for c in range(CHUNKS):
+                columns = slice(c * PAIR, (c + 1) * PAIR)
+                old = slots[low:high, columns].astype(jnp.float32)
+                slots[low:high, columns] = jnp.where(mine, rows[c : c + 1], old).astype(jnp.bfloat16)
+
+
+def segment(parts, t, rows):
+    part, at = divmod(t * len(parts), 4)
+    start = at // len(parts) * rows
+    return parts[part][start : start + rows]
+
+
+def attend_kernel(blocks, first, last, *refs):
     n = len(blocks)
     refs = list(refs)
-    heads, tails = [refs.pop(0) for _ in range(n)], [refs.pop(0) for _ in range(n)]
-    others = [refs.pop(0) for _ in range(4 - n)] if last else []
-    weights_in = [refs.pop(0) for _ in range(2)] if last else []
-    before = [] if first else [refs.pop(0) for _ in range(2)]
-    after = [refs.pop(0) for _ in range(1 if last else 2)]
-    keys = refs[0]
-    pages = 256 * n
-
+    take = lambda count: [refs.pop(0) for _ in range(count)]
+    place, length = take(2)
+    new_owner, new_slot = take(2) if last else (None, None)
+    even_q, odd_q = take(2)
+    if last:
+        heads, tails, others = [take(2)], [take(2)], [[ref] for ref in take(3)]
+        weights_in, pool = take(2), take(1)[0]
+    else:
+        heads, tails = [[ref] for ref in take(n)], [[ref] for ref in take(n)]
+    before = [] if first else take(2)
+    after = take(2)
+    keys = take(1)[0]
+
+    if last:
+        fresh, suffix, w, slots, moved = refs
+        fill = pltpu.make_async_copy(pool, slots, moved.at[0])
+        flush = pltpu.make_async_copy(slots, after[1], moved.at[1])
+        fill.start()
     for b in range(n):
         for t in range(4):
             row = b * 128 + t * 32
-            keys[row : row + 32] = heads[b][t * HEAD_ROWS : t * HEAD_ROWS + 32]
-        keys[(n + b) * 128 : (n + b + 1) * 128] = tails[b][...]
+            keys[row : row + 32] = segment(heads[b], t, HEAD_ROWS)[:32]
+            row = (n + b) * 128 + t * 32
+            keys[row : row + 32] = segment(tails[b], t, TAIL_ROWS)
     x, y = (place[0] // 4) % 4, place[0] % 4
     bias = [prefix_bias(blocks, parity, x, y, length[0]) for parity in range(2)]
     if last:
-        w = refs[1]
         for b, head in enumerate([*others, *heads]):
             for t in range(4):
-                row = pages + b * 32 + t * 8
-                keys[row : row + 8] = head[t * HEAD_ROWS + 32 : (t + 1) * HEAD_ROWS]
-        token = lax.broadcasted_iota(jnp.int32, (SUF, 128), 0)
-        hidden = [suffix_order(parity, x, y) > token for parity in range(2)]
+                row = b * 32 + t * 8
+                fresh[row : row + 8] = segment(head, t, HEAD_ROWS)[32:]
+        suffix[:128] = fresh[:, : VLAT + 128]
+        suffix[128:, :VLAT] = fresh[:, VLAT + 128 :]
+        ropes = fresh[:, VLAT : VLAT + 128].astype(jnp.float32)
+        suffix[128:, VLAT:] = pltpu.roll(ropes, 64, 1).astype(jnp.bfloat16)
+        token = lax.broadcasted_iota(jnp.int32, (SUF, SUF), 0)
+        hidden = suffix_order(x, y) > token
         for k in range(4):
             for other in range(2):
                 part = ((place[1] // 2 - HOPS[k]) & 3) * 2 + ((place[1] & 1) ^ other)
                 rows = pl.ds(pl.multiple_of(part * (VLAT // 8), VLAT // 8), VLAT // 8)
                 w[:, rows, :] = weights_in[other][k]
 
+    even = slice(0, VLAT), slice(0, VLAT + 128)
+    odd = slice(VLAT + 128, PAIR), slice(VLAT, PAIR)
+    groups = [(even_q, keys, even), (odd_q, keys, odd)]
+    if last:
+        groups.append((even_q, suffix, even))
+
     def scored(h):
         pieces = []
-        for parity, queries, cut in ((0, even_q, 0), (1, odd_q, VLAT)):
+        for g, (queries, rows, (_, columns)) in enumerate(groups):
             s = lax.dot_general(
-                queries[h],
-                keys[:, cut : cut + VLAT + 128],
-                (((1,), (1,)), ((), ())),
-                preferred_element_type=jnp.float32,
+                queries[h], rows[:, columns], (((1,), (1,)), ((), ())), preferred_element_type=jnp.float32
             )
-            if last:
-                fresh = jnp.where(hidden[parity], masked_score, s[:, pages:])
-                s = jnp.concatenate([s[:, :pages] + bias[parity], fresh], axis=1)
-            else:
-                s = s + bias[parity]
-            pieces.append(s)
+            pieces.append(jnp.where(hidden, masked_score, s) if g == 2 else s + bias[g])
         return pieces
 
     def mixed(h, pieces):
-        top = jnp.max(jnp.maximum(pieces[0], pieces[1]), axis=1, keepdims=True)
+        top = pieces[0]
+        for piece in pieces[1:]:
+            top = jnp.maximum(top, piece)
+        top = jnp.max(top, axis=1, keepdims=True)
         if not first:
             top_old, total_old = before[1][h, :, :1], before[1][h, :, 1:2]
             top = jnp.maximum(top, top_old)
         weights = [jnp.exp2((piece - top) * exponent_scale) for piece in pieces]
-        total = jnp.sum(weights[0] + weights[1], axis=1, keepdims=True)
+        total = jnp.sum(sum(weights[1:], weights[0]), axis=1, keepdims=True)
         parts = [
-            jnp.dot(
-                weights[parity].astype(jnp.bfloat16),
-                keys[:, cut : cut + VLAT],
-                preferred_element_type=jnp.float32,
-            )
-            for parity, cut in ((0, 0), (1, VLAT + 128))
+            jnp.dot(weight.astype(jnp.bfloat16), rows[:, columns], preferred_element_type=jnp.float32)
+            for weight, (_, rows, (columns, _)) in zip(weights, groups)
         ]
-        mixture = parts[0] + parts[1]
+        mixture = sum(parts[1:], parts[0])
         if not first:
             rescale = jnp.exp2((top_old - top) * exponent_scale)
             total = total + total_old * rescale
             mixture = mixture + before[0][h] * rescale
         if last:
-            mixture = (mixture / total).astype(jnp.bfloat16)
+            mixture = (mixture * (1.0 / total)).astype(jnp.bfloat16)
             out = jnp.dot(mixture, w[h], preferred_element_type=jnp.float32)
             after[0][:, h * VHEAD : (h + 1) * VHEAD] = out.astype(jnp.bfloat16)
         else:
@@ -273,20 +320,43 @@
         following = scored(h + 1) if h < 3 else None
         mixed(h, pieces)
         pieces = following
-
-
-def attended(blocks, place, length, spread, heads, tails, state, w):
-    n, first, last = len(blocks), not state, bool(w)
+        if last and h == 1:
+            page, target = new_page(place, new_owner, new_slot)
+            fill.wait()
+
+            @pl.when(target >= 0)
+            def _():
+                write_page(place, page, target, fresh[...], slots)
+
+            flush.start()
+    if last:
+        flush.wait()
+
+
+def attended(blocks, place, length, spread, heads, tails, state, ending=()):
+    n, first, last = len(blocks), not state, bool(ending)
     whole = lambda *shape: pl.BlockSpec(shape, lambda h, *_: (0,) * len(shape))
+    in_hbm = pl.BlockSpec(memory_space=pltpu.HBM)
     state_specs = [whole(4, SUF, VLAT), whole(4, SUF, 128)]
-    own_heads, own_tails = [heads[b] for b in blocks], [tails[b] for b in blocks]
-    others = [heads[b] for b in range(4) if b not in blocks] if last else []
-    rows = 256 * n + (128 if last else 0)
-    scratch = [pltpu.VMEM((rows, PAIR), jnp.bfloat16)]
-    if last:
-        out_shape = jax.ShapeDtypeStruct((SUF, 4 * VHEAD), jnp.bfloat16)
-        out_specs = whole(SUF, 4 * VHEAD)
-        scratch.append(pltpu.VMEM((4, VLAT, VHEAD), jnp.bfloat16))
+    own_heads, own_tails = ([a for b in blocks for a in parts[b]] for parts in (heads, tails))
+    others, w, tables, pool = [], [], (), []
+    scratch = [pltpu.VMEM((256 * n, PAIR), jnp.bfloat16)]
+    if last:
+        w, new_owner, new_slot, pool = ending
+        tables, pool = (new_owner, new_slot), [pool]
+        others = [a for b in range(4) if b not in blocks for a in heads[b]]
+        out_shape = [
+            jax.ShapeDtypeStruct((SUF, 4 * VHEAD), jnp.bfloat16),
+            jax.ShapeDtypeStruct((SLOTS, PAGE * LAT), jnp.bfloat16),
+        ]
+        out_specs = [whole(SUF, 4 * VHEAD), in_hbm]
+        scratch += [
+            pltpu.VMEM((128, PAIR), jnp.bfloat16),
+            pltpu.VMEM((SUF, VLAT + 128), jnp.bfloat16),
+            pltpu.VMEM((4, VLAT, VHEAD), jnp.bfloat16),
+            pltpu.VMEM((SLOTS, PAGE * LAT), jnp.bfloat16),
+            pltpu.SemaphoreType.DMA((2,)),
+        ]
     else:
         out_shape = [
             jax.ShapeDtypeStruct((4, SUF, VLAT), jnp.float32),
@@ -297,18 +367,18 @@
     def kernel(*refs):
         attend_kernel(blocks, first, last, *refs)
 
+    keys = 256 * n + (128 if last else 0)
     return pl.pallas_call(
         kernel,
         out_shape=out_shape,
         grid_spec=pltpu.PrefetchScalarGridSpec(
-            num_scalar_prefetch=2,
+            num_scalar_prefetch=2 + len(tables),
             grid=(1,),
             in_specs=[
                 *[whole(4, SUF, VLAT + 128)] * 2,
-                *[whole(4 * HEAD_ROWS, PAIR)] * n,
-                *[whole(4 * TAIL_ROWS, PAIR)] * n,
-                *[whole(4 * HEAD_ROWS, PAIR)] * len(others),
-                *([whole(4, 4, VLAT // 8, VHEAD)] * 2 if last else []),
+                *[whole(*a.shape) for a in (*own_heads, *own_tails, *others)],
+                *[whole(4, 4, VLAT // 8, VHEAD)] * len(w),
+                *[in_hbm] * len(pool),
                 *([] if first else state_specs),
             ],
             out_specs=out_specs,
@@ -316,85 +386,45 @@
         ),
         compiler_params=pltpu.CompilerParams(vmem_limit_bytes=40 * MIB),
         cost_estimate=pl.CostEstimate(
-            flops=8 * SUF * rows * (2 * VLAT + 128) * 2,
-            transcendentals=8 * SUF * rows,
+            flops=8 * SUF * keys * (2 * VLAT + 128) * 2,
+            transcendentals=8 * SUF * keys,
             bytes_accessed=16 * MIB,
         ),
         name="attend_" + "".join(str(b) for b in blocks),
-    )(place, length, *spread, *own_heads, *own_tails, *others, *w, *state)
-
-
-def update_kernel(place, new_owner, new_slot, pool_ref, *refs):
-    heads, out_ref, fresh = refs[:4], refs[4], refs[5]
-    me = place[0]
-    page, target = jnp.int32(0), jnp.int32(-1)
-    for m in range(NEWP):
-        hit = new_owner[0, m] == me
-        page = jnp.where(hit, m, page)
-        target = jnp.where(hit, new_slot[0, m], target)
-    for b in range(4):
-        for s in range(4):
-            k = 4 * b + s
-            fresh[k * 8 : (k + 1) * 8] = heads[b][s * HEAD_ROWS + 32 : (s + 1) * HEAD_ROWS]
-    x, y = (me // 4) % 4, me % 4
-    row = lax.broadcasted_iota(jnp.int32, (CHUNKS, 128), 0)
-    col = lax.broadcasted_iota(jnp.int32, (CHUNKS, 128), 1)
-    holder = page * 8 + (row >> 2)
-    part, block = gray((x - (holder >> 2)) & 3), gray((y - holder) & 3)
-    source = block * 32 + part * 8 + (holder >> 4) * 4 + (row & 3)
-    pick = (col == source).astype(jnp.float32).astype(jnp.bfloat16)
-    rows = jnp.dot(pick, fresh[...], preferred_element_type=jnp.float32)
-    turned = pltpu.roll(rows[:, VLAT:], LAT, 1)
-    rows = jnp.concatenate([rows[:, :VLAT], turned], axis=1)
-    mine = lax.broadcasted_iota(jnp.int32, (SLOTS, PAIR), 0) == target
-    for c in range(CHUNKS):
-        old = pool_ref[:, c * PAIR : (c + 1) * PAIR].astype(jnp.float32)
-        out_ref[:, c * PAIR : (c + 1) * PAIR] = jnp.where(mine, rows[c : c + 1], old).astype(jnp.bfloat16)
-
-
-def updated_pool(place, new_owner, new_slot, pool, heads):
-    return pl.pallas_call(
-        update_kernel,
-        out_shape=jax.ShapeDtypeStruct(pool.shape, pool.dtype),
-        grid_spec=pltpu.PrefetchScalarGridSpec(
-            num_scalar_prefetch=3,
-            grid=(1,),
-            in_specs=[
-                pl.BlockSpec(pool.shape, lambda i, *_: (0, 0)),
-                *[pl.BlockSpec((4 * HEAD_ROWS, PAIR), lambda i, *_: (0, 0))] * 4,
-            ],
-            out_specs=pl.BlockSpec(pool.shape, lambda i, *_: (0, 0)),
-            scratch_shapes=[pltpu.VMEM((128, PAIR), jnp.bfloat16)],
-        ),
-        compiler_params=pltpu.CompilerParams(vmem_limit_bytes=32 * MIB),
-        cost_estimate=pl.CostEstimate(flops=0, transcendentals=0, bytes_accessed=6 * MIB),
-        name="update_pool",
-    )(place, new_owner, new_slot, pool, *heads)
+    )(place, length, *tables, *spread, *own_heads, *own_tails, *others, *w, *pool, *state)
 
 
 def local(queries, new_latent, pool, page_owner, page_slot, new_owner, new_slot, prefix_len, w_uv):
     place = jnp.stack([lax.axis_index(POOL), lax.axis_index(SERVE)]).astype(jnp.int32)
     w_row = jnp.stack([w_uv] + [shifted(w_uv, "serve_0", k) for k in HOPS[1:]])
-    pieces = selected_pieces(page_owner, page_slot, place, pool[0])
+    page_owner, page_slot, new_owner, new_slot, in_place = (
+        pltpu.with_memory_space_constraint(a, pltpu.HBM)
+        for a in (page_owner, page_slot, new_owner, new_slot, pool[0])
+    )
+    pieces = selected_pieces(page_owner, page_slot, place, in_place)
     received = lax.all_to_all(pieces, PLANE, 0, 0, tiled=True).reshape(128, PAIR)
     mine = merged_rows(page_owner, place, received, new_latent)
-    mine, queries, w_row = lax.optimization_barrier((mine, queries, w_row))
-    w = [w_row, lax.ppermute(w_row, "serve_1", [(0, 1), (1, 0)])]
+    mine, queries = lax.optimization_barrier((mine, queries))
     spread = spread_queries(queries[0])
     both = mine + lax.ppermute(mine, "pool_0", [(0, 1), (1, 0)])
+    both, w_row = lax.optimization_barrier((both, w_row))
+    w = [w_row, lax.ppermute(w_row, "serve_1", [(0, 1), (1, 0)])]
     head, tail = both[:HEAD_ROWS], both[HEAD_ROWS:]
-    head_row = jnp.concatenate([head] + [shifted(head, "pool_1", k) for k in HOPS[1:]])
-    tail_row = jnp.concatenate([tail] + [shifted(tail, "pool_2", k) for k in HOPS[1:]])
-    head_row, tail_row, *w = lax.optimization_barrier((head_row, tail_row, *w))
-    state = attended((0,), place, prefix_len, spread, [head_row], [tail_row], (), ())
-    state, late = lax.optimization_barrier((state, tail_row))
-    tail_far = shifted(late, "pool_1", HOPS[3])
-    head_far = shifted(head_row, "pool_2", HOPS[3])
-    tails = [tail_row] + [shifted(tail_row, "pool_1", k) for k in HOPS[1:3]] + [tail_far]
-    heads = [head_row] + [shifted(head_row, "pool_2", k) for k in HOPS[1:3]] + [head_far]
-    state = attended((1, 2), place, prefix_len, spread, heads, tails, state, ())
-    out = attended((3,), place, prefix_len, spread, heads, tails, state, w)
-    updated = updated_pool(place, new_owner, new_slot, pool[0], heads)
+    head_parts = [shifted(head, "pool_1", k) for k in HOPS[1:]]
+    tail_parts = [shifted(tail, "pool_2", k) for k in HOPS[1:]]
+    head_parts, tail_parts[:2] = lax.optimization_barrier((head_parts, tail_parts[:2]))
+    head_row = jnp.concatenate([head, *head_parts])
+    tail_row = jnp.concatenate([tail, *tail_parts])
+    tail_row, *w = lax.optimization_barrier((tail_row, *w))
+    heads, tails = [[head_row]], [[tail_row]]
+    state = attended((0,), place, prefix_len, spread, heads, tails, ())
+    for rows, axis in ((heads, "pool_2"), (tails, "pool_1")):
+        rows += [[shifted(rows[0][0], axis, k)] for k in HOPS[1:3]]
+        half = rows[0][0].shape[0] // 2
+        rows.append([shifted(rows[1][0][:half], axis, 1), shifted(rows[2][0][half:], axis, 3)])
+    state = attended((1, 2), place, prefix_len, spread, heads, tails, state)
+    ending = (w, new_owner, new_slot, in_place)
+    out, updated = attended((3,), place, prefix_len, spread, heads, tails, state, ending)
     return (out[None], updated[None])
 
 

time: 83 us -> 75.4 us (0.908)
  the two profiles are of different devices: /device:TPU:1 before, /device:TPU:64 now
where the time goes in v3:
time: 75.4 us; the launch traced here: 75.1 us
  starting transfers between devices  38 us (50%)
  waiting for transfers between devices  18.6 us (25%)
  Pallas kernels  16.5 us (22%)
  between operations  1.68 us (2%)
    ppermute x17, starting transfers between devices, shifted(): return lax.ppermute(x, axis, [(i, (i + hop) % SIDE) for i in range(SIDE)])  25.5 us
    pallas_call x3, Pallas kernels, attended(): pl.pallas_call(kernel, out_shape=out_shape, grid_spec=pltpu.PrefetchScala...  11.7 us
    ppermute x17, waiting for transfers between devices, shifted(): return lax.ppermute(x, axis, [(i, (i + hop) % SIDE) for i in range(SIDE)])  7.63 us
    all_to_all x1, starting transfers between devices, local(): lax.all_to_all(pieces, PLANE, 0, 0, tiled=True).reshape(128, PAIR)  7.04 us
    ppermute x1, waiting for transfers between devices, local(): both = mine + lax.ppermute(mine, 'pool_0', [(0, 1), (1, 0)])  6.54 us
    ppermute x1, starting transfers between devices, local(): both = mine + lax.ppermute(mine, 'pool_0', [(0, 1), (1, 0)])  5.47 us
    all_to_all x1, waiting for transfers between devices, local(): lax.all_to_all(pieces, PLANE, 0, 0, tiled=True).reshape(128, PAIR)  4.38 us
    pallas_call x1, Pallas kernels, selected_pieces(): pl.pallas_call(select_kernel, out_shape=jax.ShapeDtypeStruct((16, 8, PAIR...  3.23 us
  transfers between devices with their start and end apart: 20, of which 5 were waited for; matrix products, arithmetic and copies ran while one was open for 0% of the time, Pallas kernels for 10%

profile of v3, /device:TPU:64, one launch (start us, length us, event | category | flops | bytes accessed | tf_op | source)
XLA Modules:
  0.0 75.1 jit_solution(5510015446976022929)
XLA Ops:
  0.7 3.2 %select_pages.1 = bf16[16,8,1152]{2,1,0:T(8,128)(2,1)} custom-call(s32[1,32]{1,0:T(1,128)} %owner.3, s32[1,32]{1,0:T(1,128)} %slot.1, s32[2]{0:T(128)S(1)} %pad_add_fusion.place.refs_0_, bf16[12,36864]{1,0:T(8,128)(2,1)} %bitcast.13), custom_call_target="tpu_custom_call" | custom-call | tf_op jit(solution)/shard_map/select_pages/pallas_call | solution.py:64
  4.0 7.0 %all-to-all-start = ((bf16[16,8,1152]{2,1,0:T(8,128)(2,1)}), bf16[16,8,1152]{2,1,0:T(8,128)(2,1)S(1)}, u32[]{:S(2)}, u32[]{:S(2)}) async-start(bf16[16,8,1152]{2,1,0:T(8,128)(2,1)} %select_pages.1), calls=%async_computation | async-start | bytes 589824 | tf_op jit(solution)/shard_map/all_to_all | solution.py:405
  11.0 2.0 %collective-permute-start.1 = (bf16[4,64,128]{2,1,0:T(8,128)(2,1)S(1)}, bf16[4,64,128]{2,1,0:T(8,128)(2,1)S(1)}, u32[]{:S(2)}, u32[]{:S(2)}) collective-permute-start(bf16[4,64,128]{2,1,0:T(8,128)(2,1)S(1)} %copy-done.2), channel_id=1, source_target_pairs={{0,2},{2,4},{4,6},{6,0},{1,3},{3,5},{5,7},{7,1},{8,10},{10,12},{12... | collective-permute-start | bytes 196616 | tf_op jit(solution)/shard_map/ppermute | solution.py:133
  13.1 2.3 %collective-permute-start.3 = (bf16[4,64,128]{2,1,0:T(8,128)(2,1)S(1)}, bf16[4,64,128]{2,1,0:T(8,128)(2,1)S(1)}, u32[]{:S(2)}, u32[]{:S(2)}) collective-permute-start(bf16[4,64,128]{2,1,0:T(8,128)(2,1)S(1)} %copy-done.2), channel_id=1, source_target_pairs={{0,4},{2,6},{4,0},{6,2},{1,5},{3,7},{5,1},{7,3},{8,12},{10,14},{12... | collective-permute-start | bytes 196616 | tf_op jit(solution)/shard_map/ppermute | solution.py:133
  15.5 4.4 %all-to-all-done = bf16[16,8,1152]{2,1,0:T(8,128)(2,1)S(1)} async-done(((bf16[16,8,1152]{2,1,0:T(8,128)(2,1)}), bf16[16,8,1152]{2,1,0:T(8,128)(2,1)S(1)}, u32[]{:S(2)}, u32[]{:S(2)}) %all-to-all-start) | async-done | bytes 294944 | tf_op jit(solution)/shard_map/all_to_all | solution.py:405
  19.9 1.2 %merge_pages.1 = bf16[72,1152]{1,0:T(8,128)(2,1)S(1)} custom-call(s32[1,32]{1,0:T(1,128)} %owner.3, s32[2]{0:T(128)S(1)} %pad_add_fusion.place.refs_0_, bf16[128,1152]{1,0:T(8,128)(2,1)S(1)} %bitcast.12, bf16[1,4608]{1,0:T(2,128)(2,1)S(1)} %copy-done.1), custom_call_target="tpu_custom_call" | custom-call | tf_op jit(solution)/shard_map/merge_pages/pallas_call | solution.py:114
  21.0 5.5 %collective-permute-start = (bf16[72,1152]{1,0:T(8,128)(2,1)S(1)}, bf16[72,1152]{1,0:T(8,128)(2,1)S(1)}, u32[]{:S(2)}, u32[]{:S(2)}) collective-permute-start(bf16[72,1152]{1,0:T(8,128)(2,1)S(1)} %merge_pages.1), channel_id=1, source_target_pairs={{0,128},{128,0},{1,129},{129,1},{2,130},{130,2},{3,131},{131,3},{4... | collective-permute-start | bytes 497672 | tf_op jit(solution)/shard_map/ppermute | solution.py:409
  26.6 6.5 %collective-permute-done = bf16[72,1152]{1,0:T(8,128)(2,1)S(1)} collective-permute-done((bf16[72,1152]{1,0:T(8,128)(2,1)S(1)}, bf16[72,1152]{1,0:T(8,128)(2,1)S(1)}, u32[]{:S(2)}, u32[]{:S(2)}) %collective-permute-start) | collective-permute-done | bytes 165920 | tf_op jit(solution)/shard_map/ppermute | solution.py:409
  33.7 2.8 %collective-permute-start.5 = (bf16[40,1152]{1,0:T(8,128)(2,1)S(1)}, bf16[40,1152]{1,0:T(8,128)(2,1)S(1)}, u32[]{:S(2)}, u32[]{:S(2)}) collective-permute-start(bf16[40,1152]{1,0:T(8,128)(2,1)S(1)} %slice.18), channel_id=1, source_target_pairs={{0,96},{32,0},{64,32},{96,64},{1,97},{33,1},{65,33},{97,65},{2,98}... | collective-permute-start | bytes 276488 | tf_op jit(solution)/shard_map/ppermute | solution.py:133
  36.9 1.0 %collective-permute-start.7 = (bf16[32,1152]{1,0:T(8,128)(2,1)S(1)}, bf16[32,1152]{1,0:T(8,128)(2,1)S(1)}, u32[]{:S(2)}, u32[]{:S(2)}) collective-permute-start(bf16[32,1152]{1,0:T(8,128)(2,1)S(1)} %slice.19), channel_id=1, source_target_pairs={{0,8},{8,16},{16,24},{24,0},{1,9},{9,17},{17,25},{25,1},{2,10},{10... | collective-permute-start | bytes 221192 | tf_op jit(solution)/shard_map/ppermute | solution.py:133
  37.9 2.2 %collective-permute-start.8 = (bf16[32,1152]{1,0:T(8,128)(2,1)S(1)}, bf16[32,1152]{1,0:T(8,128)(2,1)S(1)}, u32[]{:S(2)}, u32[]{:S(2)}) collective-permute-start(bf16[32,1152]{1,0:T(8,128)(2,1)S(1)} %slice.19), channel_id=1, source_target_pairs={{0,24},{8,0},{16,8},{24,16},{1,25},{9,1},{17,9},{25,17},{2,26},{10... | collective-permute-start | bytes 221192 | tf_op jit(solution)/shard_map/ppermute | solution.py:133
  40.1 2.3 %collective-permute-done.7 = bf16[32,1152]{1,0:T(8,128)(2,1)S(1)} collective-permute-done((bf16[32,1152]{1,0:T(8,128)(2,1)S(1)}, bf16[32,1152]{1,0:T(8,128)(2,1)S(1)}, u32[]{:S(2)}, u32[]{:S(2)}) %collective-permute-start.7) | collective-permute-done | bytes 73760 | tf_op jit(solution)/shard_map/ppermute | solution.py:133
  42.4 1.3 %collective-permute-start.13 = (bf16[32,1152]{1,0:T(8,128)(2,1)S(1)}, bf16[32,1152]{1,0:T(8,128)(2,1)S(1)}, u32[]{:S(2)}, u32[]{:S(2)}) collective-permute-start(bf16[32,1152]{1,0:T(8,128)(2,1)S(1)} %slice.19), channel_id=1, source_target_pairs={{0,16},{8,24},{16,0},{24,8},{1,17},{9,25},{17,1},{25,9},{2,18},{10... | collective-permute-start | bytes 221192 | tf_op jit(solution)/shard_map/ppermute | solution.py:133
  43.8 2.8 %collective-permute-start.11 = (bf16[160,1152]{1,0:T(8,128)(2,1)S(1)}, bf16[160,1152]{1,0:T(8,128)(2,1)S(1)}, u32[]{:S(2)}, u32[]{:S(2)}) collective-permute-start(bf16[160,1152]{1,0:T(8,128)(2,1)S(1)} %pad_maximum_fusion.refs_4_.refs_10_), channel_id=1, source_target_pairs={{0,24},{8,0},{16,8},{24,16},{1,25},{9,1},{17,9},{25,17},{2,26},{10... | collective-permute-start | bytes 1105928 | tf_op jit(solution)/shard_map/ppermute | solution.py:133
  46.6 1.7 %collective-permute-done.13 = bf16[32,1152]{1,0:T(8,128)(2,1)S(1)} collective-permute-done((bf16[32,1152]{1,0:T(8,128)(2,1)S(1)}, bf16[32,1152]{1,0:T(8,128)(2,1)S(1)}, u32[]{:S(2)}, u32[]{:S(2)}) %collective-permute-start.13) | collective-permute-done | bytes 73760 | tf_op jit(solution)/shard_map/ppermute | solution.py:133
  48.3 0.9 %collective-permute-start.15 = (bf16[128,1152]{1,0:T(8,128)(2,1)S(1)}, bf16[128,1152]{1,0:T(8,128)(2,1)S(1)}, u32[]{:S(2)}, u32[]{:S(2)}) collective-permute-start(bf16[128,1152]{1,0:T(8,128)(2,1)S(1)} %pad_maximum_fusion.1.refs_5_), channel_id=1, source_target_pairs={{0,32},{32,64},{64,96},{96,0},{1,33},{33,65},{65,97},{97,1},{2,34}... | collective-permute-start | bytes 884744 | tf_op jit(solution)/shard_map/ppermute | solution.py:133
  49.3 2.4 %collective-permute-start.17 = (bf16[128,1152]{1,0:T(8,128)(2,1)S(1)}, bf16[128,1152]{1,0:T(8,128)(2,1)S(1)}, u32[]{:S(2)}, u32[]{:S(2)}) collective-permute-start(bf16[128,1152]{1,0:T(8,128)(2,1)S(1)} %pad_maximum_fusion.1.refs_5_), channel_id=1, source_target_pairs={{0,96},{32,0},{64,32},{96,64},{1,97},{33,1},{65,33},{97,65},{2,98}... | collective-permute-start | bytes 884744 | tf_op jit(solution)/shard_map/ppermute | solution.py:133
  52.8 2.2 %attend_0.1 = (f32[4,256,512]{2,1,0:T(8,128)S(1)}, f32[4,256,128]{2,1,0:T(8,128)S(1)}) custom-call(s32[2]{0:T(128)S(1)} %pad_add_fusion.place.refs_0_, s32[1]{0:T(128)S(6)} %copy.11.refs_1_, bf16[4,256,640]{2,1,0:T(8,128)(2,1)S(1)} %get-tuple-element.23.refs_2_.refs_4_, bf16[4,256,640]{2,1,0:T(8,128)(2,1)S(1)} %get-tuple-element.24.refs_3_.refs_5_, ...), custom_call_target="tpu_custom_call" | custom-call | flops 1207959552 | bytes 16777216 | tf_op jit(solution)/shard_map/attend_0/pallas_call | solution.py:371
  55.0 3.6 %collective-permute-done.9.refs_4_.refs_11_ = bf16[160,1152]{1,0:T(8,128)(2,1)S(1)} collective-permute-done((bf16[160,1152]{1,0:T(8,128)(2,1)S(1)}, bf16[160,1152]{1,0:T(8,128)(2,1)S(1)}, u32[]{:S(2)}, u32[]{:S(2)}) %collective-permute-start.9) | collective-permute-done | bytes 368672 | tf_op jit(solution)/shard_map/ppermute | solution.py:133
  58.7 3.3 %collective-permute-start.12 = (bf16[80,1152]{1,0:T(8,128)(2,1)S(1)}, bf16[80,1152]{1,0:T(8,128)(2,1)S(1)}, u32[]{:S(2)}, u32[]{:S(2)}) collective-permute-start(bf16[80,1152]{1,0:T(8,128)(2,1)S(1)} %slice.25), channel_id=1, source_target_pairs={{0,24},{8,0},{16,8},{24,16},{1,25},{9,1},{17,9},{25,17},{2,26},{10... | collective-permute-start | bytes 552968 | tf_op jit(solution)/shard_map/ppermute | solution.py:133
  62.0 0.9 %collective-permute-start.16 = (bf16[64,1152]{1,0:T(8,128)(2,1)S(1)}, bf16[64,1152]{1,0:T(8,128)(2,1)S(1)}, u32[]{:S(2)}, u32[]{:S(2)}) collective-permute-start(bf16[64,1152]{1,0:T(8,128)(2,1)S(1)} %slice.26), channel_id=1, source_target_pairs={{0,32},{32,64},{64,96},{96,0},{1,33},{33,65},{65,97},{97,1},{2,34}... | collective-permute-start | bytes 442376 | tf_op jit(solution)/shard_map/ppermute | solution.py:133
  62.9 2.5 %collective-permute-start.18 = (bf16[64,1152]{1,0:T(8,128)(2,1)S(1)}, bf16[64,1152]{1,0:T(8,128)(2,1)S(1)}, u32[]{:S(2)}, u32[]{:S(2)}) collective-permute-start(bf16[64,1152]{1,0:T(8,128)(2,1)S(1)} %slice.27), channel_id=1, source_target_pairs={{0,96},{32,0},{64,32},{96,64},{1,97},{33,1},{65,33},{97,65},{2,98}... | collective-permute-start | bytes 442376 | tf_op jit(solution)/shard_map/ppermute | solution.py:133
  65.4 3.8 %attend_12.1 = (f32[4,256,512]{2,1,0:T(8,128)S(1)}, f32[4,256,128]{2,1,0:T(8,128)S(1)}) custom-call(s32[2]{0:T(128)S(1)} %pad_add_fusion.place.refs_0_, s32[1]{0:T(128)S(6)} %copy.11.refs_1_, bf16[4,256,640]{2,1,0:T(8,128)(2,1)S(1)} %get-tuple-element.23.refs_2_.refs_4_, bf16[4,256,640]{2,1,0:T(8,128)(2,1)S(1)} %get-tuple-element.24.refs_3_.refs_5_, ...), custom_call_target="tpu_custom_call" | custom-call | flops 2415919104 | bytes 16777216 | tf_op jit(solution)/shard_map/attend_12/pallas_call | solution.py:371
  69.3 5.7 %attend_3.1 = (bf16[256,512]{1,0:T(8,128)(2,1)}, bf16[12,36864]{1,0:T(8,128)(2,1)}) custom-call(s32[2]{0:T(128)S(1)} %pad_add_fusion.place.refs_0_, s32[1]{0:T(128)S(6)} %copy.11.refs_1_, s32[1,4]{1,0:T(1,128)} %refs_2_.1, s32[1,4]{1,0:T(1,128)} %refs_3_.1, bf16[4,256,640]{2,1,0:T(8,128)(2,1)S(1)} %get-tuple-element.23.refs_2_.refs_4_, ...), custom_call_target="tpu_custom_call" | custom-call | flops 1811939328 | bytes 16777216 | tf_op jit(solution)/shard_map/attend_3/pallas_call | solution.py:371
  (39 shorter events, 1.9 us)
Async XLA Ops:
  0.6 10.4 %copy-start.2 = (bf16[4,64,128]{2,1,0:T(8,128)(2,1)S(1)}, bf16[4,64,128]{2,1,0:T(8,128)(2,1)}, u32[]{:S(2)}) copy-start(bf16[4,64,128]{2,1,0:T(8,128)(2,1)} %param.17) | copy-start | bytes 196612
  0.6 19.2 %copy-start.1 = (bf16[1,4608]{1,0:T(2,128)(2,1)S(1)}, bf16[1,4608]{1,0:T(2,128)(2,1)}, u32[]{:S(2)}) copy-start(bf16[1,4608]{1,0:T(2,128)(2,1)} %suffix_ref.1) | copy-start | bytes 27652
  4.0 15.9 %all-to-all-start = ((bf16[16,8,1152]{2,1,0:T(8,128)(2,1)}), bf16[16,8,1152]{2,1,0:T(8,128)(2,1)S(1)}, u32[]{:S(2)}, u32[]{:S(2)}) async-start(bf16[16,8,1152]{2,1,0:T(8,128)(2,1)} %select_pages.1), calls=%async_computation | async-start | bytes 589824 | tf_op jit(solution)/shard_map/all_to_all | solution.py:405
  11.0 15.5 %collective-permute-start.1 = (bf16[4,64,128]{2,1,0:T(8,128)(2,1)S(1)}, bf16[4,64,128]{2,1,0:T(8,128)(2,1)S(1)}, u32[]{:S(2)}, u32[]{:S(2)}) collective-permute-start(bf16[4,64,128]{2,1,0:T(8,128)(2,1)S(1)} %copy-done.2), channel_id=1, source_target_pairs={{0,2},{2,4},{4,6},{6,0},{1,3},{3,5},{5,7},{7,1},{8,10},{10,12},{12... | collective-permute-start | bytes 196616 | tf_op jit(solution)/shard_map/ppermute | solution.py:133
  13.0 13.5 %collective-permute-start.2 = (bf16[4,64,128]{2,1,0:T(8,128)(2,1)S(1)}, bf16[4,64,128]{2,1,0:T(8,128)(2,1)S(1)}, u32[]{:S(2)}, u32[]{:S(2)}) collective-permute-start(bf16[4,64,128]{2,1,0:T(8,128)(2,1)S(1)} %copy-done.2), channel_id=1, source_target_pairs={{0,6},{2,0},{4,2},{6,4},{1,7},{3,1},{5,3},{7,5},{8,14},{10,8},{12,... | collective-permute-start | bytes 196616 | tf_op jit(solution)/shard_map/ppermute | solution.py:133
  13.1 13.4 %collective-permute-start.3 = (bf16[4,64,128]{2,1,0:T(8,128)(2,1)S(1)}, bf16[4,64,128]{2,1,0:T(8,128)(2,1)S(1)}, u32[]{:S(2)}, u32[]{:S(2)}) collective-permute-start(bf16[4,64,128]{2,1,0:T(8,128)(2,1)S(1)} %copy-done.2), channel_id=1, source_target_pairs={{0,4},{2,6},{4,0},{6,2},{1,5},{3,7},{5,1},{7,3},{8,12},{10,14},{12... | collective-permute-start | bytes 196616 | tf_op jit(solution)/shard_map/ppermute | solution.py:133
  21.0 12.1 %collective-permute-start = (bf16[72,1152]{1,0:T(8,128)(2,1)S(1)}, bf16[72,1152]{1,0:T(8,128)(2,1)S(1)}, u32[]{:S(2)}, u32[]{:S(2)}) collective-permute-start(bf16[72,1152]{1,0:T(8,128)(2,1)S(1)} %merge_pages.1), channel_id=1, source_target_pairs={{0,128},{128,0},{1,129},{129,1},{2,130},{130,2},{3,131},{131,3},{4... | collective-permute-start | bytes 497672 | tf_op jit(solution)/shard_map/ppermute | solution.py:409
  26.5 25.8 %copy-start = (bf16[1,256,2304]{2,1,0:T(8,128)(2,1)S(1)}, bf16[1,256,2304]{2,1,0:T(8,128)(2,1)}, u32[]{:S(2)}) copy-start(bf16[1,256,2304]{2,1,0:T(8,128)(2,1)} %param.9) | copy-start | bytes 3538948
  33.2 10.6 %collective-permute-start.4 = (bf16[40,1152]{1,0:T(8,128)(2,1)S(1)}, bf16[40,1152]{1,0:T(8,128)(2,1)S(1)}, u32[]{:S(2)}, u32[]{:S(2)}) collective-permute-start(bf16[40,1152]{1,0:T(8,128)(2,1)S(1)} %slice.18), channel_id=1, source_target_pairs={{0,32},{32,64},{64,96},{96,0},{1,33},{33,65},{65,97},{97,1},{2,34}... | collective-permute-start | bytes 276488 | tf_op jit(solution)/shard_map/ppermute | solution.py:133
  33.7 10.1 %collective-permute-start.5 = (bf16[40,1152]{1,0:T(8,128)(2,1)S(1)}, bf16[40,1152]{1,0:T(8,128)(2,1)S(1)}, u32[]{:S(2)}, u32[]{:S(2)}) collective-permute-start(bf16[40,1152]{1,0:T(8,128)(2,1)S(1)} %slice.18), channel_id=1, source_target_pairs={{0,96},{32,0},{64,32},{96,64},{1,97},{33,1},{65,33},{97,65},{2,98}... | collective-permute-start | bytes 276488 | tf_op jit(solution)/shard_map/ppermute | solution.py:133
  36.5 7.3 %collective-permute-start.6 = (bf16[40,1152]{1,0:T(8,128)(2,1)S(1)}, bf16[40,1152]{1,0:T(8,128)(2,1)S(1)}, u32[]{:S(2)}, u32[]{:S(2)}) collective-permute-start(bf16[40,1152]{1,0:T(8,128)(2,1)S(1)} %slice.18), channel_id=1, source_target_pairs={{0,64},{32,96},{64,0},{96,32},{1,65},{33,97},{65,1},{97,33},{2,66}... | collective-permute-start | bytes 276488 | tf_op jit(solution)/shard_map/ppermute | solution.py:133
  36.9 5.6 %collective-permute-start.7 = (bf16[32,1152]{1,0:T(8,128)(2,1)S(1)}, bf16[32,1152]{1,0:T(8,128)(2,1)S(1)}, u32[]{:S(2)}, u32[]{:S(2)}) collective-permute-start(bf16[32,1152]{1,0:T(8,128)(2,1)S(1)} %slice.19), channel_id=1, source_target_pairs={{0,8},{8,16},{16,24},{24,0},{1,9},{9,17},{17,25},{25,1},{2,10},{10... | collective-permute-start | bytes 221192 | tf_op jit(solution)/shard_map/ppermute | solution.py:133
  37.9 5.9 %collective-permute-start.8 = (bf16[32,1152]{1,0:T(8,128)(2,1)S(1)}, bf16[32,1152]{1,0:T(8,128)(2,1)S(1)}, u32[]{:S(2)}, u32[]{:S(2)}) collective-permute-start(bf16[32,1152]{1,0:T(8,128)(2,1)S(1)} %slice.19), channel_id=1, source_target_pairs={{0,24},{8,0},{16,8},{24,16},{1,25},{9,1},{17,9},{25,17},{2,26},{10... | collective-permute-start | bytes 221192 | tf_op jit(solution)/shard_map/ppermute | solution.py:133
  42.4 5.9 %collective-permute-start.13 = (bf16[32,1152]{1,0:T(8,128)(2,1)S(1)}, bf16[32,1152]{1,0:T(8,128)(2,1)S(1)}, u32[]{:S(2)}, u32[]{:S(2)}) collective-permute-start(bf16[32,1152]{1,0:T(8,128)(2,1)S(1)} %slice.19), channel_id=1, source_target_pairs={{0,16},{8,24},{16,0},{24,8},{1,17},{9,25},{17,1},{25,9},{2,18},{10... | collective-permute-start | bytes 221192 | tf_op jit(solution)/shard_map/ppermute | solution.py:133
  43.8 4.6 %collective-permute-start.14 = (bf16[4,4,64,128]{3,2,1,0:T(8,128)(2,1)S(1)}, bf16[4,4,64,128]{3,2,1,0:T(8,128)(2,1)S(1)}, u32[]{:S(2)}, u32[]{:S(2)}) collective-permute-start(bf16[4,4,64,128]{3,2,1,0:T(8,128)(2,1)S(1)} %pad_maximum_fusion.2.refs_13_), channel_id=1, source_target_pairs={{0,1},{1,0},{2,3},{3,2},{4,5},{5,4},{6,7},{7,6},{8,9},{9,8},{10,11... | collective-permute-start | bytes 786440 | tf_op jit(solution)/shard_map/ppermute | solution.py:411
  43.8 14.8 %collective-permute-start.11 = (bf16[160,1152]{1,0:T(8,128)(2,1)S(1)}, bf16[160,1152]{1,0:T(8,128)(2,1)S(1)}, u32[]{:S(2)}, u32[]{:S(2)}) collective-permute-start(bf16[160,1152]{1,0:T(8,128)(2,1)S(1)} %pad_maximum_fusion.refs_4_.refs_10_), channel_id=1, source_target_pairs={{0,24},{8,0},{16,8},{24,16},{1,25},{9,1},{17,9},{25,17},{2,26},{10... | collective-permute-start | bytes 1105928 | tf_op jit(solution)/shard_map/ppermute | solution.py:133
  46.6 11.9 %collective-permute-start.9 = (bf16[160,1152]{1,0:T(8,128)(2,1)S(1)}, bf16[160,1152]{1,0:T(8,128)(2,1)S(1)}, u32[]{:S(2)}, u32[]{:S(2)}) collective-permute-start(bf16[160,1152]{1,0:T(8,128)(2,1)S(1)} %pad_maximum_fusion.refs_4_.refs_10_), channel_id=1, source_target_pairs={{0,8},{8,16},{16,24},{24,0},{1,9},{9,17},{17,25},{25,1},{2,10},{10... | collective-permute-start | bytes 1105928 | tf_op jit(solution)/shard_map/ppermute | solution.py:133
  48.3 13.6 %collective-permute-start.15 = (bf16[128,1152]{1,0:T(8,128)(2,1)S(1)}, bf16[128,1152]{1,0:T(8,128)(2,1)S(1)}, u32[]{:S(2)}, u32[]{:S(2)}) collective-permute-start(bf16[128,1152]{1,0:T(8,128)(2,1)S(1)} %pad_maximum_fusion.1.refs_5_), channel_id=1, source_target_pairs={{0,32},{32,64},{64,96},{96,0},{1,33},{33,65},{65,97},{97,1},{2,34}... | collective-permute-start | bytes 884744 | tf_op jit(solution)/shard_map/ppermute | solution.py:133
  49.3 13.6 %collective-permute-start.17 = (bf16[128,1152]{1,0:T(8,128)(2,1)S(1)}, bf16[128,1152]{1,0:T(8,128)(2,1)S(1)}, u32[]{:S(2)}, u32[]{:S(2)}) collective-permute-start(bf16[128,1152]{1,0:T(8,128)(2,1)S(1)} %pad_maximum_fusion.1.refs_5_), channel_id=1, source_target_pairs={{0,96},{32,0},{64,32},{96,64},{1,97},{33,1},{65,33},{97,65},{2,98}... | collective-permute-start | bytes 884744 | tf_op jit(solution)/shard_map/ppermute | solution.py:133
  58.6 10.7 %collective-permute-start.10 = (bf16[80,1152]{1,0:T(8,128)(2,1)S(1)}, bf16[80,1152]{1,0:T(8,128)(2,1)S(1)}, u32[]{:S(2)}, u32[]{:S(2)}) collective-permute-start(bf16[80,1152]{1,0:T(8,128)(2,1)S(1)} %slice.24), channel_id=1, source_target_pairs={{0,8},{8,16},{16,24},{24,0},{1,9},{9,17},{17,25},{25,1},{2,10},{10... | collective-permute-start | bytes 552968 | tf_op jit(solution)/shard_map/ppermute | solution.py:133
  58.7 10.6 %collective-permute-start.12 = (bf16[80,1152]{1,0:T(8,128)(2,1)S(1)}, bf16[80,1152]{1,0:T(8,128)(2,1)S(1)}, u32[]{:S(2)}, u32[]{:S(2)}) collective-permute-start(bf16[80,1152]{1,0:T(8,128)(2,1)S(1)} %slice.25), channel_id=1, source_target_pairs={{0,24},{8,0},{16,8},{24,16},{1,25},{9,1},{17,9},{25,17},{2,26},{10... | collective-permute-start | bytes 552968 | tf_op jit(solution)/shard_map/ppermute | solution.py:133
  62.0 7.3 %collective-permute-start.16 = (bf16[64,1152]{1,0:T(8,128)(2,1)S(1)}, bf16[64,1152]{1,0:T(8,128)(2,1)S(1)}, u32[]{:S(2)}, u32[]{:S(2)}) collective-permute-start(bf16[64,1152]{1,0:T(8,128)(2,1)S(1)} %slice.26), channel_id=1, source_target_pairs={{0,32},{32,64},{64,96},{96,0},{1,33},{33,65},{65,97},{97,1},{2,34}... | collective-permute-start | bytes 442376 | tf_op jit(solution)/shard_map/ppermute | solution.py:133
  62.9 6.3 %collective-permute-start.18 = (bf16[64,1152]{1,0:T(8,128)(2,1)S(1)}, bf16[64,1152]{1,0:T(8,128)(2,1)S(1)}, u32[]{:S(2)}, u32[]{:S(2)}) collective-permute-start(bf16[64,1152]{1,0:T(8,128)(2,1)S(1)} %slice.27), channel_id=1, source_target_pairs={{0,96},{32,0},{64,32},{96,64},{1,97},{33,1},{65,33},{97,65},{2,98}... | collective-permute-start | bytes 442376 | tf_op jit(solution)/shard_map/ppermute | solution.py:133

commit v4 on v3

--- a/solution.py
+++ b/solution.py
@@ -32,21 +32,43 @@
 MIB = 1 << 20
 
 
-def select_kernel(owner, slot, place, pool_hbm, out_ref, rows, arrived):
-    copies = []
+def select_kernel(place, owner_hbm, slot_hbm, pool_hbm, suffix_hbm, *refs):
+    out_ref, source_ref, own_ref, rows, fresh, owner, slot, count, arrived = refs
+    copies = [
+        pltpu.make_async_copy(owner_hbm, owner, arrived.at[4]),
+        pltpu.make_async_copy(slot_hbm, slot, arrived.at[5]),
+        pltpu.make_async_copy(suffix_hbm, fresh, arrived.at[6]),
+    ]
     for i in range(4):
         columns = slice(i * 8 * PAIR, (i + 1) * 8 * PAIR)
         copies.append(
             pltpu.make_async_copy(pool_hbm.at[:, columns], rows.at[:, columns], arrived.at[i])
         )
-        copies[i].start()
-    me = place[0]
-    count = jnp.int32(0)
+    for copy in copies:
+        copy.start()
+    me, depth = place[0], place[0] // 16
+    for j in range(PPAGES):
+        count[j] = 0
+    copies[0].wait()
+    copies[1].wait()
+    row = lax.broadcasted_iota(jnp.int32, (PPAGES, 128), 0)
+    source = jnp.full((PPAGES, 128), -8, jnp.int32)
     chosen = [jnp.int32(0)] * HOT
     for j in range(PPAGES):
-        hit = owner[0, j] == me
-        chosen = [jnp.where(hit & (count == k), slot[0, j], chosen[k]) for k in range(HOT)]
-        count = count + hit.astype(jnp.int32)
+        holder = owner[0, j]
+        rank = count[holder]
+        count[holder] = rank + 1
+        chosen = [jnp.where((holder == me) & (rank == k), slot[0, j], chosen[k]) for k in range(HOT)]
+        at = jnp.where(holder // 16 == depth, (holder % 16) * 8 + rank, -8)
+        source = jnp.where(row == j, at, source)
+    source_ref[...] = source
+    copies[2].wait()
+    suffix = fresh[...].astype(jnp.float32)
+    row = lax.broadcasted_iota(jnp.int32, (8, PAIR), 0)
+    own = jnp.zeros((8, PAIR), jnp.float32)
+    for t in range(4):
+        own = jnp.where(row == depth * 4 + t, suffix[:, t * PAIR : (t + 1) * PAIR], own)
+    own_ref[...] = own
     row = lax.broadcasted_iota(jnp.int32, (8, SLOTS), 0) % 4
     col = lax.broadcasted_iota(jnp.int32, (8, SLOTS), 1)
     want = jnp.where(row == 0, chosen[0], jnp.where(row == 1, chosen[1], chosen[2]))
@@ -54,83 +76,77 @@
     upper = lax.broadcasted_iota(jnp.int32, (8, PAIR), 0) < 4
     for d in range(16):
         if d % 4 == 0:
-            copies[d // 4].wait()
+            copies[3 + d // 4].wait()
         both = rows[:, 2 * d * PAIR : (2 * d + 2) * PAIR]
         picked = jnp.dot(pick, both, preferred_element_type=jnp.float32)
         out_ref[d] = jnp.where(upper, picked[:, :PAIR], picked[:, PAIR:]).astype(jnp.bfloat16)
 
 
-def selected_pieces(owner, slot, place, pool):
+def selected_pieces(place, owner, slot, pool, suffix):
+    in_hbm = pl.BlockSpec(memory_space=pltpu.HBM)
+    whole = lambda *shape: pl.BlockSpec(shape, lambda i, *_: (0,) * len(shape))
     return pl.pallas_call(
         select_kernel,
-        out_shape=jax.ShapeDtypeStruct((16, 8, PAIR), jnp.bfloat16),
+        out_shape=[
+            jax.ShapeDtypeStruct((16, 8, PAIR), jnp.bfloat16),
+            jax.ShapeDtypeStruct((PPAGES, 128), jnp.int32),
+            jax.ShapeDtypeStruct((8, PAIR), jnp.float32),
+        ],
         grid_spec=pltpu.PrefetchScalarGridSpec(
-            num_scalar_prefetch=3,
+            num_scalar_prefetch=1,
             grid=(1,),
-            in_specs=[pl.BlockSpec(memory_space=pltpu.HBM)],
-            out_specs=pl.BlockSpec((16, 8, PAIR), lambda i, *_: (0, 0, 0)),
+            in_specs=[in_hbm] * 4,
+            out_specs=[whole(16, 8, PAIR), whole(PPAGES, 128), whole(8, PAIR)],
             scratch_shapes=[
                 pltpu.VMEM((SLOTS, PAGE * LAT), jnp.bfloat16),
-                pltpu.SemaphoreType.DMA((4,)),
+                pltpu.VMEM((1, 4 * PAIR), jnp.bfloat16),
+                pltpu.SMEM((1, PPAGES), jnp.int32),
+                pltpu.SMEM((1, PPAGES), jnp.int32),
+                pltpu.SMEM((PPAGES,), jnp.int32),
+                pltpu.SemaphoreType.DMA((7,)),
             ],
         ),
         compiler_params=pltpu.CompilerParams(vmem_limit_bytes=32 * MIB),
         name="select_pages",
-    )(owner, slot, place, pool)
-
-
-def merge_kernel(owner, place, received_ref, suffix_ref, out_ref, count):
-    depth = place[0] // 16
-    for j in range(PPAGES):
-        count[j] = 0
-    row = lax.broadcasted_iota(jnp.int32, (PPAGES, 128), 0)
+    )(place, owner, slot, pool, suffix)
+
+
+def merge_kernel(received_ref, source_ref, own_ref, out_ref):
     col = lax.broadcasted_iota(jnp.int32, (PPAGES, 128), 1)
-    source = jnp.full((PPAGES, 128), -1, jnp.int32)
-    for j in range(PPAGES):
-        holder = owner[0, j]
-        rank = count[holder]
-        count[holder] = rank + 1
-        at = jnp.where(holder // 16 == depth, (holder % 16) * 8 + rank, -8)
-        source = jnp.where(row == j, at, source)
-    suffix = suffix_ref[...].astype(jnp.float32)
-    place_row = lax.broadcasted_iota(jnp.int32, (8, PAIR), 0)
-    own = jnp.zeros((8, PAIR), jnp.float32)
-    for t in range(4):
-        own = jnp.where(place_row == depth * 4 + t, suffix[:, t * PAIR : (t + 1) * PAIR], own)
     received = received_ref[...]
     halves = []
     for p in range(2):
-        pick = (col == source + 4 * p).astype(jnp.float32).astype(jnp.bfloat16)
+        pick = (col == source_ref[...] + 4 * p).astype(jnp.float32).astype(jnp.bfloat16)
         halves.append(jnp.dot(pick, received, preferred_element_type=jnp.float32))
-    rows = jnp.concatenate([halves[0], own, halves[1]], axis=0)
+    rows = jnp.concatenate([halves[0], own_ref[...], halves[1]], axis=0)
     turned = pltpu.roll(rows[:, VLAT:], LAT, 1)
     out_ref[:, :VLAT] = rows[:, :VLAT].astype(jnp.bfloat16)
     out_ref[:, VLAT : VLAT + 128] = turned[:, VLAT:].astype(jnp.bfloat16)
     out_ref[:, VLAT + 128 :] = turned[:, :VLAT].astype(jnp.bfloat16)
 
 
-def merged_rows(owner, place, received, suffix):
+def merged_rows(received, source, own):
+    whole = lambda *shape: pl.BlockSpec(shape, lambda i: (0,) * len(shape))
     rows = HEAD_ROWS + TAIL_ROWS
     return pl.pallas_call(
         merge_kernel,
         out_shape=jax.ShapeDtypeStruct((rows, PAIR), jnp.bfloat16),
-        grid_spec=pltpu.PrefetchScalarGridSpec(
-            num_scalar_prefetch=2,
-            grid=(1,),
-            in_specs=[
-                pl.BlockSpec((128, PAIR), lambda i, *_: (0, 0)),
-                pl.BlockSpec((1, 4 * PAIR), lambda i, *_: (0, 0)),
-            ],
-            out_specs=pl.BlockSpec((rows, PAIR), lambda i, *_: (0, 0)),
-            scratch_shapes=[pltpu.SMEM((PPAGES,), jnp.int32)],
-        ),
+        grid=(1,),
+        in_specs=[whole(128, PAIR), whole(PPAGES, 128), whole(8, PAIR)],
+        out_specs=whole(rows, PAIR),
         compiler_params=pltpu.CompilerParams(vmem_limit_bytes=32 * MIB),
         name="merge_pages",
-    )(owner, place, received, suffix)
+    )(received, source, own)
 
 
 def shifted(x, axis, hop):
     return lax.ppermute(x, axis, [(i, (i + hop) % SIDE) for i in range(SIDE)])
+
+
+def mirrored(x, axis, hop):
+    places = [(i, core) for i in range(SIDE) for core in range(2)]
+    pairs = [(2 * i + c, 2 * ((i + hop * (1 - 2 * c)) % SIDE) + c) for i, c in places]
+    return lax.ppermute(x, (axis, "serve_1"), pairs)
 
 
 def gray(s):
@@ -167,7 +183,7 @@
     )(queries)
 
 
-def prefix_bias(blocks, parity, x, y, length):
+def prefix_bias(blocks, parity, x, y, way, length):
     lane = lax.broadcasted_iota(jnp.int32, (1, 256 * len(blocks)), 1)
     part, page = (lane >> 5) & 3, lane & 31
     index = (lane >> 7) & (len(blocks) - 1)
@@ -176,16 +192,17 @@
         hop = jnp.where(index == n, HOPS[blocks[n]], hop)
     head = lane < 128 * len(blocks)
     turn = gray(part)
+    hop = hop * way
     far = (x - jnp.where(head, turn, hop)) & 3
     near = (y - jnp.where(head, hop, turn)) & 3
     token = page * PAGE + (far * 4 + near) * 4 + jnp.where(head, 0, 2) + parity
     return jnp.where(token < length, 0.0, masked_score)
 
 
-def suffix_order(x, y):
+def suffix_order(x, y, way):
     lane = lax.broadcasted_iota(jnp.int32, (1, SUF), 1)
     block, part = (lane >> 5) & 3, (lane >> 3) & 3
-    far, near = (x - gray(part)) & 3, (y - gray(block)) & 3
+    far, near = (x - gray(part)) & 3, (y - gray(block) * way) & 3
     holder = ((lane >> 2) & 1) * 16 + far * 4 + near
     return holder * 8 + (lane & 3) * 2 + (lane >> 7)
 
@@ -200,11 +217,11 @@
 
 
 def write_page(place, page, target, fresh, slots):
-    x, y = (place[0] // 4) % 4, place[0] % 4
+    x, y, way = (place[0] // 4) % 4, place[0] % 4, 1 - 2 * (place[1] & 1)
     row = lax.broadcasted_iota(jnp.int32, (CHUNKS, 128), 0)
     col = lax.broadcasted_iota(jnp.int32, (CHUNKS, 128), 1)
     holder = page * 8 + (row >> 2)
-    part, block = gray((x - (holder >> 2)) & 3), gray((y - holder) & 3)
+    part, block = gray((x - (holder >> 2)) & 3), gray(((y - holder) * way) & 3)
     source = block * 32 + part * 8 + (holder >> 4) * 4 + (row & 3)
     pick = (col == source).astype(jnp.float32).astype(jnp.bfloat16)
     rows = jnp.dot(pick, fresh, preferred_element_type=jnp.float32)
@@ -220,12 +237,6 @@
                 slots[low:high, columns] = jnp.where(mine, rows[c : c + 1], old).astype(jnp.bfloat16)
 
 
-def segment(parts, t, rows):
-    part, at = divmod(t * len(parts), 4)
-    start = at // len(parts) * rows
-    return parts[part][start : start + rows]
-
-
 def attend_kernel(blocks, first, last, *refs):
     n = len(blocks)
     refs = list(refs)
@@ -233,11 +244,8 @@
     place, length = take(2)
     new_owner, new_slot = take(2) if last else (None, None)
     even_q, odd_q = take(2)
-    if last:
-        heads, tails, others = [take(2)], [take(2)], [[ref] for ref in take(3)]
-        weights_in, pool = take(2), take(1)[0]
-    else:
-        heads, tails = [[ref] for ref in take(n)], [[ref] for ref in take(n)]
+    heads, tails = take(n), take(n)
+    others, weights_in, pool = (take(4 - n), take(2), take(1)[0]) if last else ([], [], None)
     before = [] if first else take(2)
     after = take(2)
     keys = take(1)[0]
@@ -250,22 +258,21 @@
     for b in range(n):
         for t in range(4):
             row = b * 128 + t * 32
-            keys[row : row + 32] = segment(heads[b], t, HEAD_ROWS)[:32]
-            row = (n + b) * 128 + t * 32
-            keys[row : row + 32] = segment(tails[b], t, TAIL_ROWS)
-    x, y = (place[0] // 4) % 4, place[0] % 4
-    bias = [prefix_bias(blocks, parity, x, y, length[0]) for parity in range(2)]
+            keys[row : row + 32] = heads[b][t * HEAD_ROWS : t * HEAD_ROWS + 32]
+        keys[(n + b) * 128 : (n + b + 1) * 128] = tails[b][...]
+    x, y, way = (place[0] // 4) % 4, place[0] % 4, 1 - 2 * (place[1] & 1)
+    bias = [prefix_bias(blocks, parity, x, y, way, length[0]) for parity in range(2)]
     if last:
         for b, head in enumerate([*others, *heads]):
             for t in range(4):
                 row = b * 32 + t * 8
-                fresh[row : row + 8] = segment(head, t, HEAD_ROWS)[32:]
+                fresh[row : row + 8] = head[t * HEAD_ROWS + 32 : (t + 1) * HEAD_ROWS]
         suffix[:128] = fresh[:, : VLAT + 128]
         suffix[128:, :VLAT] = fresh[:, VLAT + 128 :]
         ropes = fresh[:, VLAT : VLAT + 128].astype(jnp.float32)
         suffix[128:, VLAT:] = pltpu.roll(ropes, 64, 1).astype(jnp.bfloat16)
         token = lax.broadcasted_iota(jnp.int32, (SUF, SUF), 0)
-        hidden = suffix_order(x, y) > token
+        hidden = suffix_order(x, y, way) > token
         for k in range(4):
             for other in range(2):
                 part = ((place[1] // 2 - HOPS[k]) & 3) * 2 + ((place[1] & 1) ^ other)
@@ -338,13 +345,13 @@
     whole = lambda *shape: pl.BlockSpec(shape, lambda h, *_: (0,) * len(shape))
     in_hbm = pl.BlockSpec(memory_space=pltpu.HBM)
     state_specs = [whole(4, SUF, VLAT), whole(4, SUF, 128)]
-    own_heads, own_tails = ([a for b in blocks for a in parts[b]] for parts in (heads, tails))
+    own_heads, own_tails = [heads[b] for b in blocks], [tails[b] for b in blocks]
     others, w, tables, pool = [], [], (), []
     scratch = [pltpu.VMEM((256 * n, PAIR), jnp.bfloat16)]
     if last:
         w, new_owner, new_slot, pool = ending
         tables, pool = (new_owner, new_slot), [pool]
-        others = [a for b in range(4) if b not in blocks for a in heads[b]]
+        others = [heads[b] for b in range(4) if b not in blocks]
         out_shape = [
             jax.ShapeDtypeStruct((SUF, 4 * VHEAD), jnp.bfloat16),
             jax.ShapeDtypeStruct((SLOTS, PAGE * LAT), jnp.bfloat16),
@@ -397,17 +404,17 @@
 def local(queries, new_latent, pool, page_owner, page_slot, new_owner, new_slot, prefix_len, w_uv):
     place = jnp.stack([lax.axis_index(POOL), lax.axis_index(SERVE)]).astype(jnp.int32)
     w_row = jnp.stack([w_uv] + [shifted(w_uv, "serve_0", k) for k in HOPS[1:]])
-    page_owner, page_slot, new_owner, new_slot, in_place = (
+    page_owner, page_slot, new_owner, new_slot, new_latent, in_place = (
         pltpu.with_memory_space_constraint(a, pltpu.HBM)
-        for a in (page_owner, page_slot, new_owner, new_slot, pool[0])
+        for a in (page_owner, page_slot, new_owner, new_slot, new_latent, pool[0])
     )
-    pieces = selected_pieces(page_owner, page_slot, place, in_place)
+    pieces, source, own = selected_pieces(place, page_owner, page_slot, in_place, new_latent)
     received = lax.all_to_all(pieces, PLANE, 0, 0, tiled=True).reshape(128, PAIR)
-    mine = merged_rows(page_owner, place, received, new_latent)
+    mine = merged_rows(received, source, own)
     mine, queries = lax.optimization_barrier((mine, queries))
     spread = spread_queries(queries[0])
     both = mine + lax.ppermute(mine, "pool_0", [(0, 1), (1, 0)])
-    both, w_row = lax.optimization_barrier((both, w_row))
+    both, w_row, spread = lax.optimization_barrier((both, w_row, spread))
     w = [w_row, lax.ppermute(w_row, "serve_1", [(0, 1), (1, 0)])]
     head, tail = both[:HEAD_ROWS], both[HEAD_ROWS:]
     head_parts = [shifted(head, "pool_1", k) for k in HOPS[1:]]
@@ -416,12 +423,11 @@
     head_row = jnp.concatenate([head, *head_parts])
     tail_row = jnp.concatenate([tail, *tail_parts])
     tail_row, *w = lax.optimization_barrier((tail_row, *w))
-    heads, tails = [[head_row]], [[tail_row]]
+    heads, tails = [head_row], [tail_row]
     state = attended((0,), place, prefix_len, spread, heads, tails, ())
     for rows, axis in ((heads, "pool_2"), (tails, "pool_1")):
-        rows += [[shifted(rows[0][0], axis, k)] for k in HOPS[1:3]]
-        half = rows[0][0].shape[0] // 2
-        rows.append([shifted(rows[1][0][:half], axis, 1), shifted(rows[2][0][half:], axis, 3)])
+        rows += [mirrored(rows[0], axis, 1), mirrored(rows[0], axis, 3)]
+        rows.append(mirrored(rows[1], axis, 1))
     state = attended((1, 2), place, prefix_len, spread, heads, tails, state)
     ending = (w, new_owner, new_slot, in_place)
     out, updated = attended((3,), place, prefix_len, spread, heads, tails, state, ending)

time: 75.4 us -> 72.4 us (0.960)
  starting transfers between devices: 38 us -> 30.4 us
  waiting for transfers between devices: 18.6 us -> 23.3 us
    ppermute x17 -> x9, starting transfers between devices: 25.5 us -> 13.1 us  [shifted(): return lax.ppermute(x, axis, [(i, (i + hop) % SIDE) for i in range(SIDE)])]
    ppermute x0 -> x6, waiting for transfers between devices: none -> 6.48 us  [mirrored(): return lax.ppermute(x, (axis, 'serve_1'), pairs)]
    ppermute x0 -> x6, starting transfers between devices: none -> 4.8 us  [mirrored(): return lax.ppermute(x, (axis, 'serve_1'), pairs)]
    ppermute x17 -> x9, waiting for transfers between devices: 7.63 us -> 6.44 us  [shifted(): return lax.ppermute(x, axis, [(i, (i + hop) % SIDE) for i in range(SIDE)])]
    pallas_call x1, Pallas kernels: 1.17 us -> 0.3 us  [merged_rows(): pl.pallas_call(merge_kernel, out_shape=jax.ShapeDtypeStruct((rows, PAIR),...]
  transfers between devices with their start and end apart: 20 -> 18, of which waited for: 5 -> 7; matrix products, arithmetic and copies ran while one was open for 0% -> 0% of each run, Pallas kernels for 10% -> 10%
where the time goes in v4:
time: 72.4 us; the launch traced here: 71.4 us
  starting transfers between devices  30.4 us (42%)
  waiting for transfers between devices  23.3 us (32%)
  Pallas kernels  15.8 us (22%)
  between operations  1.62 us (2%)
    ppermute x9, starting transfers between devices, shifted(): return lax.ppermute(x, axis, [(i, (i + hop) % SIDE) for i in range(SIDE)])  13.1 us
    pallas_call x3, Pallas kernels, attended(): pl.pallas_call(kernel, out_shape=out_shape, grid_spec=pltpu.PrefetchScala...  11.8 us
    all_to_all x1, starting transfers between devices, local(): lax.all_to_all(pieces, PLANE, 0, 0, tiled=True).reshape(128, PAIR)  7.04 us
    ppermute x6, waiting for transfers between devices, mirrored(): return lax.ppermute(x, (axis, 'serve_1'), pairs)  6.48 us
    ppermute x9, waiting for transfers between devices, shifted(): return lax.ppermute(x, axis, [(i, (i + hop) % SIDE) for i in range(SIDE)])  6.44 us
    ppermute x1, waiting for transfers between devices, local(): both = mine + lax.ppermute(mine, 'pool_0', [(0, 1), (1, 0)])  6.05 us
    ppermute x1, starting transfers between devices, local(): both = mine + lax.ppermute(mine, 'pool_0', [(0, 1), (1, 0)])  5.48 us
    ppermute x6, starting transfers between devices, mirrored(): return lax.ppermute(x, (axis, 'serve_1'), pairs)  4.8 us
  transfers between devices with their start and end apart: 18, of which 7 were waited for; matrix products, arithmetic and copies ran while one was open for 0% of the time, Pallas kernels for 10%

profile of v4, /device:TPU:64, one launch (start us, length us, event | category | flops | bytes accessed | tf_op | source)
XLA Modules:
  0.0 71.4 jit_solution(1444461276417307488)
XLA Ops:
  0.7 3.2 %select_pages.1 = (bf16[16,8,1152]{2,1,0:T(8,128)(2,1)}, s32[32,128]{1,0:T(8,128)S(1)}, f32[8,1152]{1,0:T(8,128)S(1)}) custom-call(s32[2]{0:T(128)S(1)} %pad_add_fusion.place.refs_0_, s32[1,32]{1,0:T(1,128)} %owner_hbm.1, s32[1,32]{1,0:T(1,128)} %slot_hbm.1, bf16[12,36864]{1,0:T(8,128)(2,1)} %bitcast.13, bf16[1,4608]{1,0:T(2,128)(2,1)} %suffix_hbm.1), custom_call_target="tpu_custom_call" | custom-call | tf_op jit(solution)/shard_map/select_pages/pallas_call | solution.py:88
  3.9 7.0 %all-to-all-start = ((bf16[16,8,1152]{2,1,0:T(8,128)(2,1)}), bf16[16,8,1152]{2,1,0:T(8,128)(2,1)S(1)}, u32[]{:S(2)}, u32[]{:S(2)}) async-start(bf16[16,8,1152]{2,1,0:T(8,128)(2,1)} %get-tuple-element.27), calls=%async_computation | async-start | bytes 589824 | tf_op jit(solution)/shard_map/all_to_all | solution.py:412
  11.0 2.0 %collective-permute-start.1 = (bf16[4,64,128]{2,1,0:T(8,128)(2,1)S(1)}, bf16[4,64,128]{2,1,0:T(8,128)(2,1)S(1)}, u32[]{:S(2)}, u32[]{:S(2)}) collective-permute-start(bf16[4,64,128]{2,1,0:T(8,128)(2,1)S(1)} %copy-done.1), channel_id=1, source_target_pairs={{0,2},{2,4},{4,6},{6,0},{1,3},{3,5},{5,7},{7,1},{8,10},{10,12},{12... | collective-permute-start | bytes 196616 | tf_op jit(solution)/shard_map/ppermute | solution.py:143
  13.1 2.3 %collective-permute-start.3 = (bf16[4,64,128]{2,1,0:T(8,128)(2,1)S(1)}, bf16[4,64,128]{2,1,0:T(8,128)(2,1)S(1)}, u32[]{:S(2)}, u32[]{:S(2)}) collective-permute-start(bf16[4,64,128]{2,1,0:T(8,128)(2,1)S(1)} %copy-done.1), channel_id=1, source_target_pairs={{0,4},{2,6},{4,0},{6,2},{1,5},{3,7},{5,1},{7,3},{8,12},{10,14},{12... | collective-permute-start | bytes 196616 | tf_op jit(solution)/shard_map/ppermute | solution.py:143
  15.4 4.4 %all-to-all-done = bf16[16,8,1152]{2,1,0:T(8,128)(2,1)S(1)} async-done(((bf16[16,8,1152]{2,1,0:T(8,128)(2,1)}), bf16[16,8,1152]{2,1,0:T(8,128)(2,1)S(1)}, u32[]{:S(2)}, u32[]{:S(2)}) %all-to-all-start) | async-done | bytes 294944 | tf_op jit(solution)/shard_map/all_to_all | solution.py:412
  20.1 5.5 %collective-permute-start = (bf16[72,1152]{1,0:T(8,128)(2,1)S(1)}, bf16[72,1152]{1,0:T(8,128)(2,1)S(1)}, u32[]{:S(2)}, u32[]{:S(2)}) collective-permute-start(bf16[72,1152]{1,0:T(8,128)(2,1)S(1)} %merge_pages.1), channel_id=1, source_target_pairs={{0,128},{128,0},{1,129},{129,1},{2,130},{130,2},{3,131},{131,3},{4... | collective-permute-start | bytes 497672 | tf_op jit(solution)/shard_map/ppermute | solution.py:416
  26.2 6.0 %collective-permute-done = bf16[72,1152]{1,0:T(8,128)(2,1)S(1)} collective-permute-done((bf16[72,1152]{1,0:T(8,128)(2,1)S(1)}, bf16[72,1152]{1,0:T(8,128)(2,1)S(1)}, u32[]{:S(2)}, u32[]{:S(2)}) %collective-permute-start) | collective-permute-done | bytes 165920 | tf_op jit(solution)/shard_map/ppermute | solution.py:416
  32.3 0.7 %collective-permute-start.4 = (bf16[40,1152]{1,0:T(8,128)(2,1)S(1)}, bf16[40,1152]{1,0:T(8,128)(2,1)S(1)}, u32[]{:S(2)}, u32[]{:S(2)}) collective-permute-start(bf16[40,1152]{1,0:T(8,128)(2,1)S(1)} %slice.6), channel_id=1, source_target_pairs={{0,32},{32,64},{64,96},{96,0},{1,33},{33,65},{65,97},{97,1},{2,34}... | collective-permute-start | bytes 276488 | tf_op jit(solution)/shard_map/ppermute | solution.py:143
  33.0 2.6 %collective-permute-start.5 = (bf16[40,1152]{1,0:T(8,128)(2,1)S(1)}, bf16[40,1152]{1,0:T(8,128)(2,1)S(1)}, u32[]{:S(2)}, u32[]{:S(2)}) collective-permute-start(bf16[40,1152]{1,0:T(8,128)(2,1)S(1)} %slice.6), channel_id=1, source_target_pairs={{0,96},{32,0},{64,32},{96,64},{1,97},{33,1},{65,33},{97,65},{2,98}... | collective-permute-start | bytes 276488 | tf_op jit(solution)/shard_map/ppermute | solution.py:143
  35.6 0.8 %collective-permute-start.6 = (bf16[40,1152]{1,0:T(8,128)(2,1)S(1)}, bf16[40,1152]{1,0:T(8,128)(2,1)S(1)}, u32[]{:S(2)}, u32[]{:S(2)}) collective-permute-start(bf16[40,1152]{1,0:T(8,128)(2,1)S(1)} %slice.6), channel_id=1, source_target_pairs={{0,64},{32,96},{64,0},{96,32},{1,65},{33,97},{65,1},{97,33},{2,66}... | collective-permute-start | bytes 276488 | tf_op jit(solution)/shard_map/ppermute | solution.py:143
  36.4 1.3 %collective-permute-start.7 = (bf16[32,1152]{1,0:T(8,128)(2,1)S(1)}, bf16[32,1152]{1,0:T(8,128)(2,1)S(1)}, u32[]{:S(2)}, u32[]{:S(2)}) collective-permute-start(bf16[32,1152]{1,0:T(8,128)(2,1)S(1)} %slice.7), channel_id=1, source_target_pairs={{0,8},{8,16},{16,24},{24,0},{1,9},{9,17},{17,25},{25,1},{2,10},{10... | collective-permute-start | bytes 221192 | tf_op jit(solution)/shard_map/ppermute | solution.py:143
  37.7 2.0 %collective-permute-start.8 = (bf16[32,1152]{1,0:T(8,128)(2,1)S(1)}, bf16[32,1152]{1,0:T(8,128)(2,1)S(1)}, u32[]{:S(2)}, u32[]{:S(2)}) collective-permute-start(bf16[32,1152]{1,0:T(8,128)(2,1)S(1)} %slice.7), channel_id=1, source_target_pairs={{0,24},{8,0},{16,8},{24,16},{1,25},{9,1},{17,9},{25,17},{2,26},{10... | collective-permute-start | bytes 221192 | tf_op jit(solution)/shard_map/ppermute | solution.py:143
  39.6 2.3 %collective-permute-done.7 = bf16[32,1152]{1,0:T(8,128)(2,1)S(1)} collective-permute-done((bf16[32,1152]{1,0:T(8,128)(2,1)S(1)}, bf16[32,1152]{1,0:T(8,128)(2,1)S(1)}, u32[]{:S(2)}, u32[]{:S(2)}) %collective-permute-start.7) | collective-permute-done | bytes 73760 | tf_op jit(solution)/shard_map/ppermute | solution.py:143
  42.0 1.3 %collective-permute-start.11 = (bf16[32,1152]{1,0:T(8,128)(2,1)S(1)}, bf16[32,1152]{1,0:T(8,128)(2,1)S(1)}, u32[]{:S(2)}, u32[]{:S(2)}) collective-permute-start(bf16[32,1152]{1,0:T(8,128)(2,1)S(1)} %slice.7), channel_id=1, source_target_pairs={{0,16},{8,24},{16,0},{24,8},{1,17},{9,25},{17,1},{25,9},{2,18},{10... | collective-permute-start | bytes 221192 | tf_op jit(solution)/shard_map/ppermute | solution.py:143
  43.7 4.1 %collective-permute-done.11 = bf16[32,1152]{1,0:T(8,128)(2,1)S(1)} collective-permute-done((bf16[32,1152]{1,0:T(8,128)(2,1)S(1)}, bf16[32,1152]{1,0:T(8,128)(2,1)S(1)}, u32[]{:S(2)}, u32[]{:S(2)}) %collective-permute-start.11) | collective-permute-done | bytes 73760 | tf_op jit(solution)/shard_map/ppermute | solution.py:143
  47.9 0.7 %collective-permute-start.13 = (bf16[128,1152]{1,0:T(8,128)(2,1)S(1)}, bf16[128,1152]{1,0:T(8,128)(2,1)S(1)}, u32[]{:S(2)}, u32[]{:S(2)}) collective-permute-start(bf16[128,1152]{1,0:T(8,128)(2,1)S(1)} %pad_maximum_fusion.1.refs_5_), channel_id=1, source_target_pairs={{0,32},{1,97},{32,64},{33,1},{64,96},{65,33},{96,0},{97,65},{2,34}... | collective-permute-start | bytes 884744 | tf_op jit(solution)/shard_map/ppermute | solution.py:149
  48.6 0.7 collective-permute-start.15
  49.3 2.7 %collective-permute-start.16 = (bf16[128,1152]{1,0:T(8,128)(2,1)S(1)}, bf16[128,1152]{1,0:T(8,128)(2,1)S(1)}, u32[]{:S(2)}, u32[]{:S(2)}) collective-permute-start(bf16[128,1152]{1,0:T(8,128)(2,1)S(1)} %pad_maximum_fusion.1.refs_5_), channel_id=1, source_target_pairs={{0,96},{1,33},{32,0},{33,65},{64,32},{65,97},{96,64},{97,1},{2,98}... | collective-permute-start | bytes 884744 | tf_op jit(solution)/shard_map/ppermute | solution.py:149
  51.9 0.9 %collective-permute-done.9.refs_4_.refs_9_ = bf16[160,1152]{1,0:T(8,128)(2,1)S(1)} collective-permute-done((bf16[160,1152]{1,0:T(8,128)(2,1)S(1)}, bf16[160,1152]{1,0:T(8,128)(2,1)S(1)}, u32[]{:S(2)}, u32[]{:S(2)}) %collective-permute-start.9) | collective-permute-done | bytes 368672 | tf_op jit(solution)/shard_map/ppermute | solution.py:149
  53.9 3.8 %collective-permute-done.13.refs_6_ = bf16[128,1152]{1,0:T(8,128)(2,1)S(1)} collective-permute-done((bf16[128,1152]{1,0:T(8,128)(2,1)S(1)}, bf16[128,1152]{1,0:T(8,128)(2,1)S(1)}, u32[]{:S(2)}, u32[]{:S(2)}) %collective-permute-start.13) | collective-permute-done | bytes 294944 | tf_op jit(solution)/shard_map/ppermute | solution.py:149
  57.6 2.2 %attend_0.1 = (f32[4,256,512]{2,1,0:T(8,128)S(1)}, f32[4,256,128]{2,1,0:T(8,128)S(1)}) custom-call(s32[2]{0:T(128)S(1)} %pad_add_fusion.place.refs_0_, s32[1]{0:T(128)S(6)} %copy.11.refs_1_, bf16[4,256,640]{2,1,0:T(8,128)(2,1)S(1)} %get-tuple-element.34.refs_2_.refs_4_, bf16[4,256,640]{2,1,0:T(8,128)(2,1)S(1)} %get-tuple-element.35.refs_3_.refs_5_, ...), custom_call_target="tpu_custom_call" | custom-call | flops 1207959552 | bytes 16777216 | tf_op jit(solution)/shard_map/attend_0/pallas_call | solution.py:378
  59.8 4.0 %attend_12.1 = (f32[4,256,512]{2,1,0:T(8,128)S(1)}, f32[4,256,128]{2,1,0:T(8,128)S(1)}) custom-call(s32[2]{0:T(128)S(1)} %pad_add_fusion.place.refs_0_, s32[1]{0:T(128)S(6)} %copy.11.refs_1_, bf16[4,256,640]{2,1,0:T(8,128)(2,1)S(1)} %get-tuple-element.34.refs_2_.refs_4_, bf16[4,256,640]{2,1,0:T(8,128)(2,1)S(1)} %get-tuple-element.35.refs_3_.refs_5_, ...), custom_call_target="tpu_custom_call" | custom-call | flops 2415919104 | bytes 16777216 | tf_op jit(solution)/shard_map/attend_12/pallas_call | solution.py:378
  63.8 1.8 %collective-permute-done.14.refs_7_ = bf16[128,1152]{1,0:T(8,128)(2,1)S(1)} collective-permute-done((bf16[128,1152]{1,0:T(8,128)(2,1)S(1)}, bf16[128,1152]{1,0:T(8,128)(2,1)S(1)}, u32[]{:S(2)}, u32[]{:S(2)}) %collective-permute-start.14) | collective-permute-done | bytes 294944 | tf_op jit(solution)/shard_map/ppermute | solution.py:149
  65.6 5.7 %attend_3.1 = (bf16[256,512]{1,0:T(8,128)(2,1)}, bf16[12,36864]{1,0:T(8,128)(2,1)}) custom-call(s32[2]{0:T(128)S(1)} %pad_add_fusion.place.refs_0_, s32[1]{0:T(128)S(6)} %copy.11.refs_1_, s32[1,4]{1,0:T(1,128)} %refs_2_.1, s32[1,4]{1,0:T(1,128)} %refs_3_.1, bf16[4,256,640]{2,1,0:T(8,128)(2,1)S(1)} %get-tuple-element.34.refs_2_.refs_4_, ...), custom_call_target="tpu_custom_call" | custom-call | flops 1811939328 | bytes 16777216 | tf_op jit(solution)/shard_map/attend_3/pallas_call | solution.py:378
  (29 shorter events, 1.9 us)
Async XLA Ops:
  0.6 10.4 %copy-start.1 = (bf16[4,64,128]{2,1,0:T(8,128)(2,1)S(1)}, bf16[4,64,128]{2,1,0:T(8,128)(2,1)}, u32[]{:S(2)}) copy-start(bf16[4,64,128]{2,1,0:T(8,128)(2,1)} %param.17) | copy-start | bytes 196612
  0.7 24.9 %copy-start = (bf16[1,256,2304]{2,1,0:T(8,128)(2,1)S(1)}, bf16[1,256,2304]{2,1,0:T(8,128)(2,1)}, u32[]{:S(2)}) copy-start(bf16[1,256,2304]{2,1,0:T(8,128)(2,1)} %param.9) | copy-start | bytes 3538948
  3.9 15.9 %all-to-all-start = ((bf16[16,8,1152]{2,1,0:T(8,128)(2,1)}), bf16[16,8,1152]{2,1,0:T(8,128)(2,1)S(1)}, u32[]{:S(2)}, u32[]{:S(2)}) async-start(bf16[16,8,1152]{2,1,0:T(8,128)(2,1)} %get-tuple-element.27), calls=%async_computation | async-start | bytes 589824 | tf_op jit(solution)/shard_map/all_to_all | solution.py:412
  11.0 14.6 %collective-permute-start.1 = (bf16[4,64,128]{2,1,0:T(8,128)(2,1)S(1)}, bf16[4,64,128]{2,1,0:T(8,128)(2,1)S(1)}, u32[]{:S(2)}, u32[]{:S(2)}) collective-permute-start(bf16[4,64,128]{2,1,0:T(8,128)(2,1)S(1)} %copy-done.1), channel_id=1, source_target_pairs={{0,2},{2,4},{4,6},{6,0},{1,3},{3,5},{5,7},{7,1},{8,10},{10,12},{12... | collective-permute-start | bytes 196616 | tf_op jit(solution)/shard_map/ppermute | solution.py:143
  13.0 12.6 %collective-permute-start.2 = (bf16[4,64,128]{2,1,0:T(8,128)(2,1)S(1)}, bf16[4,64,128]{2,1,0:T(8,128)(2,1)S(1)}, u32[]{:S(2)}, u32[]{:S(2)}) collective-permute-start(bf16[4,64,128]{2,1,0:T(8,128)(2,1)S(1)} %copy-done.1), channel_id=1, source_target_pairs={{0,6},{2,0},{4,2},{6,4},{1,7},{3,1},{5,3},{7,5},{8,14},{10,8},{12,... | collective-permute-start | bytes 196616 | tf_op jit(solution)/shard_map/ppermute | solution.py:143
  13.1 12.5 %collective-permute-start.3 = (bf16[4,64,128]{2,1,0:T(8,128)(2,1)S(1)}, bf16[4,64,128]{2,1,0:T(8,128)(2,1)S(1)}, u32[]{:S(2)}, u32[]{:S(2)}) collective-permute-start(bf16[4,64,128]{2,1,0:T(8,128)(2,1)S(1)} %copy-done.1), channel_id=1, source_target_pairs={{0,4},{2,6},{4,0},{6,2},{1,5},{3,7},{5,1},{7,3},{8,12},{10,14},{12... | collective-permute-start | bytes 196616 | tf_op jit(solution)/shard_map/ppermute | solution.py:143
  20.1 12.1 %collective-permute-start = (bf16[72,1152]{1,0:T(8,128)(2,1)S(1)}, bf16[72,1152]{1,0:T(8,128)(2,1)S(1)}, u32[]{:S(2)}, u32[]{:S(2)}) collective-permute-start(bf16[72,1152]{1,0:T(8,128)(2,1)S(1)} %merge_pages.1), channel_id=1, source_target_pairs={{0,128},{128,0},{1,129},{129,1},{2,130},{130,2},{3,131},{131,3},{4... | collective-permute-start | bytes 497672 | tf_op jit(solution)/shard_map/ppermute | solution.py:416
  32.3 11.0 %collective-permute-start.4 = (bf16[40,1152]{1,0:T(8,128)(2,1)S(1)}, bf16[40,1152]{1,0:T(8,128)(2,1)S(1)}, u32[]{:S(2)}, u32[]{:S(2)}) collective-permute-start(bf16[40,1152]{1,0:T(8,128)(2,1)S(1)} %slice.6), channel_id=1, source_target_pairs={{0,32},{32,64},{64,96},{96,0},{1,33},{33,65},{65,97},{97,1},{2,34}... | collective-permute-start | bytes 276488 | tf_op jit(solution)/shard_map/ppermute | solution.py:143
  33.0 10.3 %collective-permute-start.5 = (bf16[40,1152]{1,0:T(8,128)(2,1)S(1)}, bf16[40,1152]{1,0:T(8,128)(2,1)S(1)}, u32[]{:S(2)}, u32[]{:S(2)}) collective-permute-start(bf16[40,1152]{1,0:T(8,128)(2,1)S(1)} %slice.6), channel_id=1, source_target_pairs={{0,96},{32,0},{64,32},{96,64},{1,97},{33,1},{65,33},{97,65},{2,98}... | collective-permute-start | bytes 276488 | tf_op jit(solution)/shard_map/ppermute | solution.py:143
  35.6 7.7 %collective-permute-start.6 = (bf16[40,1152]{1,0:T(8,128)(2,1)S(1)}, bf16[40,1152]{1,0:T(8,128)(2,1)S(1)}, u32[]{:S(2)}, u32[]{:S(2)}) collective-permute-start(bf16[40,1152]{1,0:T(8,128)(2,1)S(1)} %slice.6), channel_id=1, source_target_pairs={{0,64},{32,96},{64,0},{96,32},{1,65},{33,97},{65,1},{97,33},{2,66}... | collective-permute-start | bytes 276488 | tf_op jit(solution)/shard_map/ppermute | solution.py:143
  36.4 5.6 %collective-permute-start.7 = (bf16[32,1152]{1,0:T(8,128)(2,1)S(1)}, bf16[32,1152]{1,0:T(8,128)(2,1)S(1)}, u32[]{:S(2)}, u32[]{:S(2)}) collective-permute-start(bf16[32,1152]{1,0:T(8,128)(2,1)S(1)} %slice.7), channel_id=1, source_target_pairs={{0,8},{8,16},{16,24},{24,0},{1,9},{9,17},{17,25},{25,1},{2,10},{10... | collective-permute-start | bytes 221192 | tf_op jit(solution)/shard_map/ppermute | solution.py:143
  37.7 5.6 %collective-permute-start.8 = (bf16[32,1152]{1,0:T(8,128)(2,1)S(1)}, bf16[32,1152]{1,0:T(8,128)(2,1)S(1)}, u32[]{:S(2)}, u32[]{:S(2)}) collective-permute-start(bf16[32,1152]{1,0:T(8,128)(2,1)S(1)} %slice.7), channel_id=1, source_target_pairs={{0,24},{8,0},{16,8},{24,16},{1,25},{9,1},{17,9},{25,17},{2,26},{10... | collective-permute-start | bytes 221192 | tf_op jit(solution)/shard_map/ppermute | solution.py:143
  42.0 5.9 %collective-permute-start.11 = (bf16[32,1152]{1,0:T(8,128)(2,1)S(1)}, bf16[32,1152]{1,0:T(8,128)(2,1)S(1)}, u32[]{:S(2)}, u32[]{:S(2)}) collective-permute-start(bf16[32,1152]{1,0:T(8,128)(2,1)S(1)} %slice.7), channel_id=1, source_target_pairs={{0,16},{8,24},{16,0},{24,8},{1,17},{9,25},{17,1},{25,9},{2,18},{10... | collective-permute-start | bytes 221192 | tf_op jit(solution)/shard_map/ppermute | solution.py:143
  43.3 4.6 %collective-permute-start.12 = (bf16[4,4,64,128]{3,2,1,0:T(8,128)(2,1)S(1)}, bf16[4,4,64,128]{3,2,1,0:T(8,128)(2,1)S(1)}, u32[]{:S(2)}, u32[]{:S(2)}) collective-permute-start(bf16[4,4,64,128]{3,2,1,0:T(8,128)(2,1)S(1)} %pad_maximum_fusion.2.refs_11_), channel_id=1, source_target_pairs={{0,1},{1,0},{2,3},{3,2},{4,5},{5,4},{6,7},{7,6},{8,9},{9,8},{10,11... | collective-permute-start | bytes 786440 | tf_op jit(solution)/shard_map/ppermute | solution.py:418
  43.3 9.6 %collective-permute-start.9 = (bf16[160,1152]{1,0:T(8,128)(2,1)S(1)}, bf16[160,1152]{1,0:T(8,128)(2,1)S(1)}, u32[]{:S(2)}, u32[]{:S(2)}) collective-permute-start(bf16[160,1152]{1,0:T(8,128)(2,1)S(1)} %pad_maximum_fusion.refs_4_.refs_8_), channel_id=1, source_target_pairs={{0,8},{1,25},{8,16},{9,1},{16,24},{17,9},{24,0},{25,17},{2,10},{3,... | collective-permute-start | bytes 1105928 | tf_op jit(solution)/shard_map/ppermute | solution.py:149
  47.9 9.8 %collective-permute-start.13 = (bf16[128,1152]{1,0:T(8,128)(2,1)S(1)}, bf16[128,1152]{1,0:T(8,128)(2,1)S(1)}, u32[]{:S(2)}, u32[]{:S(2)}) collective-permute-start(bf16[128,1152]{1,0:T(8,128)(2,1)S(1)} %pad_maximum_fusion.1.refs_5_), channel_id=1, source_target_pairs={{0,32},{1,97},{32,64},{33,1},{64,96},{65,33},{96,0},{97,65},{2,34}... | collective-permute-start | bytes 884744 | tf_op jit(solution)/shard_map/ppermute | solution.py:149
  48.6 11.2 %collective-permute-start.15 = (bf16[160,1152]{1,0:T(8,128)(2,1)S(1)}, bf16[160,1152]{1,0:T(8,128)(2,1)S(1)}, u32[]{:S(2)}, u32[]{:S(2)}) collective-permute-start(bf16[160,1152]{1,0:T(8,128)(2,1)S(1)} %pad_maximum_fusion.refs_4_.refs_8_), channel_id=1, source_target_pairs={{0,24},{1,9},{8,0},{9,17},{16,8},{17,25},{24,16},{25,1},{2,26},{3,... | collective-permute-start | bytes 1105928 | tf_op jit(solution)/shard_map/ppermute | solution.py:149
  49.3 10.5 %collective-permute-start.16 = (bf16[128,1152]{1,0:T(8,128)(2,1)S(1)}, bf16[128,1152]{1,0:T(8,128)(2,1)S(1)}, u32[]{:S(2)}, u32[]{:S(2)}) collective-permute-start(bf16[128,1152]{1,0:T(8,128)(2,1)S(1)} %pad_maximum_fusion.1.refs_5_), channel_id=1, source_target_pairs={{0,96},{1,33},{32,0},{33,65},{64,32},{65,97},{96,64},{97,1},{2,98}... | collective-permute-start | bytes 884744 | tf_op jit(solution)/shard_map/ppermute | solution.py:149
  52.9 10.9 %collective-permute-start.10 = (bf16[160,1152]{1,0:T(8,128)(2,1)S(1)}, bf16[160,1152]{1,0:T(8,128)(2,1)S(1)}, u32[]{:S(2)}, u32[]{:S(2)}) collective-permute-start(bf16[160,1152]{1,0:T(8,128)(2,1)S(1)} %collective-permute-done.9.refs_4_.refs_9_), channel_id=1, source_target_pairs={{0,8},{1,25},{8,16},{9,1},{16,24},{17,9},{24,0},{25,17},{2,10},{3,... | collective-permute-start | bytes 1105928 | tf_op jit(solution)/shard_map/ppermute | solution.py:149
  57.6 7.9 %collective-permute-start.14 = (bf16[128,1152]{1,0:T(8,128)(2,1)S(1)}, bf16[128,1152]{1,0:T(8,128)(2,1)S(1)}, u32[]{:S(2)}, u32[]{:S(2)}) collective-permute-start(bf16[128,1152]{1,0:T(8,128)(2,1)S(1)} %collective-permute-done.13.refs_6_), channel_id=1, source_target_pairs={{0,32},{1,97},{32,64},{33,1},{64,96},{65,33},{96,0},{97,65},{2,34}... | collective-permute-start | bytes 884744 | tf_op jit(solution)/shard_map/ppermute | solution.py:149

commit v5 on v4

--- a/solution.py
+++ b/solution.py
@@ -427,7 +427,11 @@
     state = attended((0,), place, prefix_len, spread, heads, tails, ())
     for rows, axis in ((heads, "pool_2"), (tails, "pool_1")):
         rows += [mirrored(rows[0], axis, 1), mirrored(rows[0], axis, 3)]
-        rows.append(mirrored(rows[1], axis, 1))
+    heads.append(mirrored(heads[1], "pool_2", 1))
+    state, tails[1:] = lax.optimization_barrier((state, tails[1:]))
+    half = tail_row.shape[0] // 2
+    far = mirrored(tails[1][:half], "pool_1", 1), mirrored(tails[2][half:], "pool_1", 3)
+    tails.append(jnp.concatenate(far))
     state = attended((1, 2), place, prefix_len, spread, heads, tails, state)
     ending = (w, new_owner, new_slot, in_place)
     out, updated = attended((3,), place, prefix_len, spread, heads, tails, state, ending)

time: 72.4 us -> 73 us (level)
  starting transfers between devices: 30.4 us -> 35.1 us
  waiting for transfers between devices: 23.3 us -> 18.6 us
    ppermute x6 -> x7, starting transfers between devices: 4.8 us -> 9.46 us  [mirrored(): return lax.ppermute(x, (axis, 'serve_1'), pairs)]
    ppermute x6 -> x7, waiting for transfers between devices: 6.48 us -> 4.12 us  [mirrored(): return lax.ppermute(x, (axis, 'serve_1'), pairs)]
    ppermute x9, waiting for transfers between devices: 6.44 us -> 4.08 us  [shifted(): return lax.ppermute(x, axis, [(i, (i + hop) % SIDE) for i in range(SIDE)])]
  transfers between devices with their start and end apart: 18 -> 19, of which waited for: 7 -> 6; matrix products, arithmetic and copies ran while one was open for 0% -> 0% of each run, Pallas kernels for 10% -> 10%
where the time goes in v5:
time: 73 us; the launch traced here: 71.8 us
  starting transfers between devices  35.1 us (48%)
  waiting for transfers between devices  18.6 us (25%)
  Pallas kernels  16.2 us (22%)
  between operations  1.65 us (2%)
    ppermute x9, starting transfers between devices, shifted(): return lax.ppermute(x, axis, [(i, (i + hop) % SIDE) for i in range(SIDE)])  13.1 us
    pallas_call x3, Pallas kernels, attended(): pl.pallas_call(kernel, out_shape=out_shape, grid_spec=pltpu.PrefetchScala...  12.2 us
    ppermute x7, starting transfers between devices, mirrored(): return lax.ppermute(x, (axis, 'serve_1'), pairs)  9.46 us
    all_to_all x1, starting transfers between devices, local(): lax.all_to_all(pieces, PLANE, 0, 0, tiled=True).reshape(128, PAIR)  7.04 us
    ppermute x1, waiting for transfers between devices, local(): both = mine + lax.ppermute(mine, 'pool_0', [(0, 1), (1, 0)])  6.05 us
    ppermute x1, starting transfers between devices, local(): both = mine + lax.ppermute(mine, 'pool_0', [(0, 1), (1, 0)])  5.48 us
    all_to_all x1, waiting for transfers between devices, local(): lax.all_to_all(pieces, PLANE, 0, 0, tiled=True).reshape(128, PAIR)  4.37 us
    ppermute x7, waiting for transfers between devices, mirrored(): return lax.ppermute(x, (axis, 'serve_1'), pairs)  4.12 us
  transfers between devices with their start and end apart: 19, of which 6 were waited for; matrix products, arithmetic and copies ran while one was open for 0% of the time, Pallas kernels for 10%

profile of v5, /device:TPU:64, one launch (start us, length us, event | category | flops | bytes accessed | tf_op | source)
XLA Modules:
  0.0 71.8 jit_solution(1188412156826343239)
XLA Ops:
  0.7 3.2 %select_pages.1 = (bf16[16,8,1152]{2,1,0:T(8,128)(2,1)}, s32[32,128]{1,0:T(8,128)S(1)}, f32[8,1152]{1,0:T(8,128)S(1)}) custom-call(s32[2]{0:T(128)S(1)} %pad_add_fusion.place.refs_0_, s32[1,32]{1,0:T(1,128)} %owner_hbm.1, s32[1,32]{1,0:T(1,128)} %slot_hbm.1, bf16[12,36864]{1,0:T(8,128)(2,1)} %bitcast.13, bf16[1,4608]{1,0:T(2,128)(2,1)} %suffix_hbm.1), custom_call_target="tpu_custom_call" | custom-call | tf_op jit(solution)/shard_map/select_pages/pallas_call | solution.py:88
  3.9 7.0 %all-to-all-start = ((bf16[16,8,1152]{2,1,0:T(8,128)(2,1)}), bf16[16,8,1152]{2,1,0:T(8,128)(2,1)S(1)}, u32[]{:S(2)}, u32[]{:S(2)}) async-start(bf16[16,8,1152]{2,1,0:T(8,128)(2,1)} %get-tuple-element.31), calls=%async_computation | async-start | bytes 589824 | tf_op jit(solution)/shard_map/all_to_all | solution.py:412
  11.0 2.0 %collective-permute-start.1 = (bf16[4,64,128]{2,1,0:T(8,128)(2,1)S(1)}, bf16[4,64,128]{2,1,0:T(8,128)(2,1)S(1)}, u32[]{:S(2)}, u32[]{:S(2)}) collective-permute-start(bf16[4,64,128]{2,1,0:T(8,128)(2,1)S(1)} %copy-done.1), channel_id=1, source_target_pairs={{0,2},{2,4},{4,6},{6,0},{1,3},{3,5},{5,7},{7,1},{8,10},{10,12},{12... | collective-permute-start | bytes 196616 | tf_op jit(solution)/shard_map/ppermute | solution.py:143
  13.1 2.3 %collective-permute-start.3 = (bf16[4,64,128]{2,1,0:T(8,128)(2,1)S(1)}, bf16[4,64,128]{2,1,0:T(8,128)(2,1)S(1)}, u32[]{:S(2)}, u32[]{:S(2)}) collective-permute-start(bf16[4,64,128]{2,1,0:T(8,128)(2,1)S(1)} %copy-done.1), channel_id=1, source_target_pairs={{0,4},{2,6},{4,0},{6,2},{1,5},{3,7},{5,1},{7,3},{8,12},{10,14},{12... | collective-permute-start | bytes 196616 | tf_op jit(solution)/shard_map/ppermute | solution.py:143
  15.4 4.4 %all-to-all-done = bf16[16,8,1152]{2,1,0:T(8,128)(2,1)S(1)} async-done(((bf16[16,8,1152]{2,1,0:T(8,128)(2,1)}), bf16[16,8,1152]{2,1,0:T(8,128)(2,1)S(1)}, u32[]{:S(2)}, u32[]{:S(2)}) %all-to-all-start) | async-done | bytes 294944 | tf_op jit(solution)/shard_map/all_to_all | solution.py:412
  20.1 5.5 %collective-permute-start = (bf16[72,1152]{1,0:T(8,128)(2,1)S(1)}, bf16[72,1152]{1,0:T(8,128)(2,1)S(1)}, u32[]{:S(2)}, u32[]{:S(2)}) collective-permute-start(bf16[72,1152]{1,0:T(8,128)(2,1)S(1)} %merge_pages.1), channel_id=1, source_target_pairs={{0,128},{128,0},{1,129},{129,1},{2,130},{130,2},{3,131},{131,3},{4... | collective-permute-start | bytes 497672 | tf_op jit(solution)/shard_map/ppermute | solution.py:416
  26.2 6.0 %collective-permute-done = bf16[72,1152]{1,0:T(8,128)(2,1)S(1)} collective-permute-done((bf16[72,1152]{1,0:T(8,128)(2,1)S(1)}, bf16[72,1152]{1,0:T(8,128)(2,1)S(1)}, u32[]{:S(2)}, u32[]{:S(2)}) %collective-permute-start) | collective-permute-done | bytes 165920 | tf_op jit(solution)/shard_map/ppermute | solution.py:416
  32.3 0.7 %collective-permute-start.4 = (bf16[40,1152]{1,0:T(8,128)(2,1)S(1)}, bf16[40,1152]{1,0:T(8,128)(2,1)S(1)}, u32[]{:S(2)}, u32[]{:S(2)}) collective-permute-start(bf16[40,1152]{1,0:T(8,128)(2,1)S(1)} %slice.12), channel_id=1, source_target_pairs={{0,32},{32,64},{64,96},{96,0},{1,33},{33,65},{65,97},{97,1},{2,34}... | collective-permute-start | bytes 276488 | tf_op jit(solution)/shard_map/ppermute | solution.py:143
  33.0 2.6 %collective-permute-start.5 = (bf16[40,1152]{1,0:T(8,128)(2,1)S(1)}, bf16[40,1152]{1,0:T(8,128)(2,1)S(1)}, u32[]{:S(2)}, u32[]{:S(2)}) collective-permute-start(bf16[40,1152]{1,0:T(8,128)(2,1)S(1)} %slice.12), channel_id=1, source_target_pairs={{0,96},{32,0},{64,32},{96,64},{1,97},{33,1},{65,33},{97,65},{2,98}... | collective-permute-start | bytes 276488 | tf_op jit(solution)/shard_map/ppermute | solution.py:143
  35.6 0.8 %collective-permute-start.6 = (bf16[40,1152]{1,0:T(8,128)(2,1)S(1)}, bf16[40,1152]{1,0:T(8,128)(2,1)S(1)}, u32[]{:S(2)}, u32[]{:S(2)}) collective-permute-start(bf16[40,1152]{1,0:T(8,128)(2,1)S(1)} %slice.12), channel_id=1, source_target_pairs={{0,64},{32,96},{64,0},{96,32},{1,65},{33,97},{65,1},{97,33},{2,66}... | collective-permute-start | bytes 276488 | tf_op jit(solution)/shard_map/ppermute | solution.py:143
  36.4 1.3 %collective-permute-start.7 = (bf16[32,1152]{1,0:T(8,128)(2,1)S(1)}, bf16[32,1152]{1,0:T(8,128)(2,1)S(1)}, u32[]{:S(2)}, u32[]{:S(2)}) collective-permute-start(bf16[32,1152]{1,0:T(8,128)(2,1)S(1)} %slice.13), channel_id=1, source_target_pairs={{0,8},{8,16},{16,24},{24,0},{1,9},{9,17},{17,25},{25,1},{2,10},{10... | collective-permute-start | bytes 221192 | tf_op jit(solution)/shard_map/ppermute | solution.py:143
  37.7 2.0 %collective-permute-start.8 = (bf16[32,1152]{1,0:T(8,128)(2,1)S(1)}, bf16[32,1152]{1,0:T(8,128)(2,1)S(1)}, u32[]{:S(2)}, u32[]{:S(2)}) collective-permute-start(bf16[32,1152]{1,0:T(8,128)(2,1)S(1)} %slice.13), channel_id=1, source_target_pairs={{0,24},{8,0},{16,8},{24,16},{1,25},{9,1},{17,9},{25,17},{2,26},{10... | collective-permute-start | bytes 221192 | tf_op jit(solution)/shard_map/ppermute | solution.py:143
  39.6 2.3 %collective-permute-done.7 = bf16[32,1152]{1,0:T(8,128)(2,1)S(1)} collective-permute-done((bf16[32,1152]{1,0:T(8,128)(2,1)S(1)}, bf16[32,1152]{1,0:T(8,128)(2,1)S(1)}, u32[]{:S(2)}, u32[]{:S(2)}) %collective-permute-start.7) | collective-permute-done | bytes 73760 | tf_op jit(solution)/shard_map/ppermute | solution.py:143
  42.0 1.3 %collective-permute-start.11 = (bf16[32,1152]{1,0:T(8,128)(2,1)S(1)}, bf16[32,1152]{1,0:T(8,128)(2,1)S(1)}, u32[]{:S(2)}, u32[]{:S(2)}) collective-permute-start(bf16[32,1152]{1,0:T(8,128)(2,1)S(1)} %slice.13), channel_id=1, source_target_pairs={{0,16},{8,24},{16,0},{24,8},{1,17},{9,25},{17,1},{25,9},{2,18},{10... | collective-permute-start | bytes 221192 | tf_op jit(solution)/shard_map/ppermute | solution.py:143
  43.3 2.8 %collective-permute-start.17 = (bf16[160,1152]{1,0:T(8,128)(2,1)S(1)}, bf16[160,1152]{1,0:T(8,128)(2,1)S(1)}, u32[]{:S(2)}, u32[]{:S(2)}) collective-permute-start(bf16[160,1152]{1,0:T(8,128)(2,1)S(1)} %pad_maximum_fusion.refs_4_.refs_8_), channel_id=1, source_target_pairs={{0,24},{1,9},{8,0},{9,17},{16,8},{17,25},{24,16},{25,1},{2,26},{3,... | collective-permute-start | bytes 1105928 | tf_op jit(solution)/shard_map/ppermute | solution.py:149
  46.1 1.7 %collective-permute-done.11 = bf16[32,1152]{1,0:T(8,128)(2,1)S(1)} collective-permute-done((bf16[32,1152]{1,0:T(8,128)(2,1)S(1)}, bf16[32,1152]{1,0:T(8,128)(2,1)S(1)}, u32[]{:S(2)}, u32[]{:S(2)}) %collective-permute-start.11) | collective-permute-done | bytes 73760 | tf_op jit(solution)/shard_map/ppermute | solution.py:143
  47.9 0.8 %collective-permute-start.13 = (bf16[128,1152]{1,0:T(8,128)(2,1)S(1)}, bf16[128,1152]{1,0:T(8,128)(2,1)S(1)}, u32[]{:S(2)}, u32[]{:S(2)}) collective-permute-start(bf16[128,1152]{1,0:T(8,128)(2,1)S(1)} %pad_maximum_fusion.1.refs_5_), channel_id=1, source_target_pairs={{0,32},{1,97},{32,64},{33,1},{64,96},{65,33},{96,0},{97,65},{2,34}... | collective-permute-start | bytes 884744 | tf_op jit(solution)/shard_map/ppermute | solution.py:149
  48.6 2.5 %collective-permute-start.14 = (bf16[128,1152]{1,0:T(8,128)(2,1)S(1)}, bf16[128,1152]{1,0:T(8,128)(2,1)S(1)}, u32[]{:S(2)}, u32[]{:S(2)}) collective-permute-start(bf16[128,1152]{1,0:T(8,128)(2,1)S(1)} %pad_maximum_fusion.1.refs_5_), channel_id=1, source_target_pairs={{0,96},{1,33},{32,0},{33,65},{64,32},{65,97},{96,64},{97,1},{2,98}... | collective-permute-start | bytes 884744 | tf_op jit(solution)/shard_map/ppermute | solution.py:149
  51.8 2.2 %attend_0.1 = (f32[4,256,512]{2,1,0:T(8,128)S(1)}, f32[4,256,128]{2,1,0:T(8,128)S(1)}) custom-call(s32[2]{0:T(128)S(1)} %pad_add_fusion.place.refs_0_, s32[1]{0:T(128)S(6)} %copy.11.refs_1_, bf16[4,256,640]{2,1,0:T(8,128)(2,1)S(1)} %get-tuple-element.38.refs_2_.refs_4_, bf16[4,256,640]{2,1,0:T(8,128)(2,1)S(1)} %get-tuple-element.39.refs_3_.refs_5_, ...), custom_call_target="tpu_custom_call" | custom-call | flops 1207959552 | bytes 16777216 | tf_op jit(solution)/shard_map/attend_0/pallas_call | solution.py:378
  54.0 1.7 %collective-permute-done.9.refs_4_.refs_9_ = bf16[160,1152]{1,0:T(8,128)(2,1)S(1)} collective-permute-done((bf16[160,1152]{1,0:T(8,128)(2,1)S(1)}, bf16[160,1152]{1,0:T(8,128)(2,1)S(1)}, u32[]{:S(2)}, u32[]{:S(2)}) %collective-permute-start.9) | collective-permute-done | bytes 368672 | tf_op jit(solution)/shard_map/ppermute | solution.py:149
  55.7 2.4 %collective-permute-done.13.refs_6_ = bf16[128,1152]{1,0:T(8,128)(2,1)S(1)} collective-permute-done((bf16[128,1152]{1,0:T(8,128)(2,1)S(1)}, bf16[128,1152]{1,0:T(8,128)(2,1)S(1)}, u32[]{:S(2)}, u32[]{:S(2)}) %collective-permute-start.13) | collective-permute-done | bytes 294944 | tf_op jit(solution)/shard_map/ppermute | solution.py:149
  58.2 3.3 %collective-permute-start.16 = (bf16[64,1152]{1,0:T(8,128)(2,1)S(1)}, bf16[64,1152]{1,0:T(8,128)(2,1)S(1)}, u32[]{:S(2)}, u32[]{:S(2)}) collective-permute-start(bf16[64,1152]{1,0:T(8,128)(2,1)S(1)} %slice.15), channel_id=1, source_target_pairs={{0,96},{1,33},{32,0},{33,65},{64,32},{65,97},{96,64},{97,1},{2,98}... | collective-permute-start | bytes 442376 | tf_op jit(solution)/shard_map/ppermute | solution.py:149
  61.5 4.0 %attend_12.1 = (f32[4,256,512]{2,1,0:T(8,128)S(1)}, f32[4,256,128]{2,1,0:T(8,128)S(1)}) custom-call(s32[2]{0:T(128)S(1)} %pad_add_fusion.place.refs_0_, s32[1]{0:T(128)S(6)} %copy.11.refs_1_, bf16[4,256,640]{2,1,0:T(8,128)(2,1)S(1)} %get-tuple-element.38.refs_2_.refs_4_, bf16[4,256,640]{2,1,0:T(8,128)(2,1)S(1)} %get-tuple-element.39.refs_3_.refs_5_, ...), custom_call_target="tpu_custom_call" | custom-call | flops 2415919104 | bytes 16777216 | tf_op jit(solution)/shard_map/attend_12/pallas_call | solution.py:378
  65.6 6.1 %attend_3.1 = (bf16[256,512]{1,0:T(8,128)(2,1)}, bf16[12,36864]{1,0:T(8,128)(2,1)}) custom-call(s32[2]{0:T(128)S(1)} %pad_add_fusion.place.refs_0_, s32[1]{0:T(128)S(6)} %copy.11.refs_1_, s32[1,4]{1,0:T(1,128)} %refs_2_.1, s32[1,4]{1,0:T(1,128)} %refs_3_.1, bf16[4,256,640]{2,1,0:T(8,128)(2,1)S(1)} %get-tuple-element.38.refs_2_.refs_4_, ...), custom_call_target="tpu_custom_call" | custom-call | flops 1811939328 | bytes 16777216 | tf_op jit(solution)/shard_map/attend_3/pallas_call | solution.py:378
  (34 shorter events, 1.3 us)
Async XLA Ops:
  0.6 10.4 %copy-start.1 = (bf16[4,64,128]{2,1,0:T(8,128)(2,1)S(1)}, bf16[4,64,128]{2,1,0:T(8,128)(2,1)}, u32[]{:S(2)}) copy-start(bf16[4,64,128]{2,1,0:T(8,128)(2,1)} %param.17) | copy-start | bytes 196612
  0.7 24.9 %copy-start = (bf16[1,256,2304]{2,1,0:T(8,128)(2,1)S(1)}, bf16[1,256,2304]{2,1,0:T(8,128)(2,1)}, u32[]{:S(2)}) copy-start(bf16[1,256,2304]{2,1,0:T(8,128)(2,1)} %param.9) | copy-start | bytes 3538948
  3.9 15.9 %all-to-all-start = ((bf16[16,8,1152]{2,1,0:T(8,128)(2,1)}), bf16[16,8,1152]{2,1,0:T(8,128)(2,1)S(1)}, u32[]{:S(2)}, u32[]{:S(2)}) async-start(bf16[16,8,1152]{2,1,0:T(8,128)(2,1)} %get-tuple-element.31), calls=%async_computation | async-start | bytes 589824 | tf_op jit(solution)/shard_map/all_to_all | solution.py:412
  11.0 14.6 %collective-permute-start.1 = (bf16[4,64,128]{2,1,0:T(8,128)(2,1)S(1)}, bf16[4,64,128]{2,1,0:T(8,128)(2,1)S(1)}, u32[]{:S(2)}, u32[]{:S(2)}) collective-permute-start(bf16[4,64,128]{2,1,0:T(8,128)(2,1)S(1)} %copy-done.1), channel_id=1, source_target_pairs={{0,2},{2,4},{4,6},{6,0},{1,3},{3,5},{5,7},{7,1},{8,10},{10,12},{12... | collective-permute-start | bytes 196616 | tf_op jit(solution)/shard_map/ppermute | solution.py:143
  13.0 12.6 %collective-permute-start.2 = (bf16[4,64,128]{2,1,0:T(8,128)(2,1)S(1)}, bf16[4,64,128]{2,1,0:T(8,128)(2,1)S(1)}, u32[]{:S(2)}, u32[]{:S(2)}) collective-permute-start(bf16[4,64,128]{2,1,0:T(8,128)(2,1)S(1)} %copy-done.1), channel_id=1, source_target_pairs={{0,6},{2,0},{4,2},{6,4},{1,7},{3,1},{5,3},{7,5},{8,14},{10,8},{12,... | collective-permute-start | bytes 196616 | tf_op jit(solution)/shard_map/ppermute | solution.py:143
  13.1 12.5 %collective-permute-start.3 = (bf16[4,64,128]{2,1,0:T(8,128)(2,1)S(1)}, bf16[4,64,128]{2,1,0:T(8,128)(2,1)S(1)}, u32[]{:S(2)}, u32[]{:S(2)}) collective-permute-start(bf16[4,64,128]{2,1,0:T(8,128)(2,1)S(1)} %copy-done.1), channel_id=1, source_target_pairs={{0,4},{2,6},{4,0},{6,2},{1,5},{3,7},{5,1},{7,3},{8,12},{10,14},{12... | collective-permute-start | bytes 196616 | tf_op jit(solution)/shard_map/ppermute | solution.py:143
  20.1 12.1 %collective-permute-start = (bf16[72,1152]{1,0:T(8,128)(2,1)S(1)}, bf16[72,1152]{1,0:T(8,128)(2,1)S(1)}, u32[]{:S(2)}, u32[]{:S(2)}) collective-permute-start(bf16[72,1152]{1,0:T(8,128)(2,1)S(1)} %merge_pages.1), channel_id=1, source_target_pairs={{0,128},{128,0},{1,129},{129,1},{2,130},{130,2},{3,131},{131,3},{4... | collective-permute-start | bytes 497672 | tf_op jit(solution)/shard_map/ppermute | solution.py:416
  32.3 11.0 %collective-permute-start.4 = (bf16[40,1152]{1,0:T(8,128)(2,1)S(1)}, bf16[40,1152]{1,0:T(8,128)(2,1)S(1)}, u32[]{:S(2)}, u32[]{:S(2)}) collective-permute-start(bf16[40,1152]{1,0:T(8,128)(2,1)S(1)} %slice.12), channel_id=1, source_target_pairs={{0,32},{32,64},{64,96},{96,0},{1,33},{33,65},{65,97},{97,1},{2,34}... | collective-permute-start | bytes 276488 | tf_op jit(solution)/shard_map/ppermute | solution.py:143
  33.0 10.3 %collective-permute-start.5 = (bf16[40,1152]{1,0:T(8,128)(2,1)S(1)}, bf16[40,1152]{1,0:T(8,128)(2,1)S(1)}, u32[]{:S(2)}, u32[]{:S(2)}) collective-permute-start(bf16[40,1152]{1,0:T(8,128)(2,1)S(1)} %slice.12), channel_id=1, source_target_pairs={{0,96},{32,0},{64,32},{96,64},{1,97},{33,1},{65,33},{97,65},{2,98}... | collective-permute-start | bytes 276488 | tf_op jit(solution)/shard_map/ppermute | solution.py:143
  35.6 7.7 %collective-permute-start.6 = (bf16[40,1152]{1,0:T(8,128)(2,1)S(1)}, bf16[40,1152]{1,0:T(8,128)(2,1)S(1)}, u32[]{:S(2)}, u32[]{:S(2)}) collective-permute-start(bf16[40,1152]{1,0:T(8,128)(2,1)S(1)} %slice.12), channel_id=1, source_target_pairs={{0,64},{32,96},{64,0},{96,32},{1,65},{33,97},{65,1},{97,33},{2,66}... | collective-permute-start | bytes 276488 | tf_op jit(solution)/shard_map/ppermute | solution.py:143
  36.4 5.6 %collective-permute-start.7 = (bf16[32,1152]{1,0:T(8,128)(2,1)S(1)}, bf16[32,1152]{1,0:T(8,128)(2,1)S(1)}, u32[]{:S(2)}, u32[]{:S(2)}) collective-permute-start(bf16[32,1152]{1,0:T(8,128)(2,1)S(1)} %slice.13), channel_id=1, source_target_pairs={{0,8},{8,16},{16,24},{24,0},{1,9},{9,17},{17,25},{25,1},{2,10},{10... | collective-permute-start | bytes 221192 | tf_op jit(solution)/shard_map/ppermute | solution.py:143
  37.7 5.6 %collective-permute-start.8 = (bf16[32,1152]{1,0:T(8,128)(2,1)S(1)}, bf16[32,1152]{1,0:T(8,128)(2,1)S(1)}, u32[]{:S(2)}, u32[]{:S(2)}) collective-permute-start(bf16[32,1152]{1,0:T(8,128)(2,1)S(1)} %slice.13), channel_id=1, source_target_pairs={{0,24},{8,0},{16,8},{24,16},{1,25},{9,1},{17,9},{25,17},{2,26},{10... | collective-permute-start | bytes 221192 | tf_op jit(solution)/shard_map/ppermute | solution.py:143
  42.0 5.9 %collective-permute-start.11 = (bf16[32,1152]{1,0:T(8,128)(2,1)S(1)}, bf16[32,1152]{1,0:T(8,128)(2,1)S(1)}, u32[]{:S(2)}, u32[]{:S(2)}) collective-permute-start(bf16[32,1152]{1,0:T(8,128)(2,1)S(1)} %slice.13), channel_id=1, source_target_pairs={{0,16},{8,24},{16,0},{24,8},{1,17},{9,25},{17,1},{25,9},{2,18},{10... | collective-permute-start | bytes 221192 | tf_op jit(solution)/shard_map/ppermute | solution.py:143
  43.3 4.6 %collective-permute-start.12 = (bf16[4,4,64,128]{3,2,1,0:T(8,128)(2,1)S(1)}, bf16[4,4,64,128]{3,2,1,0:T(8,128)(2,1)S(1)}, u32[]{:S(2)}, u32[]{:S(2)}) collective-permute-start(bf16[4,4,64,128]{3,2,1,0:T(8,128)(2,1)S(1)} %pad_maximum_fusion.3.refs_11_), channel_id=1, source_target_pairs={{0,1},{1,0},{2,3},{3,2},{4,5},{5,4},{6,7},{7,6},{8,9},{9,8},{10,11... | collective-permute-start | bytes 786440 | tf_op jit(solution)/shard_map/ppermute | solution.py:418
  43.3 18.2 %collective-permute-start.17 = (bf16[160,1152]{1,0:T(8,128)(2,1)S(1)}, bf16[160,1152]{1,0:T(8,128)(2,1)S(1)}, u32[]{:S(2)}, u32[]{:S(2)}) collective-permute-start(bf16[160,1152]{1,0:T(8,128)(2,1)S(1)} %pad_maximum_fusion.refs_4_.refs_8_), channel_id=1, source_target_pairs={{0,24},{1,9},{8,0},{9,17},{16,8},{17,25},{24,16},{25,1},{2,26},{3,... | collective-permute-start | bytes 1105928 | tf_op jit(solution)/shard_map/ppermute | solution.py:149
  46.1 9.6 %collective-permute-start.9 = (bf16[160,1152]{1,0:T(8,128)(2,1)S(1)}, bf16[160,1152]{1,0:T(8,128)(2,1)S(1)}, u32[]{:S(2)}, u32[]{:S(2)}) collective-permute-start(bf16[160,1152]{1,0:T(8,128)(2,1)S(1)} %pad_maximum_fusion.refs_4_.refs_8_), channel_id=1, source_target_pairs={{0,8},{1,25},{8,16},{9,1},{16,24},{17,9},{24,0},{25,17},{2,10},{3,... | collective-permute-start | bytes 1105928 | tf_op jit(solution)/shard_map/ppermute | solution.py:149
  47.9 10.2 %collective-permute-start.13 = (bf16[128,1152]{1,0:T(8,128)(2,1)S(1)}, bf16[128,1152]{1,0:T(8,128)(2,1)S(1)}, u32[]{:S(2)}, u32[]{:S(2)}) collective-permute-start(bf16[128,1152]{1,0:T(8,128)(2,1)S(1)} %pad_maximum_fusion.1.refs_5_), channel_id=1, source_target_pairs={{0,32},{1,97},{32,64},{33,1},{64,96},{65,33},{96,0},{97,65},{2,34}... | collective-permute-start | bytes 884744 | tf_op jit(solution)/shard_map/ppermute | solution.py:149
  48.6 9.5 %collective-permute-start.14 = (bf16[128,1152]{1,0:T(8,128)(2,1)S(1)}, bf16[128,1152]{1,0:T(8,128)(2,1)S(1)}, u32[]{:S(2)}, u32[]{:S(2)}) collective-permute-start(bf16[128,1152]{1,0:T(8,128)(2,1)S(1)} %pad_maximum_fusion.1.refs_5_), channel_id=1, source_target_pairs={{0,96},{1,33},{32,0},{33,65},{64,32},{65,97},{96,64},{97,1},{2,98}... | collective-permute-start | bytes 884744 | tf_op jit(solution)/shard_map/ppermute | solution.py:149
  55.7 9.9 %collective-permute-start.10 = (bf16[160,1152]{1,0:T(8,128)(2,1)S(1)}, bf16[160,1152]{1,0:T(8,128)(2,1)S(1)}, u32[]{:S(2)}, u32[]{:S(2)}) collective-permute-start(bf16[160,1152]{1,0:T(8,128)(2,1)S(1)} %collective-permute-done.9.refs_4_.refs_9_), channel_id=1, source_target_pairs={{0,8},{1,25},{8,16},{9,1},{16,24},{17,9},{24,0},{25,17},{2,10},{3,... | collective-permute-start | bytes 1105928 | tf_op jit(solution)/shard_map/ppermute | solution.py:149
  58.1 7.4 %collective-permute-start.15 = (bf16[64,1152]{1,0:T(8,128)(2,1)S(1)}, bf16[64,1152]{1,0:T(8,128)(2,1)S(1)}, u32[]{:S(2)}, u32[]{:S(2)}) collective-permute-start(bf16[64,1152]{1,0:T(8,128)(2,1)S(1)} %slice.14), channel_id=1, source_target_pairs={{0,32},{1,97},{32,64},{33,1},{64,96},{65,33},{96,0},{97,65},{2,34}... | collective-permute-start | bytes 442376 | tf_op jit(solution)/shard_map/ppermute | solution.py:149
  58.2 7.3 %collective-permute-start.16 = (bf16[64,1152]{1,0:T(8,128)(2,1)S(1)}, bf16[64,1152]{1,0:T(8,128)(2,1)S(1)}, u32[]{:S(2)}, u32[]{:S(2)}) collective-permute-start(bf16[64,1152]{1,0:T(8,128)(2,1)S(1)} %slice.15), channel_id=1, source_target_pairs={{0,96},{1,33},{32,0},{33,65},{64,32},{65,97},{96,64},{97,1},{2,98}... | collective-permute-start | bytes 442376 | tf_op jit(solution)/shard_map/ppermute | solution.py:149
